TPU v7x, 256 devices: a whole 4x4x8 slice. The times are simulated.
256 devices in a mesh: fsdp: 16 (over y, x), tp: 8 (over z_hi, core), tower: 2 (over z_lo).
Axes of the slice: x: 4, y: 4, z: 8 (z_hi: 4, z_lo: 2; z = z_hi * 2 + z_lo), core: 2. Of those that a mesh axis runs over, the one named last changes fastest.
Arguments:
- images: bfloat16 [16384, 5120], P(('fsdp', 'tower')), may hold values from -61 to 61
- img_weight: bfloat16 [5120, 1024], P('fsdp', 'tp')
- texts: bfloat16 [16384, 1024], P(('fsdp', 'tp', 'tower')), may hold values from -1 to 1
- pair_perm: int32 [16384], P(('fsdp', 'tower')), may hold values from 0 to 16383, as said below
- forget: int32 [16384], P(('fsdp', 'tower')), may hold values 0 or 1
Outputs:
- pair_loss: float32 [16384], P(('fsdp', 'tower'))
- weight_grad: float32 [5120, 1024], P('fsdp', 'tp')
Inputs may be any that keep to these rules, and one draw needn't show every extreme that they name: `pair_perm`: each number 0 to 16383 appears once.
All inputs are finite; a program needn't handle non-finite values. No bound on the sum of `forget` on one device may be relied on, other than what follows from the above.
Results may differ from a plain program's by a relative error of at most 0.0036.
Values may be sent and summed in bfloat16 or wider, within the bound.
No kernel may reach another device: no remote copies, remote signals or barrier semaphores. Data moves between devices by JAX's collectives and lax.ppermute only.
A program may use at most 64 MiB of HBM per device.

v0:
```python
import jax
import jax.numpy as jnp
from jax import lax
from jax.sharding import Mesh
from jax.sharding import PartitionSpec as P

FSDP = ("fsdp_0", "fsdp_1")
FSDP_TOWER = ("fsdp_0", "fsdp_1", "tower")
FSDP_TP_TOWER = ("fsdp_0", "fsdp_1", "tp", "tower")


epsilon = 1e-06
score_scale = 100.0


def copy_for_each(x, axis):
    copies = jnp.broadcast_to(x, (lax.axis_size(axis), *x.shape))
    return lax.all_to_all(copies, axis, split_axis=0, concat_axis=0, tiled=True)


def in_order(parts, dim):
    lengths = list(parts.shape[1:])
    lengths[dim] *= parts.shape[0]
    return jnp.moveaxis(parts, 0, dim).reshape(lengths)


def gather_directly(x, axis, dim):
    parts = copy_for_each(x, axis)
    return in_order(parts, dim)


def stacked_from(x, axes, order):
    parts = x[None]
    for k in order:
        parts = lax.all_gather(parts, axes[k], axis=0, tiled=True)
    carried = [lax.axis_size(axes[k]) for k in reversed(order)]
    parts = parts.reshape(*carried, *x.shape)
    turned = sorted(range(len(order)), key=lambda place: order[len(order) - 1 - place])
    return parts.transpose(*turned, *range(len(order), parts.ndim)).reshape(-1, *x.shape)


def gather_axes(x, axes, order, dim):
    return in_order(stacked_from(x, axes, order), dim)


def all_in_one(x, axis):
    leaves = jax.tree.leaves(x)
    order = sorted(range(len(leaves)), key=lambda k: -leaves[k].size)
    width = (1, *leaves[order[0]].shape)[-1]
    lines = [
        jnp.pad(leaves[k].reshape(-1), (0, -leaves[k].size % width)).reshape(-1, width)
        for k in order
    ]
    both, at, found = (copy_for_each(jnp.concatenate(lines), axis), 0, {})
    for k, line in zip(order, lines):
        section = both[:, at : at + len(line)].reshape(len(both), -1)
        found[k] = section[:, : leaves[k].size].reshape(-1, *leaves[k].shape)
        at += len(line)
    numbers = iter(range(len(leaves)))
    return jax.tree.map(lambda _: found[next(numbers)], x)


def folded_in_pairs(pieces, combine):
    while len(jax.tree.leaves(pieces)[0]) > 1:
        pieces = jax.vmap(combine)(
            *(jax.tree.map(lambda part: part[side::2], pieces) for side in (0, 1))
        )
    return jax.tree.map(lambda part: part[0], pieces)


def merged(x, axis, combine):
    pieces = all_in_one(x, axis)
    return folded_in_pairs(pieces, combine)


def cut_along(x, dim, peers):
    before, after = (x.shape[:dim], x.shape[dim + 1 :])
    return jnp.moveaxis(x.reshape(*before, peers, -1, *after), dim, 0)


def summed_on_arrival(x, axis, dim):
    peers = lax.axis_size(axis)
    parts = lax.all_to_all(cut_along(x, dim, peers), axis, 0, 0, tiled=True)
    return jnp.sum(parts, axis=0)


def over_copies(x, axis):
    return copy_for_each(x, axis).sum(axis=0)


def local(images, img_weight, texts, pair_perm, forget):
    part = images
    emb_part = jnp.dot(
        part, gather_directly(img_weight, FSDP, 0), preferred_element_type=jnp.float32
    ).astype(jnp.bfloat16)
    emb = gather_directly(emb_part, "tp", 1)
    efloat = emb.astype(jnp.float32)
    rnorm = lax.rsqrt(jnp.sum(efloat * efloat, axis=1, keepdims=True) + epsilon)
    unit = efloat * rnorm
    unit_b = unit.astype(jnp.bfloat16)
    signs = 1.0 - 2.0 * forget.astype(jnp.float32)
    tp_index = lax.axis_index("tp")
    tp_count = lax.axis_size("tp")
    span = texts.shape[0] * lax.axis_size("tower")
    gathered = gather_axes(texts, FSDP_TOWER, (2, 0, 1), 0)
    logits = score_scale * lax.dot_general(
        unit_b, gathered, (((1,), (1,)), ((), ())), preferred_element_type=jnp.float32
    )
    positions = 0 + jnp.arange(gathered.shape[0], dtype=jnp.int32)
    hit = (
        pair_perm[:, None]
        == ((positions // span * tp_count + tp_index) * span + positions % span)[None, :]
    )
    logits, hit = (logits, hit)
    top = jnp.max(logits, axis=1)
    total = jnp.sum(jnp.exp(logits - top[:, None]), axis=1)
    positive = jnp.sum(jnp.where(hit, logits, 0.0), axis=1)

    def combine(first, second):
        joined = jnp.maximum(first[0], second[0])
        summed = first[1] * jnp.exp(first[0] - joined) + second[1] * jnp.exp(second[0] - joined)
        return (joined, summed, first[2] + second[2])

    top, total, positive = merged((top, total, positive), "tp", combine)
    lse = top + jnp.log(total)
    pair_loss = lse - positive
    grad_part = score_scale * jnp.dot(
        (signs[:, None] * (jnp.exp(logits - lse[:, None]) - hit.astype(jnp.float32))).astype(
            jnp.bfloat16
        ),
        gathered,
        preferred_element_type=jnp.float32,
    )
    grad_unit = summed_on_arrival(grad_part, "tp", 1)
    unit_part = emb_part.astype(jnp.float32) * rnorm
    radial = over_copies(jnp.sum(unit_part * grad_unit, axis=1, keepdims=True), "tp")
    grad_emb = (rnorm * (grad_unit - unit_part * radial)).astype(jnp.bfloat16)
    part = images
    share = summed_on_arrival(
        lax.dot_general(
            part, grad_emb, (((0,), (0,)), ((), ())), preferred_element_type=jnp.float32
        ),
        FSDP,
        0,
    )
    weight_grad = over_copies(share, "tower")
    return (pair_loss, weight_grad)


def solution(mesh):
    finer = Mesh(
        mesh.devices.reshape(4, 4, mesh.shape["tp"], mesh.shape["tower"]),
        ("fsdp_0", "fsdp_1", "tp", "tower"),
    )
    placed = (
        P(FSDP_TOWER, None),
        P(FSDP, "tp"),
        P(FSDP_TP_TOWER, None),
        P(FSDP_TOWER),
        P(FSDP_TOWER),
    )
    return jax.shard_map(
        local,
        mesh=finer,
        in_specs=placed,
        out_specs=(P(FSDP_TOWER), P(FSDP, "tp")),
        check_vma=False,
    )
```

profile of v0, /device:TPU:2, one launch (start us, length us, event | category | flops | bytes accessed | tf_op | source)
XLA Modules:
  0.0 273.6 jit_solution(9530620597705469932)
XLA Ops:
  7.2 0.0 all-gather.4.cloned.1.call-start
  7.2 7.9 %all-gather = bf16[128,1024]{1,0:T(8,128)(2,1)} all-gather(bf16[64,1024]{1,0:T(8,128)(2,1)} %param.7), channel_id=2, replica_groups=mesh['fsdp_0'=4,'fsdp_1'=4,'tp'=8,'tower'=2] {'tower'}, dimensions={0}, use_global_device_ids=true | all-gather | bytes 393216 | tf_op jit(solution)/shard_map/all_gather | solution.py:35
  15.1 0.0 all-gather.4.cloned.1.call-update
  15.2 0.0 all-gather.6.cloned.1.call-start
  15.2 28.8 %all-gather.4.cloned.1.call-done = bf16[8,64,1024]{2,1,0:T(8,128)(2,1)} async-done(((bf16[2,64,1024]{2,1,0:T(8,128)(2,1)}), bf16[8,64,1024]{2,1,0:T(8,128)(2,1)}) %all-gather.4.cloned.1.call-update) | async-done | bytes 1048592 | tf_op jit(solution)/shard_map/all_gather | solution.py:35
  44.1 0.0 all-gather.6.cloned.1.call-update
  44.1 1.1 broadcast_in_dim.29
  45.2 30.1 %all_to_all.35 = bf16[16,320,128]{2,1,0:T(8,128)(2,1)S(1)} all-to-all(bf16[16,320,128]{2,1,0:T(8,128)(2,1)S(1)} %broadcast_in_dim.29), channel_id=1, replica_groups=mesh['fsdp_0'=4,'fsdp_1'=4,'tp'=8,'tower'=2] {'fsdp_0','fsdp_1'}, dimensions={0} | all-to-all | bytes 2621440 | tf_op jit(solution)/shard_map/all_to_all | solution.py:18
  75.3 4.4 %convolution_convert_fusion = bf16[512,128]{0,1:T(8,128)(2,1)S(1)} fusion(bf16[512,5120]{1,0:T(8,128)(2,1)} %param.5, bf16[5120,128]{1,0:T(8,128)(2,1)S(1)} %bitcast.40), kind=kOutput, calls=%fused_computation.21 | convolution fusion | flops 671154176 | bytes 6684672 | tf_op jit(solution)/shard_map/dot_general | solution.py:93
  79.7 1.1 broadcast_in_dim.30
  80.8 7.0 %all-to-all-start.1 = ((bf16[8,512,128]{1,2,0:T(8,128)(2,1)}), bf16[8,512,128]{1,2,0:T(8,128)(2,1)S(1)}, u32[]{:S(2)}, u32[]{:S(2)}) async-start(bf16[8,512,128]{1,2,0:T(8,128)(2,1)} %broadcast_in_dim.30), calls=%async_computation.1 | async-start | bytes 2097152 | tf_op jit(solution)/shard_map/all_to_all | solution.py:18
  87.9 28.9 %all-to-all-done.1 = bf16[8,512,128]{1,2,0:T(8,128)(2,1)S(1)} async-done(((bf16[8,512,128]{1,2,0:T(8,128)(2,1)}), bf16[8,512,128]{1,2,0:T(8,128)(2,1)S(1)}, u32[]{:S(2)}, u32[]{:S(2)}) %all-to-all-start.1) | async-done | bytes 1048608 | tf_op jit(solution)/shard_map/all_to_all | solution.py:18
  116.7 0.3 fusion.4
  117.0 0.2 fusion.5
  117.2 0.0 all-gather.6.cloned.1.call-done
  117.3 2.6 copy.21
  119.9 0.0 copy-start
  119.9 0.0 copy-start.2
  119.9 2.5 multiply_reduce_fusion
  122.4 0.0 copy-done
  122.4 0.0 copy-start.1
  122.4 0.0 copy-start.3
  122.4 2.0 copy-done.1
  124.4 0.0 copy-done.2
  124.4 1.8 exponential_reduce_fusion
  126.1 0.6 broadcast_in_dim.33
  126.8 3.4 %all-to-all-start.2 = ((f32[8,3,512]{2,1,0:T(4,128)}), f32[8,3,512]{2,1,0:T(4,128)S(1)}, u32[]{:S(2)}, u32[]{:S(2)}) async-start(f32[8,3,512]{2,1,0:T(4,128)} %broadcast_in_dim.33), calls=%async_computation.2 | async-start | bytes 131072 | tf_op jit(solution)/shard_map/all_to_all | solution.py:18
  130.1 0.0 copy-done.3
  130.2 8.4 %all-to-all-done.2 = f32[8,3,512]{2,1,0:T(4,128)S(1)} async-done(((f32[8,3,512]{2,1,0:T(4,128)}), f32[8,3,512]{2,1,0:T(4,128)S(1)}, u32[]{:S(2)}, u32[]{:S(2)}) %all-to-all-start.2) | async-done | bytes 49184 | tf_op jit(solution)/shard_map/all_to_all | solution.py:18
  138.9 5.8 %multiply_bitcast_fusion = f32[64,8,8,128]{3,2,1,0:T(8,128)S(1)} fusion(bf16[2048,1024]{1,0:T(8,128)(2,1)} %bitcast.42, f32[512,2048]{1,0:T(8,128)} %copy-done.1, f32[512]{0:T(512)S(1)} %bitcast.51, f32[512]{0:T(512)S(1)} %multiply_subtract_fusion, s32[2048]{0:T(1024)S(1)} %fusion.26, s32[512]{0:T(512)S(1)} %copy-done.2), kind=kOutput, calls=%fused_computation.15 | convolution fusion | flops 2155347968 | bytes 10500096 | tf_op jit(solution)/shard_map/dot_general | solution.py:127
  144.7 0.1 copy.37
  144.8 54.2 %all_to_all.36 = f32[8,512,128]{2,1,0:T(8,128)S(1)} all-to-all(f32[8,512,128]{2,1,0:T(8,128)S(1)} %bitcast.39), channel_id=1, replica_groups=mesh['fsdp_0'=4,'fsdp_1'=4,'tp'=8,'tower'=2] {'tp'}, dimensions={0} | all-to-all | bytes 4194304 | tf_op jit(solution)/shard_map/all_to_all | solution.py:83
  199.0 0.1 reduce_sum.75
  199.1 0.1 copy.26
  199.3 0.1 multiply_reduce_fusion.1
  199.3 10.2 %all_to_all.37 = f32[8,512,1]{1,2,0:T(1,128)S(1)} all-to-all(f32[8,512,1]{1,2,0:T(1,128)S(1)} %broadcast_in_dim.34), channel_id=1, replica_groups=mesh['fsdp_0'=4,'fsdp_1'=4,'tp'=8,'tower'=2] {'tp'}, dimensions={0} | all-to-all | bytes 32768 | tf_op jit(solution)/shard_map/all_to_all | solution.py:18
  209.5 4.8 %convolution_bitcast_fusion = f32[5120,128]{0,1:T(8,128)} fusion(bf16[512,5120]{1,0:T(8,128)(2,1)} %param.5, f32[512,128]{0,1:T(8,128)S(1)} %copy.26, bf16[512,128]{0,1:T(8,128)(2,1)S(1)} %convolution_convert_fusion, f32[512]{0:T(512)S(1)} %reduce_sum.77, f32[512]{0:T(512)S(1)} %add_rsqrt_fusion), kind=kOutput, calls=%fused_computation | convolution fusion | flops 671481856 | bytes 8261632 | tf_op jit(solution)/shard_map/dot_general | solution.py:140
  214.4 2.1 copy.27
  216.5 38.0 %all_to_all.38 = f32[16,320,128]{2,1,0:T(8,128)} all-to-all(f32[16,320,128]{2,1,0:T(8,128)S(1)} %bitcast.38), channel_id=1, replica_groups=mesh['fsdp_0'=4,'fsdp_1'=4,'tp'=8,'tower'=2] {'fsdp_0','fsdp_1'}, dimensions={0} | all-to-all | bytes 5242880 | tf_op jit(solution)/shard_map/all_to_all | solution.py:83
  254.5 1.9 reduce_sum.78
  256.4 0.7 broadcast_in_dim.35
  257.1 3.5 %all-to-all-start.6 = ((f32[2,320,128]{2,1,0:T(8,128)}), f32[2,320,128]{2,1,0:T(8,128)S(1)}, u32[]{:S(2)}, u32[]{:S(2)}) async-start(f32[2,320,128]{2,1,0:T(8,128)} %broadcast_in_dim.35), calls=%async_computation.6 | async-start | bytes 655360 | tf_op jit(solution)/shard_map/all_to_all | solution.py:18
  260.7 0.6 sub.64
  261.3 4.8 %all-to-all-done.6 = f32[2,320,128]{2,1,0:T(8,128)S(1)} async-done(((f32[2,320,128]{2,1,0:T(8,128)}), f32[2,320,128]{2,1,0:T(8,128)S(1)}, u32[]{:S(2)}, u32[]{:S(2)}) %all-to-all-start.6) | async-done | bytes 327712 | tf_op jit(solution)/shard_map/all_to_all | solution.py:18
  266.1 0.7 reduce_sum.79
  (27 shorter events, 0.5 us)
Async XLA Ops:
  7.2 36.9 %all-gather.4.cloned.1.call-start = ((), (), s32[]{:S(2)}) async-start(), calls=%async_computation.7 | async-start | bytes 1310720 | tf_op jit(solution)/shard_map/all_gather | solution.py:35
  15.2 102.1 %all-gather.6.cloned.1.call-start = ((), (), s32[]{:S(2)}) async-start(), calls=%async_computation.8 | async-start | bytes 5242880 | tf_op jit(solution)/shard_map/all_gather | solution.py:35
  80.8 35.9 %all-to-all-start.1 = ((bf16[8,512,128]{1,2,0:T(8,128)(2,1)}), bf16[8,512,128]{1,2,0:T(8,128)(2,1)S(1)}, u32[]{:S(2)}, u32[]{:S(2)}) async-start(bf16[8,512,128]{1,2,0:T(8,128)(2,1)} %broadcast_in_dim.30), calls=%async_computation.1 | async-start | bytes 2097152 | tf_op jit(solution)/shard_map/all_to_all | solution.py:18
  119.9 2.5 copy-start
  119.9 4.5 %copy-start.2 = (s32[512]{0:T(512)S(1)}, s32[512]{0:T(512)}, u32[]{:S(2)}) copy-start(s32[512]{0:T(512)} %param.8) | copy-start | bytes 6148
  122.4 2.0 copy-start.1
  122.4 7.8 %copy-start.3 = (s32[512]{0:T(512)S(1)}, s32[512]{0:T(512)}, u32[]{:S(2)}) copy-start(s32[512]{0:T(512)} %param.9) | copy-start | bytes 6148
  126.8 11.8 %all-to-all-start.2 = ((f32[8,3,512]{2,1,0:T(4,128)}), f32[8,3,512]{2,1,0:T(4,128)S(1)}, u32[]{:S(2)}, u32[]{:S(2)}) async-start(f32[8,3,512]{2,1,0:T(4,128)} %broadcast_in_dim.33), calls=%async_computation.2 | async-start | bytes 131072 | tf_op jit(solution)/shard_map/all_to_all | solution.py:18
  257.1 9.0 %all-to-all-start.6 = ((f32[2,320,128]{2,1,0:T(8,128)}), f32[2,320,128]{2,1,0:T(8,128)S(1)}, u32[]{:S(2)}, u32[]{:S(2)}) async-start(f32[2,320,128]{2,1,0:T(8,128)} %broadcast_in_dim.35), calls=%async_computation.6 | async-start | bytes 655360 | tf_op jit(solution)/shard_map/all_to_all | solution.py:18
Sparse Core Ops, SparseCore 0:
  15.3 28.7 all-gather.3
  45.9 53.7 all-gather.5
where the time goes:
time: 274 us
  blocking collectives  140 us (51%)
  waiting for transfers between devices  70.9 us (26%)
  matrix products  17.5 us (6%)
  between operations  14.2 us (5%)
  starting transfers between devices  13.9 us (5%)
  local copies, waits for them, and re-layouts  11 us (4%)
  other arithmetic  5.72 us (2%)
    all_to_all x2, blocking collectives, summed_on_arrival(): parts = lax.all_to_all(cut_along(x, dim, peers), axis, 0, 0, tiled=True)  92.2 us
    all_to_all x3, waiting for transfers between devices, copy_for_each(): return lax.all_to_all(copies, axis, split_axis=0, concat_axis=0, tiled=True)  42 us
    all_to_all x2, blocking collectives, copy_for_each(): return lax.all_to_all(copies, axis, split_axis=0, concat_axis=0, tiled=True)  40.3 us
    all_gather x2, waiting for transfers between devices, stacked_from(): parts = lax.all_gather(parts, axes[k], axis=0, tiled=True)  28.9 us
    all_to_all x3, starting transfers between devices, copy_for_each(): return lax.all_to_all(copies, axis, split_axis=0, concat_axis=0, tiled=True)  13.8 us
    all_gather x1, blocking collectives, stacked_from(): parts = lax.all_gather(parts, axes[k], axis=0, tiled=True)  7.94 us
    dot_general x1, matrix products, local(): jnp.dot((signs[:, None] * (jnp.exp(logits - lse[:, None]) - hit.astype(jn...  5.78 us
  transfers between devices with their start and end apart: 5, of which 4 were waited for; matrix products, arithmetic and copies ran while one was open for 3% of the time, Pallas kernels for 0%

commit v1 on v0

v1 whole, which is shorter than its diff:
```python
import jax
import jax.numpy as jnp
from jax import lax
from jax.experimental import pallas as pl
from jax.experimental.pallas import tpu as pltpu
from jax.sharding import Mesh
from jax.sharding import PartitionSpec as P

AXES = ("y", "x", "zh", "core", "tw")
PLANE = ("y", "x")
FSDP_TOWER = ("y", "x", "tw")
REL = (0, 3, 1, 2)

epsilon = 1e-06
score_scale = 100.0
f32 = jnp.float32
bf16 = jnp.bfloat16
VMEM = pl.BlockSpec(memory_space=pltpu.VMEM)
HBM = pl.BlockSpec(memory_space=pltpu.HBM)
SMEM = pl.BlockSpec(memory_space=pltpu.SMEM)


def shifted(x, axis, step):
    n = lax.axis_size(axis)
    return lax.ppermute(x, axis, [(i, (i + step) % n) for i in range(n)])


def in_hbm(x):
    return pltpu.with_memory_space_constraint(x, pltpu.HBM)


def exchanged(x, axis):
    return lax.all_to_all(x, axis, 0, 0, tiled=True)


def from_all(x, axis):
    return exchanged(jnp.broadcast_to(x, (lax.axis_size(axis), *x.shape)), axis)


def gathered_texts(texts, other_texts):
    pieces = []
    for part, inner, outer in ((texts, "x", "y"), (other_texts, "y", "x")):
        below, above, far = (shifted(part, inner, step) for step in (1, -1, 2))
        halves = [jnp.concatenate([part, below]), jnp.concatenate([above, far])]
        for half, toward in zip(halves, (1, -1)):
            first = shifted(half, outer, toward)
            second = shifted(half, outer, -toward)
            far = shifted(first, outer, toward)
            pieces += [half, first, second, far] if toward == 1 else [half, second, first, far]
    return [in_hbm(piece) for piece in pieces]


def fetch(pieces, whole, sem):
    at, copies = 0, []
    for k, piece in enumerate(pieces):
        n = piece.shape[0]
        copies.append(pltpu.make_async_copy(piece, whole.at[pl.ds(at, n)], sem.at[k]))
        at += n
    for copy in copies:
        copy.start()
    return copies


def column_places(at_ref, group):
    y, x, tp, tower = (at_ref[k] for k in range(4))
    lane = lax.broadcasted_iota(jnp.int32, (1, 128), 1)
    places = []
    for side in range(2):
        tw = tower if side == 0 else 1 - tower
        for half in range(2):
            for step in REL:
                firsts = []
                for inner in REL[2 * half : 2 * half + 2]:
                    ahead = (step, inner) if side == 0 else (inner, step)
                    plane = lax.rem(y + ahead[0], 4) * 4 + lax.rem(x + ahead[1], 4)
                    firsts.append(((plane * 8 + tp) * 2 + tw) * group)
                places.append(jnp.where(lane < group, firsts[0], firsts[1] - group) + lane)
    return places


def as_columns(lines):
    n = lines[0].shape[1]
    spare = jnp.zeros((128 - len(lines), n), f32)
    return jnp.concatenate([*lines, spare], axis=0).T


def embed_kernel(images_ref, weight_ref, out_ref, total):
    k = pl.program_id(0)

    @pl.when(k == 0)
    def _():
        total[...] = jnp.zeros_like(total)

    total[...] += jnp.dot(images_ref[...], weight_ref[...], preferred_element_type=f32)

    @pl.when(k == pl.num_programs(0) - 1)
    def _():
        rounded = total[...].astype(bf16)
        for z in range(out_ref.shape[0]):
            out_ref[z] = rounded


def score_kernel(n_pieces, group, *refs):
    at_ref, mine_ref, theirs_ref, perm_ref = refs[:4]
    pieces = refs[4 : 4 + n_pieces]
    out_ref, stats_ref = refs[4 + n_pieces : 6 + n_pieces]
    whole, unit, score, high, soft, sem, out_sem = refs[6 + n_pieces :]
    copies = fetch(pieces, whole, sem)
    rows, feats = mine_ref.shape[1], mine_ref.shape[2]
    core = lax.rem(at_ref[2], 2)

    square = jnp.zeros((rows, feats), f32)
    for k in range(4):
        for ref in (mine_ref, theirs_ref):
            part = ref[k].astype(f32)
            square += part * part
    rnorm = lax.rsqrt(jnp.sum(square, axis=1, keepdims=True) + epsilon)
    for k in range(4):
        for ref, which in ((mine_ref, core), (theirs_ref, 1 - core)):
            to = pl.multiple_of((2 * k + which) * feats, feats)
            unit[:, pl.ds(to, feats)] = (ref[k].astype(f32) * rnorm).astype(bf16)
    high[...] = jnp.full_like(high, -jnp.inf)

    for copy in copies:
        copy.wait()
    step = 256

    @pl.loop(0, whole.shape[0] // step)
    def _(c):
        at = pl.multiple_of(c * step, step)
        chunk = score_scale * lax.dot_general(
            unit[...], whole[pl.ds(at, step)], (((1,), (1,)), ((), ())), preferred_element_type=f32
        )
        score[:, pl.ds(at, step)] = chunk
        high[...] = jnp.maximum(high[...], jnp.maximum(chunk[:, :128], chunk[:, 128:]))

    places = column_places(at_ref, group)
    band = 64

    @pl.loop(0, rows // band)
    def _(r):
        here = pl.ds(pl.multiple_of(r * band, band), band)
        perm = perm_ref[here, :]
        top = jnp.max(high[here, :], axis=1, keepdims=True)
        total = jnp.zeros((band, 128), f32)
        moment = jnp.zeros((band, 128), f32)
        found = jnp.zeros((band, 128), f32)
        for k in range(len(places)):
            cols = pl.ds(k * 128, 128)
            logit = score[here, cols]
            p = jnp.exp(logit - top)
            hit = perm == places[k]
            total += p
            moment += p * logit
            found += jnp.where(hit, logit, 0.0)
            soft[here, cols] = jnp.where(hit, 0.0, p).astype(bf16)
        pltpu.make_async_copy(soft.at[here], out_ref.at[here], out_sem).start()
        sums = [jnp.sum(v, axis=1, keepdims=True) for v in (total, moment, found)]
        which = lax.broadcasted_iota(jnp.int32, (band, 128), 1)
        tile = jnp.where(which == 0, top, 0.0)
        for k, v in enumerate(sums):
            tile = jnp.where(which == k + 1, v, tile)
        high[here, :] = tile

    which = lax.broadcasted_iota(jnp.int32, (rows, 128), 1)
    lines = jnp.where(which == 4, rnorm, high[...]).T
    stats_ref[...] = lines[:8]
    pltpu.make_async_copy(soft, out_ref, out_sem).wait()


def gradient_kernel(n_pieces, group, *refs):
    at_ref, perm_ref, p_ref = refs[:3]
    pieces = refs[3 : 3 + n_pieces]
    soft_ref, hard_ref = refs[3 + n_pieces : 5 + n_pieces]
    whole, both, sem, p_sem = refs[5 + n_pieces :]
    rows = soft_ref.shape[0]
    copies = [pltpu.make_async_copy(p_ref, both.at[pl.ds(0, rows)], p_sem)]
    copies[0].start()
    copies += fetch(pieces, whole, sem)
    places = column_places(at_ref, group)
    band = 64

    @pl.loop(0, rows // band)
    def _(r):
        at = pl.multiple_of(r * band, band)
        perm = perm_ref[pl.ds(at, band), :]
        for k in range(len(places)):
            both[pl.ds(at + rows, band), pl.ds(k * 128, 128)] = jnp.where(
                perm == places[k], 1.0, 0.0
            ).astype(bf16)

    for copy in copies:
        copy.wait()
    step = 256

    @pl.loop(0, whole.shape[1] // step)
    def _(c):
        cols = pl.ds(pl.multiple_of(c * step, step), step)
        out = jnp.dot(both[...], whole[:, cols], preferred_element_type=f32)
        soft_ref[:, cols] = out[:rows]
        hard_ref[:, cols] = out[rows:].astype(bf16)


def combine_kernel(at_ref, own_ref, every_ref, sign_ref, soft_ref, hard_ref, keep_ref, give_ref, lines_ref):
    core = lax.rem(at_ref[2], 2)
    feats = keep_ref.shape[2]
    rest = [every_ref[k] for k in range(every_ref.shape[0])]
    tops = [v[0:1] for v in rest]
    high = tops[0]
    for t in tops[1:]:
        high = jnp.maximum(high, t)
    scales = [jnp.exp(t - high) for t in tops]
    mass = sum(s * v[1:2] for s, v in zip(scales, rest))
    lse = high + jnp.log(mass)
    target = sum(v[3:4] for v in rest)
    mean = sum(jnp.exp(t - lse) * v[2:3] for t, v in zip(tops, rest))
    sign = sign_ref[...]
    lines_ref[0:1] = lse - target
    lines_ref[1:2] = sign * (mean - target)
    lines_ref[2:3] = own_ref[4:5]
    for_soft = score_scale * sign * jnp.exp(own_ref[0:1] - lse)
    weight = (sign * (jnp.exp(target - lse) - 1.0)).astype(bf16).astype(f32)
    cols = as_columns([for_soft, score_scale * weight])
    first, second = cols[:, 0:1], cols[:, 1:2]
    for k in range(4):
        for out, which in ((keep_ref, core), (give_ref, 1 - core)):
            at = pl.ds(pl.multiple_of((2 * k + which) * feats, feats), feats)
            out[k] = first * soft_ref[:, at] + second * hard_ref[:, at].astype(f32)


def local(images, img_weight, texts, pair_perm, forget):
    y, x, zh = (lax.axis_index(a) for a in ("y", "x", "zh"))
    core, tower = lax.axis_index("core"), lax.axis_index("tw")
    rows, width = images.shape
    feats = img_weight.shape[1]
    group = texts.shape[0]
    at = jnp.stack([y, x, zh * 2 + core, tower]).astype(jnp.int32)
    signs = 1.0 - 2.0 * forget.astype(f32)
    perm = pair_perm.reshape(rows, 1)

    weight = from_all(img_weight, PLANE).reshape(width, feats)
    other_texts = shifted(texts, "tw", 1)
    pieces = gathered_texts(texts, other_texts)
    n = len(pieces)
    texts_here = sum(piece.shape[0] for piece in pieces)
    embed = pieces[0].shape[1]

    block = 640
    emb_copies = pl.pallas_call(
        embed_kernel,
        name="embed",
        grid=(width // block,),
        out_shape=jax.ShapeDtypeStruct((4, rows, feats), bf16),
        in_specs=[
            pl.BlockSpec((rows, block), lambda k: (0, k)),
            pl.BlockSpec((block, feats), lambda k: (k, 0)),
        ],
        out_specs=pl.BlockSpec((4, rows, feats), lambda k: (0, 0, 0)),
        scratch_shapes=[pltpu.VMEM((rows, feats), f32)],
        compiler_params=pltpu.CompilerParams(vmem_limit_bytes=8 << 20),
        cost_estimate=pl.CostEstimate(
            flops=2 * rows * width * feats, bytes_accessed=7 << 20, transcendentals=0
        ),
    )(in_hbm(images), weight)
    emb_part = emb_copies[0]
    mine = exchanged(emb_copies, "zh")
    theirs = shifted(mine, "core", 1)

    p, stats = pl.pallas_call(
        lambda *refs: score_kernel(n, group, *refs),
        name="scores",
        out_shape=(
            pltpu.HBM((rows, texts_here), bf16),
            jax.ShapeDtypeStruct((8, rows), f32),
        ),
        in_specs=[SMEM, VMEM, VMEM, VMEM, *[HBM] * n],
        out_specs=(HBM, VMEM),
        scratch_shapes=[
            pltpu.VMEM((texts_here, embed), bf16),
            pltpu.VMEM((rows, embed), bf16),
            pltpu.VMEM((rows, texts_here), f32),
            pltpu.VMEM((rows, 128), f32),
            pltpu.VMEM((rows, texts_here), bf16),
            pltpu.SemaphoreType.DMA((n,)),
            pltpu.SemaphoreType.DMA,
        ],
        compiler_params=pltpu.CompilerParams(vmem_limit_bytes=20 << 20),
        cost_estimate=pl.CostEstimate(
            flops=2 * rows * texts_here * embed,
            bytes_accessed=8 << 20,
            transcendentals=rows * texts_here,
        ),
    )(at, mine, theirs, perm, *pieces)

    every = from_all(stats, ("zh", "core"))

    soft, hard = pl.pallas_call(
        lambda *refs: gradient_kernel(n, group, *refs),
        name="gradient",
        out_shape=(
            jax.ShapeDtypeStruct((rows, embed), f32),
            jax.ShapeDtypeStruct((rows, embed), bf16),
        ),
        in_specs=[SMEM, VMEM, HBM, *[HBM] * n],
        out_specs=(VMEM, VMEM),
        scratch_shapes=[
            pltpu.VMEM((texts_here, embed), bf16),
            pltpu.VMEM((2 * rows, texts_here), bf16),
            pltpu.SemaphoreType.DMA((n,)),
            pltpu.SemaphoreType.DMA,
        ],
        compiler_params=pltpu.CompilerParams(vmem_limit_bytes=20 << 20),
        cost_estimate=pl.CostEstimate(
            flops=4 * rows * texts_here * embed, bytes_accessed=10 << 20, transcendentals=0
        ),
    )(at, perm, in_hbm(p), *pieces)

    keep, give, lines = pl.pallas_call(
        combine_kernel,
        name="combine",
        out_shape=(
            jax.ShapeDtypeStruct((4, rows, feats), f32),
            jax.ShapeDtypeStruct((4, rows, feats), f32),
            jax.ShapeDtypeStruct((8, rows), f32),
        ),
        in_specs=[SMEM, VMEM, VMEM, VMEM, VMEM, VMEM],
        out_specs=(VMEM, VMEM, VMEM),
        compiler_params=pltpu.CompilerParams(vmem_limit_bytes=20 << 20),
    )(at, stats, every, signs.reshape(1, rows), soft, hard)

    pair_loss, radial, rnorm = lines[0], lines[1], lines[2]
    chip = keep + shifted(give, "core", 1)
    parts = exchanged(chip.astype(bf16), "zh")
    mask = (jnp.arange(4) == zh)[:, None, None]
    grad_unit = jnp.sum(jnp.where(mask, chip, parts.astype(f32)), axis=0)
    unit_part = emb_part.astype(f32) * rnorm[:, None]
    grad_emb = (rnorm[:, None] * (grad_unit - unit_part * radial[:, None])).astype(bf16)
    share = lax.dot_general(
        images, grad_emb, (((0,), (0,)), ((), ())), preferred_element_type=f32
    ).astype(bf16)
    summed = jnp.sum(exchanged(share.reshape(16, -1, feats), PLANE).astype(f32), axis=0)
    weight_grad = summed + shifted(summed, "tw", 1)
    return (pair_loss, weight_grad)


def solution(mesh):
    finer = Mesh(mesh.devices.reshape(4, 4, 4, 2, mesh.shape["tower"]), AXES)
    return jax.shard_map(
        local,
        mesh=finer,
        in_specs=(
            P(FSDP_TOWER, None),
            P(PLANE, ("zh", "core")),
            P(("y", "x", "zh", "core", "tw"), None),
            P(FSDP_TOWER),
            P(FSDP_TOWER),
        ),
        out_specs=(P(FSDP_TOWER), P(PLANE, ("zh", "core"))),
        check_vma=False,
    )
```

time: 274 us -> 181 us (0.66)
  blocking collectives: 140 us -> 22 us
  starting transfers between devices: 13.9 us -> 57.5 us
  Pallas kernels: 0 us -> 27.6 us
  matrix products: 17.5 us -> 3.58 us
  between operations: 14.2 us -> 0.92 us
  waiting for transfers between devices: 70.9 us -> 58.2 us
  local copies, waits for them, and re-layouts: 11 us -> 7.19 us
  other arithmetic: 5.72 us -> 2.68 us
    all_to_all x4 -> x1, blocking collectives: 132 us -> 22 us  [exchanged(): return lax.all_to_all(x, axis, 0, 0, tiled=True)]
    ppermute x0 -> x22, waiting for transfers between devices: none -> 29.9 us  [shifted(): return lax.ppermute(x, axis, [(i, (i + step) % n) for i in range(n)])]
    all_gather x2 -> x0, waiting for transfers between devices: 28.9 us -> none  [stacked_from(): parts = lax.all_gather(parts, axes[k], axis=0, tiled=True)]
    ppermute x0 -> x22, starting transfers between devices: none -> 27.8 us  [shifted(): return lax.ppermute(x, axis, [(i, (i + step) % n) for i in range(n)])]
    pallas_call x0 -> x4, Pallas kernels: none -> 27.6 us  [the longest x1 10.3 us: local(): pl.pallas_call(lambda *refs: score_kernel(n, group, *refs), name='scores'...]
    all_to_all x3 -> x4, starting transfers between devices: 13.8 us -> 29.7 us  [exchanged(): return lax.all_to_all(x, axis, 0, 0, tiled=True)]
    dot_general x4 -> x1, matrix products: 17.5 us -> 3.58 us  [local(): lax.dot_general(images, grad_emb, (((0,), (0,)), ((), ())), preferred_ele...]
    all_to_all x3 -> x4, waiting for transfers between devices: 42 us -> 28.3 us  [exchanged(): return lax.all_to_all(x, axis, 0, 0, tiled=True)]
  transfers between devices with their start and end apart: 5 -> 26, of which waited for: 4 -> 13; matrix products, arithmetic and copies ran while one was open for 3% -> 1% of each run, Pallas kernels for 0% -> 9%
where the time goes in v1:
time: 181 us; the launch traced here: 180 us
  waiting for transfers between devices  58.2 us (32%)
  starting transfers between devices  57.5 us (32%)
  Pallas kernels  27.6 us (15%)
  blocking collectives  22 us (12%)
  local copies, waits for them, and re-layouts  7.19 us (4%)
  matrix products  3.58 us (2%)
  other arithmetic  2.68 us (1%)
    ppermute x22, waiting for transfers between devices, shifted(): return lax.ppermute(x, axis, [(i, (i + step) % n) for i in range(n)])  29.9 us
    all_to_all x4, starting transfers between devices, exchanged(): return lax.all_to_all(x, axis, 0, 0, tiled=True)  29.7 us
    all_to_all x4, waiting for transfers between devices, exchanged(): return lax.all_to_all(x, axis, 0, 0, tiled=True)  28.3 us
    ppermute x22, starting transfers between devices, shifted(): return lax.ppermute(x, axis, [(i, (i + step) % n) for i in range(n)])  27.8 us
    all_to_all x1, blocking collectives, exchanged(): return lax.all_to_all(x, axis, 0, 0, tiled=True)  22 us
    pallas_call x1, Pallas kernels, local(): pl.pallas_call(lambda *refs: score_kernel(n, group, *refs), name='scores'...  10.3 us
    pallas_call x1, Pallas kernels, local(): pl.pallas_call(lambda *refs: gradient_kernel(n, group, *refs), name='grad...  8.7 us
    pallas_call x1, Pallas kernels, local(): pl.pallas_call(embed_kernel, name='embed', grid=(width // block,), out_sh...  7.09 us
  transfers between devices with their start and end apart: 26, of which 13 were waited for; matrix products, arithmetic and copies ran while one was open for 1% of the time, Pallas kernels for 9%

profile of v1, /device:TPU:2, one launch (start us, length us, event | category | flops | bytes accessed | tf_op | source)
XLA Modules:
  0.0 179.7 jit_solution(18383434699749561963)
XLA Ops:
  0.6 2.3 %broadcast_in_dim.15 = bf16[16,320,128]{2,1,0:T(8,128)(2,1)} broadcast(bf16[320,128]{1,0:T(8,128)(2,1)} %param.6), dimensions={1,2} | broadcast | bytes 1392640 | tf_op jit(solution)/shard_map/broadcast_in_dim | solution.py:37
  2.9 7.5 %all-to-all-start = ((bf16[16,320,128]{2,1,0:T(8,128)(2,1)}), bf16[16,320,128]{2,1,0:T(8,128)(2,1)S(1)}, u32[]{:S(2)}, u32[]{:S(2)}) async-start(bf16[16,320,128]{2,1,0:T(8,128)(2,1)} %broadcast_in_dim.15), calls=%async_computation | async-start | bytes 2621440 | tf_op jit(solution)/shard_map/all_to_all | solution.py:33
  10.4 2.0 %collective-permute-start.10 = (bf16[64,1024]{1,0:T(8,128)(2,1)S(1)}, bf16[64,1024]{1,0:T(8,128)(2,1)S(1)}, u32[]{:S(2)}, u32[]{:S(2)}) collective-permute-start(bf16[64,1024]{1,0:T(8,128)(2,1)S(1)} %copy-done.4), channel_id=1, source_target_pairs={{0,1},{1,0},{2,3},{3,2},{4,5},{5,4},{6,7},{7,6},{8,9},{9,8},{10,11... | collective-permute-start | bytes 393224 | tf_op jit(solution)/shard_map/ppermute | solution.py:25
  12.4 0.1 collective-permute-start.5
  12.5 2.8 %collective-permute-start.6 = (bf16[64,1024]{1,0:T(8,128)(2,1)S(1)}, bf16[64,1024]{1,0:T(8,128)(2,1)S(1)}, u32[]{:S(2)}, u32[]{:S(2)}) collective-permute-start(bf16[64,1024]{1,0:T(8,128)(2,1)S(1)} %copy-done.4), channel_id=1, source_target_pairs={{0,32},{16,48},{32,0},{48,16},{1,33},{17,49},{33,1},{49,17},{2,34}... | collective-permute-start | bytes 393224 | tf_op jit(solution)/shard_map/ppermute | solution.py:25
  15.3 1.8 collective-permute-start.1
  17.1 13.2 %all-to-all-done = bf16[16,320,128]{2,1,0:T(8,128)(2,1)S(1)} async-done(((bf16[16,320,128]{2,1,0:T(8,128)(2,1)}), bf16[16,320,128]{2,1,0:T(8,128)(2,1)S(1)}, u32[]{:S(2)}, u32[]{:S(2)}) %all-to-all-start) | async-done | bytes 1310752 | tf_op jit(solution)/shard_map/all_to_all | solution.py:33
  30.4 7.1 %embed.1 = bf16[4,512,128]{2,1,0:T(8,128)(2,1)} custom-call(bf16[512,5120]{1,0:T(8,128)(2,1)} %images_ref.1, bf16[5120,128]{1,0:T(8,128)(2,1)S(1)} %bitcast.20), custom_call_target="tpu_custom_call" | custom-call | flops 671088640 | bytes 7340032 | tf_op jit(solution)/shard_map/embed/pallas_call | solution.py:249
  37.4 8.6 %all-to-all-start.1 = ((bf16[4,512,128]{2,1,0:T(8,128)(2,1)}), bf16[4,512,128]{2,1,0:T(8,128)(2,1)S(1)}, u32[]{:S(2)}, u32[]{:S(2)}) async-start(bf16[4,512,128]{2,1,0:T(8,128)(2,1)} %embed.1), calls=%async_computation.1 | async-start | bytes 1048576 | tf_op jit(solution)/shard_map/all_to_all | solution.py:33
  46.1 0.9 collective-permute-start.8
  47.0 1.2 collective-permute-start.7
  48.2 0.0 collective-permute-done.10
  48.2 2.1 %collective-permute-start.15 = (bf16[64,1024]{1,0:T(8,128)(2,1)S(1)}, bf16[64,1024]{1,0:T(8,128)(2,1)S(1)}, u32[]{:S(2)}, u32[]{:S(2)}) collective-permute-start(bf16[64,1024]{1,0:T(8,128)(2,1)S(1)} %collective-permute-done.10), channel_id=1, source_target_pairs={{0,192},{64,0},{128,64},{192,128},{1,193},{65,1},{129,65},{193,129... | collective-permute-start | bytes 393224 | tf_op jit(solution)/shard_map/ppermute | solution.py:25
  50.3 0.0 collective-permute-done.1
  50.3 0.1 collective-permute-start.2
  50.4 1.5 collective-permute-start.16
  51.9 4.3 %collective-permute-done.15 = bf16[64,1024]{1,0:T(8,128)(2,1)S(1)} collective-permute-done((bf16[64,1024]{1,0:T(8,128)(2,1)S(1)}, bf16[64,1024]{1,0:T(8,128)(2,1)S(1)}, u32[]{:S(2)}, u32[]{:S(2)}) %collective-permute-start.15) | collective-permute-done | bytes 131104 | tf_op jit(solution)/shard_map/ppermute | solution.py:25
  56.1 0.0 collective-permute-start.11
  56.2 8.0 %collective-permute-done.16 = bf16[64,1024]{1,0:T(8,128)(2,1)S(1)} collective-permute-done((bf16[64,1024]{1,0:T(8,128)(2,1)S(1)}, bf16[64,1024]{1,0:T(8,128)(2,1)S(1)}, u32[]{:S(2)}, u32[]{:S(2)}) %collective-permute-start.16) | collective-permute-done | bytes 131104 | tf_op jit(solution)/shard_map/ppermute | solution.py:25
  64.2 1.2 collective-permute-done.11
  65.4 0.9 collective-permute-start.18
  66.3 3.4 %collective-permute-start.12 = (bf16[128,1024]{1,0:T(8,128)(2,1)S(1)}, bf16[128,1024]{1,0:T(8,128)(2,1)}, u32[]{:S(2)}, u32[]{:S(2)}) collective-permute-start(bf16[128,1024]{1,0:T(8,128)(2,1)S(1)} %constant_dynamic-update-slice_fusion.4.refs_12_.refs_11_), channel_id=1, source_target_pairs={{0,16},{16,32},{32,48},{48,0},{1,17},{17,33},{33,49},{49,1},{2,18}... | collective-permute-start | bytes 786440 | tf_op jit(solution)/shard_map/ppermute | solution.py:25
  69.7 0.0 collective-permute-done.2.refs_5_.refs_4_
  69.7 2.0 %collective-permute-start.17 = (bf16[128,1024]{1,0:T(8,128)(2,1)S(1)}, bf16[128,1024]{1,0:T(8,128)(2,1)S(1)}, u32[]{:S(2)}, u32[]{:S(2)}) collective-permute-start(bf16[128,1024]{1,0:T(8,128)(2,1)S(1)} %constant_dynamic-update-slice_fusion.6.refs_16_.refs_15_), channel_id=1, source_target_pairs={{0,16},{16,32},{32,48},{48,0},{1,17},{17,33},{33,49},{49,1},{2,18}... | collective-permute-start | bytes 786440 | tf_op jit(solution)/shard_map/ppermute | solution.py:25
  71.7 0.0 collective-permute-done.7.refs_9_.refs_8_
  71.7 0.0 collective-permute-start.13
  71.7 0.0 all-to-all-done.1.refs_1_
  71.7 0.3 collective-permute-start
  72.0 4.8 %collective-permute-done.18.refs_18_.refs_17_ = bf16[128,1024]{1,0:T(8,128)(2,1)} collective-permute-done((bf16[128,1024]{1,0:T(8,128)(2,1)S(1)}, bf16[128,1024]{1,0:T(8,128)(2,1)}, u32[]{:S(2)}, u32[]{:S(2)}) %collective-permute-start.18) | collective-permute-done | bytes 262176 | tf_op jit(solution)/shard_map/ppermute | solution.py:25
  76.8 2.0 %collective-permute-start.4 = (bf16[128,1024]{1,0:T(8,128)(2,1)}, bf16[128,1024]{1,0:T(8,128)(2,1)}, u32[]{:S(2)}, u32[]{:S(2)}) collective-permute-start(bf16[128,1024]{1,0:T(8,128)(2,1)} %collective-permute-done.2.refs_5_.refs_4_), channel_id=1, source_target_pairs={{0,64},{64,128},{128,192},{192,0},{1,65},{65,129},{129,193},{193,1... | collective-permute-start | bytes 786440 | tf_op jit(solution)/shard_map/ppermute | solution.py:25
  78.9 0.8 collective-permute-done.17.refs_17_.refs_16_
  79.6 3.1 %collective-permute-start.19 = (bf16[128,1024]{1,0:T(8,128)(2,1)}, bf16[128,1024]{1,0:T(8,128)(2,1)}, u32[]{:S(2)}, u32[]{:S(2)}) collective-permute-start(bf16[128,1024]{1,0:T(8,128)(2,1)} %collective-permute-done.18.refs_18_.refs_17_), channel_id=1, source_target_pairs={{0,48},{16,0},{32,16},{48,32},{1,49},{17,1},{33,17},{49,33},{2,50}... | collective-permute-start | bytes 786440 | tf_op jit(solution)/shard_map/ppermute | solution.py:25
  82.7 0.0 collective-permute-start.14
  82.7 0.1 pad_add_fusion.refs_0_.at_ref
  82.8 0.6 copy-done.14
  83.5 0.1 copy.7.refs_3_.refs_1_
  83.6 0.6 multiply_subtract_fusion
  84.2 0.0 collective-permute-done.9.refs_11_.refs_10_
  84.2 0.5 collective-permute-done.4.refs_7_.refs_6_
  84.7 2.2 %collective-permute-done.19.refs_19_.refs_18_ = bf16[128,1024]{1,0:T(8,128)(2,1)} collective-permute-done((bf16[128,1024]{1,0:T(8,128)(2,1)}, bf16[128,1024]{1,0:T(8,128)(2,1)}, u32[]{:S(2)}, u32[]{:S(2)}) %collective-permute-start.19) | collective-permute-done | bytes 262176 | tf_op jit(solution)/shard_map/ppermute | solution.py:25
  86.9 2.5 %collective-permute-done.14.refs_15_.refs_14_ = bf16[128,1024]{1,0:T(8,128)(2,1)} collective-permute-done((bf16[128,1024]{1,0:T(8,128)(2,1)}, bf16[128,1024]{1,0:T(8,128)(2,1)}, u32[]{:S(2)}, u32[]{:S(2)}) %collective-permute-start.14) | collective-permute-done | bytes 262176 | tf_op jit(solution)/shard_map/ppermute | solution.py:25
  89.5 10.3 %scores.1 = (bf16[512,2048]{1,0:T(8,128)(2,1)}, f32[8,512]{1,0:T(8,128)S(1)}) custom-call(s32[4]{0:T(128)S(1)} %pad_add_fusion.refs_0_.at_ref, bf16[4,512,128]{2,1,0:T(8,128)(2,1)S(1)} %all-to-all-done.1.refs_1_, bf16[4,512,128]{2,1,0:T(8,128)(2,1)S(1)} %collective-permute-done.refs_2_, s32[512,1]{1,0:T(8,128)S(1)} %copy.7.refs_3_.refs_1_, ...), custom_call_target="tpu_custom_call" | custom-call | flops 2147483648 | bytes 8388608 | tf_op jit(solution)/shard_map/scores/pallas_call | solution.py:269
  99.8 0.7 broadcast_in_dim.16
  100.5 6.6 %all-to-all-start.2 = ((f32[8,8,512]{2,1,0:T(8,128)}), f32[8,8,512]{2,1,0:T(8,128)S(1)}, u32[]{:S(2)}, u32[]{:S(2)}) async-start(f32[8,8,512]{2,1,0:T(8,128)} %broadcast_in_dim.16), calls=%async_computation.2 | async-start | bytes 262144 | tf_op jit(solution)/shard_map/all_to_all | solution.py:33
  107.1 0.7 copy-done.2
  107.8 8.7 %gradient.1 = (f32[512,1024]{1,0:T(8,128)S(1)}, bf16[512,1024]{1,0:T(8,128)(2,1)S(1)}) custom-call(s32[4]{0:T(128)S(1)} %copy-done.2, s32[512,1]{1,0:T(8,128)S(1)} %copy.7.refs_3_.refs_1_, bf16[512,2048]{1,0:T(8,128)(2,1)} %get-tuple-element.10.refs_2_, bf16[128,1024]{1,0:T(8,128)(2,1)} %copy-done.5, ...), custom_call_target="tpu_custom_call" | custom-call | flops 4294967296 | bytes 10485760 | tf_op jit(solution)/shard_map/gradient/pallas_call | solution.py:297
  116.5 0.2 all-to-all-done.2.every_ref
  116.7 0.7 copy-done
  117.4 0.7 copy-done.3
  118.0 1.4 combine.1
  119.5 0.4 collective-permute-start.20
  119.9 2.3 %collective-permute-done.20 = f32[4,512,128]{2,1,0:T(8,128)S(1)} collective-permute-done((f32[4,512,128]{2,1,0:T(8,128)S(1)}, f32[4,512,128]{2,1,0:T(8,128)S(1)}, u32[]{:S(2)}, u32[]{:S(2)}) %collective-permute-start.20) | collective-permute-done | bytes 1048608 | tf_op jit(solution)/shard_map/ppermute | solution.py:25
  122.2 0.9 fusion.8
  123.2 7.0 %all-to-all-start.3 = ((bf16[4,512,128]{2,1,0:T(8,128)(2,1)}), bf16[4,512,128]{2,1,0:T(8,128)(2,1)S(1)}, u32[]{:S(2)}, u32[]{:S(2)}) async-start(bf16[4,512,128]{2,1,0:T(8,128)(2,1)} %get-tuple-element.16), calls=%async_computation.3 | async-start | bytes 1048576 | tf_op jit(solution)/shard_map/all_to_all | solution.py:33
  130.2 0.6 fusion.9
  130.8 14.9 %all-to-all-done.3 = bf16[4,512,128]{2,1,0:T(8,128)(2,1)S(1)} async-done(((bf16[4,512,128]{2,1,0:T(8,128)(2,1)}), bf16[4,512,128]{2,1,0:T(8,128)(2,1)S(1)}, u32[]{:S(2)}, u32[]{:S(2)}) %all-to-all-start.3) | async-done | bytes 524320 | tf_op jit(solution)/shard_map/all_to_all | solution.py:33
  145.7 0.2 select_reduce_fusion
  145.9 3.6 %fusion = bf16[5120,128]{0,1:T(8,128)(2,1)S(1)} fusion(bf16[512,5120]{1,0:T(8,128)(2,1)} %images_ref.1, f32[512,128]{1,0:T(8,128)S(1)} %select_reduce_fusion, bf16[4,512,128]{2,1,0:T(8,128)(2,1)} %embed.1, f32[512]{0:T(512)S(1)} %bitcast.24, f32[512]{0:T(512)S(1)} %bitcast.23), kind=kOutput, calls=%fused_computation.1 | convolution fusion | flops 672137216 | bytes 6950912 | tf_op jit(solution)/shard_map/dot_general | solution.py:338
  149.5 0.8 copy.9
  150.3 22.0 %all_to_all.25 = bf16[16,320,128]{2,1,0:T(8,128)(2,1)S(1)} all-to-all(bf16[16,320,128]{2,1,0:T(8,128)(2,1)S(1)} %bitcast.22), channel_id=1, replica_groups=mesh['y'=4,'x'=4,'zh'=4,'core'=2,'tw'=2] {'y','x'}, dimensions={0} | all-to-all | bytes 2621440 | tf_op jit(solution)/shard_map/all_to_all | solution.py:33
  172.3 0.2 convert_reduce_fusion
  172.4 3.3 %collective-permute-start.21 = (f32[320,128]{1,0:T(8,128)S(1)}, f32[320,128]{1,0:T(8,128)S(1)}, u32[]{:S(2)}, u32[]{:S(2)}) collective-permute-start(f32[320,128]{1,0:T(8,128)S(1)} %convert_reduce_fusion), channel_id=1, source_target_pairs={{0,1},{1,0},{2,3},{3,2},{4,5},{5,4},{6,7},{7,6},{8,9},{9,8},{10,11... | collective-permute-start | bytes 491528 | tf_op jit(solution)/shard_map/ppermute | solution.py:25
  175.7 3.3 %collective-permute-done.21 = f32[320,128]{1,0:T(8,128)S(1)} collective-permute-done((f32[320,128]{1,0:T(8,128)S(1)}, f32[320,128]{1,0:T(8,128)S(1)}, u32[]{:S(2)}, u32[]{:S(2)}) %collective-permute-start.21) | collective-permute-done | bytes 163872 | tf_op jit(solution)/shard_map/ppermute | solution.py:25
  179.0 0.7 add.11
  (44 shorter events, 0.2 us)
Async XLA Ops:
  0.6 9.8 %copy-start.4 = (bf16[64,1024]{1,0:T(8,128)(2,1)S(1)}, bf16[64,1024]{1,0:T(8,128)(2,1)}, u32[]{:S(2)}) copy-start(bf16[64,1024]{1,0:T(8,128)(2,1)} %param.7) | copy-start | bytes 393220
  2.9 27.4 %all-to-all-start = ((bf16[16,320,128]{2,1,0:T(8,128)(2,1)}), bf16[16,320,128]{2,1,0:T(8,128)(2,1)S(1)}, u32[]{:S(2)}, u32[]{:S(2)}) async-start(bf16[16,320,128]{2,1,0:T(8,128)(2,1)} %broadcast_in_dim.15), calls=%async_computation | async-start | bytes 2621440 | tf_op jit(solution)/shard_map/all_to_all | solution.py:33
  10.4 37.8 %collective-permute-start.10 = (bf16[64,1024]{1,0:T(8,128)(2,1)S(1)}, bf16[64,1024]{1,0:T(8,128)(2,1)S(1)}, u32[]{:S(2)}, u32[]{:S(2)}) collective-permute-start(bf16[64,1024]{1,0:T(8,128)(2,1)S(1)} %copy-done.4), channel_id=1, source_target_pairs={{0,1},{1,0},{2,3},{3,2},{4,5},{5,4},{6,7},{7,6},{8,9},{9,8},{10,11... | collective-permute-start | bytes 393224 | tf_op jit(solution)/shard_map/ppermute | solution.py:25
  12.4 33.6 %collective-permute-start.5 = (bf16[64,1024]{1,0:T(8,128)(2,1)S(1)}, bf16[64,1024]{1,0:T(8,128)(2,1)S(1)}, u32[]{:S(2)}, u32[]{:S(2)}) collective-permute-start(bf16[64,1024]{1,0:T(8,128)(2,1)S(1)} %copy-done.4), channel_id=1, source_target_pairs={{0,48},{16,0},{32,16},{48,32},{1,49},{17,1},{33,17},{49,33},{2,50}... | collective-permute-start | bytes 393224 | tf_op jit(solution)/shard_map/ppermute | solution.py:25
  12.5 33.6 %collective-permute-start.6 = (bf16[64,1024]{1,0:T(8,128)(2,1)S(1)}, bf16[64,1024]{1,0:T(8,128)(2,1)S(1)}, u32[]{:S(2)}, u32[]{:S(2)}) collective-permute-start(bf16[64,1024]{1,0:T(8,128)(2,1)S(1)} %copy-done.4), channel_id=1, source_target_pairs={{0,32},{16,48},{32,0},{48,16},{1,33},{17,49},{33,1},{49,17},{2,34}... | collective-permute-start | bytes 393224 | tf_op jit(solution)/shard_map/ppermute | solution.py:25
  15.3 35.0 %collective-permute-start.1 = (bf16[64,1024]{1,0:T(8,128)(2,1)S(1)}, bf16[64,1024]{1,0:T(8,128)(2,1)S(1)}, u32[]{:S(2)}, u32[]{:S(2)}) collective-permute-start(bf16[64,1024]{1,0:T(8,128)(2,1)S(1)} %copy-done.4), channel_id=1, source_target_pairs={{0,16},{16,32},{32,48},{48,0},{1,17},{17,33},{33,49},{49,1},{2,18}... | collective-permute-start | bytes 393224 | tf_op jit(solution)/shard_map/ppermute | solution.py:25
  37.4 46.0 %copy-start.9 = (s32[512]{0:T(512)S(1)}, s32[512]{0:T(512)}, u32[]{:S(2)}) copy-start(s32[512]{0:T(512)} %param.8) | copy-start | bytes 6148
  37.4 46.2 %copy-start.10 = (s32[512]{0:T(512)S(1)}, s32[512]{0:T(512)}, u32[]{:S(2)}) copy-start(s32[512]{0:T(512)} %param.9) | copy-start | bytes 6148
  37.4 34.3 %all-to-all-start.1 = ((bf16[4,512,128]{2,1,0:T(8,128)(2,1)}), bf16[4,512,128]{2,1,0:T(8,128)(2,1)S(1)}, u32[]{:S(2)}, u32[]{:S(2)}) async-start(bf16[4,512,128]{2,1,0:T(8,128)(2,1)} %embed.1), calls=%async_computation.1 | async-start | bytes 1048576 | tf_op jit(solution)/shard_map/all_to_all | solution.py:33
  46.1 43.4 %copy-start.8 = (bf16[128,1024]{1,0:T(8,128)(2,1)}, bf16[128,1024]{1,0:T(8,128)(2,1)S(1)}, u32[]{:S(2)}) copy-start(bf16[128,1024]{1,0:T(8,128)(2,1)S(1)} %constant_dynamic-update-slice_fusion.2.refs_8_.refs_7_) | copy-start | bytes 786436
  46.1 20.2 %collective-permute-start.8 = (bf16[128,1024]{1,0:T(8,128)(2,1)S(1)}, bf16[128,1024]{1,0:T(8,128)(2,1)S(1)}, u32[]{:S(2)}, u32[]{:S(2)}) collective-permute-start(bf16[128,1024]{1,0:T(8,128)(2,1)S(1)} %constant_dynamic-update-slice_fusion.2.refs_8_.refs_7_), channel_id=1, source_target_pairs={{0,192},{64,0},{128,64},{192,128},{1,193},{65,1},{129,65},{193,129... | collective-permute-start | bytes 786440 | tf_op jit(solution)/shard_map/ppermute | solution.py:25
  47.0 24.7 %collective-permute-start.7 = (bf16[128,1024]{1,0:T(8,128)(2,1)S(1)}, bf16[128,1024]{1,0:T(8,128)(2,1)S(1)}, u32[]{:S(2)}, u32[]{:S(2)}) collective-permute-start(bf16[128,1024]{1,0:T(8,128)(2,1)S(1)} %constant_dynamic-update-slice_fusion.2.refs_8_.refs_7_), channel_id=1, source_target_pairs={{0,64},{64,128},{128,192},{192,0},{1,65},{65,129},{129,193},{193,1... | collective-permute-start | bytes 786440 | tf_op jit(solution)/shard_map/ppermute | solution.py:25
  48.2 7.9 %collective-permute-start.15 = (bf16[64,1024]{1,0:T(8,128)(2,1)S(1)}, bf16[64,1024]{1,0:T(8,128)(2,1)S(1)}, u32[]{:S(2)}, u32[]{:S(2)}) collective-permute-start(bf16[64,1024]{1,0:T(8,128)(2,1)S(1)} %collective-permute-done.10), channel_id=1, source_target_pairs={{0,192},{64,0},{128,64},{192,128},{1,193},{65,1},{129,65},{193,129... | collective-permute-start | bytes 393224 | tf_op jit(solution)/shard_map/ppermute | solution.py:25
  50.3 39.1 %copy-start.5 = (bf16[128,1024]{1,0:T(8,128)(2,1)}, bf16[128,1024]{1,0:T(8,128)(2,1)S(1)}, u32[]{:S(2)}) copy-start(bf16[128,1024]{1,0:T(8,128)(2,1)S(1)} %constant_dynamic-update-slice_fusion.refs_4_.refs_3_) | copy-start | bytes 786436
  50.3 19.4 %collective-permute-start.2 = (bf16[128,1024]{1,0:T(8,128)(2,1)S(1)}, bf16[128,1024]{1,0:T(8,128)(2,1)}, u32[]{:S(2)}, u32[]{:S(2)}) collective-permute-start(bf16[128,1024]{1,0:T(8,128)(2,1)S(1)} %constant_dynamic-update-slice_fusion.refs_4_.refs_3_), channel_id=1, source_target_pairs={{0,64},{64,128},{128,192},{192,0},{1,65},{65,129},{129,193},{193,1... | collective-permute-start | bytes 786440 | tf_op jit(solution)/shard_map/ppermute | solution.py:25
  50.4 13.8 %collective-permute-start.16 = (bf16[64,1024]{1,0:T(8,128)(2,1)S(1)}, bf16[64,1024]{1,0:T(8,128)(2,1)S(1)}, u32[]{:S(2)}, u32[]{:S(2)}) collective-permute-start(bf16[64,1024]{1,0:T(8,128)(2,1)S(1)} %collective-permute-done.10), channel_id=1, source_target_pairs={{0,128},{64,192},{128,0},{192,64},{1,129},{65,193},{129,1},{193,65... | collective-permute-start | bytes 393224 | tf_op jit(solution)/shard_map/ppermute | solution.py:25
  56.1 9.2 %collective-permute-start.11 = (bf16[64,1024]{1,0:T(8,128)(2,1)S(1)}, bf16[64,1024]{1,0:T(8,128)(2,1)S(1)}, u32[]{:S(2)}, u32[]{:S(2)}) collective-permute-start(bf16[64,1024]{1,0:T(8,128)(2,1)S(1)} %collective-permute-done.10), channel_id=1, source_target_pairs={{0,64},{64,128},{128,192},{192,0},{1,65},{65,129},{129,193},{193,1... | collective-permute-start | bytes 393224 | tf_op jit(solution)/shard_map/ppermute | solution.py:25
  64.1 7.6 %collective-permute-start.3 = (bf16[128,1024]{1,0:T(8,128)(2,1)S(1)}, bf16[128,1024]{1,0:T(8,128)(2,1)}, u32[]{:S(2)}, u32[]{:S(2)}) collective-permute-start(bf16[128,1024]{1,0:T(8,128)(2,1)S(1)} %constant_dynamic-update-slice_fusion.refs_4_.refs_3_), channel_id=1, source_target_pairs={{0,192},{64,0},{128,64},{192,128},{1,193},{65,1},{129,65},{193,129... | collective-permute-start | bytes 786440 | tf_op jit(solution)/shard_map/ppermute | solution.py:25
  64.2 25.3 %copy-start.7 = (bf16[128,1024]{1,0:T(8,128)(2,1)}, bf16[128,1024]{1,0:T(8,128)(2,1)S(1)}, u32[]{:S(2)}) copy-start(bf16[128,1024]{1,0:T(8,128)(2,1)S(1)} %constant_dynamic-update-slice_fusion.6.refs_16_.refs_15_) | copy-start | bytes 786436
  65.4 11.5 %collective-permute-start.18 = (bf16[128,1024]{1,0:T(8,128)(2,1)S(1)}, bf16[128,1024]{1,0:T(8,128)(2,1)}, u32[]{:S(2)}, u32[]{:S(2)}) collective-permute-start(bf16[128,1024]{1,0:T(8,128)(2,1)S(1)} %constant_dynamic-update-slice_fusion.6.refs_16_.refs_15_), channel_id=1, source_target_pairs={{0,48},{16,0},{32,16},{48,32},{1,49},{17,1},{33,17},{49,33},{2,50}... | collective-permute-start | bytes 786440 | tf_op jit(solution)/shard_map/ppermute | solution.py:25
  66.3 23.2 %copy-start.6 = (bf16[128,1024]{1,0:T(8,128)(2,1)}, bf16[128,1024]{1,0:T(8,128)(2,1)S(1)}, u32[]{:S(2)}) copy-start(bf16[128,1024]{1,0:T(8,128)(2,1)S(1)} %constant_dynamic-update-slice_fusion.4.refs_12_.refs_11_) | copy-start | bytes 786436
  66.3 23.2 %copy-start.11 = (bf16[128,1024]{1,0:T(8,128)(2,1)}, bf16[128,1024]{1,0:T(8,128)(2,1)S(1)}, u32[]{:S(2)}) copy-start(bf16[128,1024]{1,0:T(8,128)(2,1)S(1)} %collective-permute-done.8.refs_10_.refs_9_) | copy-start | bytes 786436
  66.3 10.5 %collective-permute-start.12 = (bf16[128,1024]{1,0:T(8,128)(2,1)S(1)}, bf16[128,1024]{1,0:T(8,128)(2,1)}, u32[]{:S(2)}, u32[]{:S(2)}) collective-permute-start(bf16[128,1024]{1,0:T(8,128)(2,1)S(1)} %constant_dynamic-update-slice_fusion.4.refs_12_.refs_11_), channel_id=1, source_target_pairs={{0,16},{16,32},{32,48},{48,0},{1,17},{17,33},{33,49},{49,1},{2,18}... | collective-permute-start | bytes 786440 | tf_op jit(solution)/shard_map/ppermute | solution.py:25
  69.7 10.0 %collective-permute-start.17 = (bf16[128,1024]{1,0:T(8,128)(2,1)S(1)}, bf16[128,1024]{1,0:T(8,128)(2,1)S(1)}, u32[]{:S(2)}, u32[]{:S(2)}) collective-permute-start(bf16[128,1024]{1,0:T(8,128)(2,1)S(1)} %constant_dynamic-update-slice_fusion.6.refs_16_.refs_15_), channel_id=1, source_target_pairs={{0,16},{16,32},{32,48},{48,0},{1,17},{17,33},{33,49},{49,1},{2,18}... | collective-permute-start | bytes 786440 | tf_op jit(solution)/shard_map/ppermute | solution.py:25
  71.7 17.8 %copy-start.12 = (bf16[128,1024]{1,0:T(8,128)(2,1)}, bf16[128,1024]{1,0:T(8,128)(2,1)S(1)}, u32[]{:S(2)}) copy-start(bf16[128,1024]{1,0:T(8,128)(2,1)S(1)} %collective-permute-done.7.refs_9_.refs_8_) | copy-start | bytes 786436
  71.7 11.0 %collective-permute-start.13 = (bf16[128,1024]{1,0:T(8,128)(2,1)S(1)}, bf16[128,1024]{1,0:T(8,128)(2,1)S(1)}, u32[]{:S(2)}, u32[]{:S(2)}) collective-permute-start(bf16[128,1024]{1,0:T(8,128)(2,1)S(1)} %constant_dynamic-update-slice_fusion.4.refs_12_.refs_11_), channel_id=1, source_target_pairs={{0,48},{16,0},{32,16},{48,32},{1,49},{17,1},{33,17},{49,33},{2,50}... | collective-permute-start | bytes 786440 | tf_op jit(solution)/shard_map/ppermute | solution.py:25
  71.7 17.7 %collective-permute-start = (bf16[4,512,128]{2,1,0:T(8,128)(2,1)S(1)}, bf16[4,512,128]{2,1,0:T(8,128)(2,1)S(1)}, u32[]{:S(2)}, u32[]{:S(2)}) collective-permute-start(bf16[4,512,128]{2,1,0:T(8,128)(2,1)S(1)} %all-to-all-done.1.refs_1_), channel_id=1, source_target_pairs={{0,2},{2,0},{1,3},{3,1},{4,6},{6,4},{5,7},{7,5},{8,10},{10,8},{9,1... | collective-permute-start | bytes 1572872 | tf_op jit(solution)/shard_map/ppermute | solution.py:25
  76.8 7.4 %collective-permute-start.9 = (bf16[128,1024]{1,0:T(8,128)(2,1)S(1)}, bf16[128,1024]{1,0:T(8,128)(2,1)}, u32[]{:S(2)}, u32[]{:S(2)}) collective-permute-start(bf16[128,1024]{1,0:T(8,128)(2,1)S(1)} %collective-permute-done.8.refs_10_.refs_9_), channel_id=1, source_target_pairs={{0,192},{64,0},{128,64},{192,128},{1,193},{65,1},{129,65},{193,129... | collective-permute-start | bytes 786440 | tf_op jit(solution)/shard_map/ppermute | solution.py:25
  76.8 7.9 %collective-permute-start.4 = (bf16[128,1024]{1,0:T(8,128)(2,1)}, bf16[128,1024]{1,0:T(8,128)(2,1)}, u32[]{:S(2)}, u32[]{:S(2)}) collective-permute-start(bf16[128,1024]{1,0:T(8,128)(2,1)} %collective-permute-done.2.refs_5_.refs_4_), channel_id=1, source_target_pairs={{0,64},{64,128},{128,192},{192,0},{1,65},{65,129},{129,193},{193,1... | collective-permute-start | bytes 786440 | tf_op jit(solution)/shard_map/ppermute | solution.py:25
  79.6 3.2 %copy-start.13 = (bf16[128,1024]{1,0:T(8,128)(2,1)}, bf16[128,1024]{1,0:T(8,128)(2,1)S(1)}, u32[]{:S(2)}) copy-start(bf16[128,1024]{1,0:T(8,128)(2,1)S(1)} %collective-permute-done.17.refs_17_.refs_16_) | copy-start | bytes 786436
  79.6 7.3 %collective-permute-start.19 = (bf16[128,1024]{1,0:T(8,128)(2,1)}, bf16[128,1024]{1,0:T(8,128)(2,1)}, u32[]{:S(2)}, u32[]{:S(2)}) collective-permute-start(bf16[128,1024]{1,0:T(8,128)(2,1)} %collective-permute-done.18.refs_18_.refs_17_), channel_id=1, source_target_pairs={{0,48},{16,0},{32,16},{48,32},{1,49},{17,1},{33,17},{49,33},{2,50}... | collective-permute-start | bytes 786440 | tf_op jit(solution)/shard_map/ppermute | solution.py:25
  82.7 0.7 copy-start.14
  82.7 6.7 %collective-permute-start.14 = (bf16[128,1024]{1,0:T(8,128)(2,1)}, bf16[128,1024]{1,0:T(8,128)(2,1)}, u32[]{:S(2)}, u32[]{:S(2)}) collective-permute-start(bf16[128,1024]{1,0:T(8,128)(2,1)} %collective-permute-done.12.refs_13_.refs_12_), channel_id=1, source_target_pairs={{0,16},{16,32},{32,48},{48,0},{1,17},{17,33},{33,49},{49,1},{2,18}... | collective-permute-start | bytes 786440 | tf_op jit(solution)/shard_map/ppermute | solution.py:25
  83.4 16.4 %copy-start.1 = (s32[4]{0:T(128)}, s32[4]{0:T(128)S(1)}, u32[]{:S(2)}) copy-start(s32[4]{0:T(128)S(1)} %pad_add_fusion.refs_0_.at_ref) | copy-start | bytes 52
  100.5 16.2 %all-to-all-start.2 = ((f32[8,8,512]{2,1,0:T(8,128)}), f32[8,8,512]{2,1,0:T(8,128)S(1)}, u32[]{:S(2)}, u32[]{:S(2)}) async-start(f32[8,8,512]{2,1,0:T(8,128)} %broadcast_in_dim.16), calls=%async_computation.2 | async-start | bytes 262144 | tf_op jit(solution)/shard_map/all_to_all | solution.py:33
  107.1 0.7 copy-start.2
  116.7 0.7 copy-start
  117.4 0.7 copy-start.3
  119.5 2.7 %collective-permute-start.20 = (f32[4,512,128]{2,1,0:T(8,128)S(1)}, f32[4,512,128]{2,1,0:T(8,128)S(1)}, u32[]{:S(2)}, u32[]{:S(2)}) collective-permute-start(f32[4,512,128]{2,1,0:T(8,128)S(1)} %get-tuple-element.15), channel_id=1, source_target_pairs={{0,2},{2,0},{1,3},{3,1},{4,6},{6,4},{5,7},{7,5},{8,10},{10,8},{9,1... | collective-permute-start | bytes 3145736 | tf_op jit(solution)/shard_map/ppermute | solution.py:25
  123.2 22.5 %all-to-all-start.3 = ((bf16[4,512,128]{2,1,0:T(8,128)(2,1)}), bf16[4,512,128]{2,1,0:T(8,128)(2,1)S(1)}, u32[]{:S(2)}, u32[]{:S(2)}) async-start(bf16[4,512,128]{2,1,0:T(8,128)(2,1)} %get-tuple-element.16), calls=%async_computation.3 | async-start | bytes 1048576 | tf_op jit(solution)/shard_map/all_to_all | solution.py:33
  172.4 6.6 %collective-permute-start.21 = (f32[320,128]{1,0:T(8,128)S(1)}, f32[320,128]{1,0:T(8,128)S(1)}, u32[]{:S(2)}, u32[]{:S(2)}) collective-permute-start(f32[320,128]{1,0:T(8,128)S(1)} %convert_reduce_fusion), channel_id=1, source_target_pairs={{0,1},{1,0},{2,3},{3,2},{4,5},{5,4},{6,7},{7,6},{8,9},{9,8},{10,11... | collective-permute-start | bytes 491528 | tf_op jit(solution)/shard_map/ppermute | solution.py:25

commit v2 on v1

v2 whole, which is shorter than its diff:
```python
import jax
import jax.numpy as jnp
from jax import lax
from jax.experimental import pallas as pl
from jax.experimental.pallas import tpu as pltpu
from jax.sharding import Mesh
from jax.sharding import PartitionSpec as P

AXES = ("y", "x", "zh", "core", "tw")
PLANE = ("y", "x")
FSDP_TOWER = ("y", "x", "tw")
REL = (0, 3, 1, 2)
NEAR = (0, 3, 1)
FAR = (2,)

epsilon = 1e-06
score_scale = 100.0
f32 = jnp.float32
bf16 = jnp.bfloat16
VMEM = pl.BlockSpec(memory_space=pltpu.VMEM)
HBM = pl.BlockSpec(memory_space=pltpu.HBM)
SMEM = pl.BlockSpec(memory_space=pltpu.SMEM)


def shifted(x, axis, step):
    n = lax.axis_size(axis)
    return lax.ppermute(x, axis, [(i, (i + step) % n) for i in range(n)])


def in_hbm(x):
    return pltpu.with_memory_space_constraint(x, pltpu.HBM)


def exchanged(x, axis):
    return lax.all_to_all(x, axis, 0, 0, tiled=True)


def from_all(x, axis):
    return exchanged(jnp.broadcast_to(x, (lax.axis_size(axis), *x.shape)), axis)


def gathered_texts(texts, other_texts):
    near, far = [], []
    for part, inner, outer in ((texts, "x", "y"), (other_texts, "y", "x")):
        below, above, across = (shifted(part, inner, step) for step in (1, -1, 2))
        halves = [jnp.concatenate([part, below]), jnp.concatenate([above, across])]
        for half, toward in zip(halves, (1, -1)):
            first = shifted(half, outer, toward)
            second = shifted(half, outer, -toward)
            near += [half, first, second] if toward == 1 else [half, second, first]
            far.append(shifted(first, outer, toward))
    return [in_hbm(piece) for piece in near], [in_hbm(piece) for piece in far]


def fetch(pieces, whole, sem):
    at, copies = 0, []
    for k, piece in enumerate(pieces):
        n = piece.shape[0]
        copies.append(pltpu.make_async_copy(piece, whole.at[pl.ds(at, n)], sem.at[k]))
        at += n
    for copy in copies:
        copy.start()
    return copies


def column_places(at_ref, group, steps):
    y, x, tp, tower = (at_ref[k] for k in range(4))
    lane = lax.broadcasted_iota(jnp.int32, (1, 128), 1)
    places = []
    for side in range(2):
        tw = tower if side == 0 else 1 - tower
        for half in range(2):
            for step in steps:
                firsts = []
                for inner in REL[2 * half : 2 * half + 2]:
                    ahead = (step, inner) if side == 0 else (inner, step)
                    plane = lax.rem(y + ahead[0], 4) * 4 + lax.rem(x + ahead[1], 4)
                    firsts.append(((plane * 8 + tp) * 2 + tw) * group)
                places.append(jnp.where(lane < group, firsts[0], firsts[1] - group) + lane)
    return places


def as_columns(lines):
    n = lines[0].shape[1]
    spare = jnp.zeros((128 - len(lines), n), f32)
    return jnp.concatenate([*lines, spare], axis=0).T


def column_copies(whole, held, sem, step):
    copies = []
    for k in range(whole.shape[1] // step):
        here = pl.ds(k * step, step)
        copies.append(pltpu.make_async_copy(whole.at[:, here], held.at[:, here], sem.at[k]))
        copies[-1].start()
    return copies


def gate_kernel(in_ref, out_ref):
    out_ref[...] = in_ref[...]


def sign_kernel(forget_ref, out_ref):
    out_ref[...] = 1.0 - 2.0 * forget_ref[...].astype(f32)


def place_kernel(perm_ref, out_ref):
    out_ref[...] = as_columns([perm_ref[...].astype(f32)])[:, 0:1].astype(jnp.int32)


def embed_kernel(images_ref, weight_ref, out_ref, held, sem):
    step = 128
    copies = []
    for k in range(images_ref.shape[0] // step):
        here = pl.ds(k * step, step)
        copies.append(pltpu.make_async_copy(images_ref.at[here], held.at[here], sem.at[k]))
        copies[-1].start()
    for k, copy in enumerate(copies):
        copy.wait()
        here = pl.ds(k * step, step)
        rounded = jnp.dot(
            held[here, :], weight_ref[...], preferred_element_type=f32
        ).astype(bf16)
        for z in range(out_ref.shape[0]):
            out_ref[z, here, :] = rounded


def merged(one, two):
    top = jnp.maximum(one[0:1], two[0:1])
    first, second = jnp.exp(one[0:1] - top), jnp.exp(two[0:1] - top)
    total = one[1:2] * first + two[1:2] * second
    moment = one[2:3] * first + two[2:3] * second
    return jnp.concatenate([top, total, moment, one[3:4] + two[3:4], one[4:8]], axis=0)


def score_columns(unit, pieces, whole, score, high, soft, sem, out_sem, at_ref, perm_ref, out_ref, group, steps, rnorm):
    copies = fetch(pieces, whole, sem)
    rows = unit.shape[0]
    step = 512
    per = step // pieces[0].shape[0]
    for c in range(whole.shape[0] // step):
        for copy in copies[c * per : (c + 1) * per]:
            copy.wait()
        at = c * step
        chunk = score_scale * lax.dot_general(
            unit[...], whole[pl.ds(at, step)], (((1,), (1,)), ((), ())), preferred_element_type=f32
        )
        score[:, pl.ds(at, step)] = chunk
        peak = chunk[:, :128]
        for k in range(128, step, 128):
            peak = jnp.maximum(peak, chunk[:, k : k + 128])
        high[...] = peak if c == 0 else jnp.maximum(high[...], peak)

    places = column_places(at_ref, group, steps)
    band = 128

    @pl.loop(0, rows // band)
    def _(r):
        here = pl.ds(pl.multiple_of(r * band, band), band)
        perm = perm_ref[here, :]
        top = jnp.max(high[here, :], axis=1, keepdims=True)
        total = jnp.zeros((band, 128), f32)
        moment = jnp.zeros((band, 128), f32)
        found = jnp.zeros((band, 128), f32)
        for k in range(len(places)):
            cols = pl.ds(k * 128, 128)
            logit = score[here, cols]
            p = jnp.exp(logit - top)
            hit = perm == places[k]
            total += p
            moment += p * logit
            found += jnp.where(hit, logit, 0.0)
            soft[here, cols] = jnp.where(hit, 0.0, p).astype(bf16)
        pltpu.make_async_copy(soft.at[here], out_ref.at[here], out_sem).start()
        sums = [jnp.sum(v, axis=1, keepdims=True) for v in (total, moment, found)]
        which = lax.broadcasted_iota(jnp.int32, (band, 128), 1)
        tile = jnp.where(which == 0, top, 0.0)
        for k, v in enumerate(sums):
            tile = jnp.where(which == k + 1, v, tile)
        high[here, :] = tile

    filled = high[...]
    if rnorm is not None:
        which = lax.broadcasted_iota(jnp.int32, (rows, 128), 1)
        filled = jnp.where(which == 4, rnorm, filled)
    lines = filled.T[:8]
    pltpu.make_async_copy(soft, out_ref, out_sem).wait()
    return lines


def near_score_kernel(n, group, *refs):
    at_ref, mine_ref, theirs_ref, perm_ref = refs[:4]
    pieces = refs[4 : 4 + n]
    out_ref, stats_ref, unit = refs[4 + n : 7 + n]
    whole, score, high, soft, sem, out_sem = refs[7 + n :]
    rows, feats = mine_ref.shape[1], mine_ref.shape[2]
    core = lax.rem(at_ref[2], 2)
    square = jnp.zeros((rows, feats), f32)
    for k in range(4):
        for ref in (mine_ref, theirs_ref):
            part = ref[k].astype(f32)
            square += part * part
    rnorm = lax.rsqrt(jnp.sum(square, axis=1, keepdims=True) + epsilon)
    for k in range(4):
        for ref, which in ((mine_ref, core), (theirs_ref, 1 - core)):
            to = pl.multiple_of((2 * k + which) * feats, feats)
            unit[:, pl.ds(to, feats)] = (ref[k].astype(f32) * rnorm).astype(bf16)
    stats_ref[...] = score_columns(
        unit, pieces, whole, score, high, soft, sem, out_sem, at_ref, perm_ref, out_ref, group, NEAR, rnorm
    )


def far_score_kernel(n, group, *refs):
    at_ref, unit, perm_ref, near_ref = refs[:4]
    pieces = refs[4 : 4 + n]
    out_ref, stats_ref, every_ref = refs[4 + n : 7 + n]
    whole, score, high, soft, sem, out_sem = refs[7 + n :]
    lines = score_columns(
        unit, pieces, whole, score, high, soft, sem, out_sem, at_ref, perm_ref, out_ref, group, FAR, None
    )
    stats_ref[...] = lines
    both = merged(near_ref[...], lines)
    for k in range(every_ref.shape[0]):
        every_ref[k] = both


def gradient_columns(at_ref, perm_ref, p_ref, pieces, whole, both, sem, p_sem, group, steps):
    rows = p_ref.shape[0]
    p_copy = pltpu.make_async_copy(p_ref, both.at[pl.ds(0, rows)], p_sem)
    p_copy.start()
    step = 512
    for c in range(whole.shape[1] // step):
        cols, at = pl.ds(c * step, step), 0
        for piece in pieces:
            there = whole.at[pl.ds(at, piece.shape[0]), cols]
            pltpu.make_async_copy(piece.at[:, cols], there, sem.at[c]).start()
            at += piece.shape[0]
    places = column_places(at_ref, group, steps)
    band = 64

    @pl.loop(0, rows // band)
    def _(r):
        at = pl.multiple_of(r * band, band)
        perm = perm_ref[pl.ds(at, band), :]
        for k in range(len(places)):
            both[pl.ds(at + rows, band), pl.ds(k * 128, 128)] = jnp.where(
                perm == places[k], 1.0, 0.0
            ).astype(bf16)

    p_copy.wait()
    for c in range(whole.shape[1] // step):
        cols = pl.ds(c * step, step)
        pltpu.make_async_copy(whole.at[:, cols], whole.at[:, cols], sem.at[c]).wait()
        out = jnp.dot(both[...], whole[:, cols], preferred_element_type=f32)
        yield cols, out[:rows], out[rows:]


def near_gradient_kernel(n, group, *refs):
    at_ref, perm_ref, p_ref = refs[:3]
    pieces = refs[3 : 3 + n]
    soft_ref, hard_ref = refs[3 + n : 5 + n]
    for cols, soft, hard in gradient_columns(
        at_ref, perm_ref, p_ref, pieces, *refs[5 + n :], group, NEAR
    ):
        soft_ref[:, cols] = soft
        hard_ref[:, cols] = hard.astype(bf16)


def far_gradient_kernel(n, group, *refs):
    at_ref, perm_ref, p_ref, near_ref, far_ref, near_soft, near_hard = refs[:7]
    pieces = refs[7 : 7 + n]
    soft_ref, hard_ref = refs[7 + n : 9 + n]
    top = jnp.maximum(near_ref[0:1], far_ref[0:1])
    cols = as_columns([jnp.exp(near_ref[0:1] - top), jnp.exp(far_ref[0:1] - top)])
    first, second = cols[:, 0:1], cols[:, 1:2]
    for cols, soft, hard in gradient_columns(
        at_ref, perm_ref, p_ref, pieces, *refs[9 + n :], group, FAR
    ):
        soft_ref[:, cols] = first * near_soft[:, cols] + second * soft
        hard_ref[:, cols] = near_hard[:, cols] + hard.astype(bf16)


def combine_kernel(at_ref, near_ref, far_ref, every_ref, sign_ref, soft_ref, hard_ref, keep_ref, give_ref, lines_ref):
    core = lax.rem(at_ref[2], 2)
    feats = keep_ref.shape[2]
    rest = [every_ref[k] for k in range(every_ref.shape[0])]
    tops = [v[0:1] for v in rest]
    high = tops[0]
    for t in tops[1:]:
        high = jnp.maximum(high, t)
    scales = [jnp.exp(t - high) for t in tops]
    mass = sum(s * v[1:2] for s, v in zip(scales, rest))
    lse = high + jnp.log(mass)
    target = sum(v[3:4] for v in rest)
    mean = sum(jnp.exp(t - lse) * v[2:3] for t, v in zip(tops, rest))
    sign = sign_ref[...]
    lines_ref[0:1] = lse - target
    lines_ref[1:2] = sign * (mean - target)
    lines_ref[2:3] = near_ref[4:5]
    for_soft = score_scale * sign * jnp.exp(jnp.maximum(near_ref[0:1], far_ref[0:1]) - lse)
    weight = (sign * (jnp.exp(target - lse) - 1.0)).astype(bf16).astype(f32)
    cols = as_columns([for_soft, score_scale * weight])
    first, second = cols[:, 0:1], cols[:, 1:2]
    for k in range(4):
        for out, which in ((keep_ref, core), (give_ref, 1 - core)):
            at = pl.ds(pl.multiple_of((2 * k + which) * feats, feats), feats)
            out[k] = first * soft_ref[:, at] + second * hard_ref[:, at].astype(f32)


def weight_kernel(at_ref, images_ref, chip_ref, parts_ref, emb_ref, lines_ref, out_ref, held, sem):
    step = 1024
    copies = column_copies(images_ref, held, sem, step)
    zh = lax.div(at_ref[2], 2)
    grad_unit = jnp.zeros(chip_ref.shape[1:], f32)
    for k in range(4):
        grad_unit += jnp.where(zh == k, chip_ref[k], parts_ref[k].astype(f32))
    cols = as_columns([lines_ref[1:2], lines_ref[2:3]])
    radial, rnorm = cols[:, 0:1], cols[:, 1:2]
    unit = emb_ref[0].astype(f32) * rnorm
    grad_emb = (rnorm * (grad_unit - unit * radial)).astype(bf16)
    for k, copy in enumerate(copies):
        copy.wait()
        here = pl.ds(k * step, step)
        out_ref[here, :] = lax.dot_general(
            held[:, here], grad_emb, (((0,), (0,)), ((), ())), preferred_element_type=f32
        ).astype(bf16)


def local(images, img_weight, texts, pair_perm, forget):
    y, x, zh = (lax.axis_index(a) for a in ("y", "x", "zh"))
    core, tower = lax.axis_index("core"), lax.axis_index("tw")
    rows, width = images.shape
    feats = img_weight.shape[1]
    group = texts.shape[0]
    at = jnp.stack([y, x, zh * 2 + core, tower]).astype(jnp.int32)

    weight = from_all(img_weight, PLANE).reshape(width, feats)
    other_texts = shifted(texts, "tw", 1)
    other_texts = pl.pallas_call(
        gate_kernel,
        name="gate",
        out_shape=jax.ShapeDtypeStruct(texts.shape, bf16),
        in_specs=[VMEM],
        out_specs=VMEM,
        compiler_params=pltpu.CompilerParams(vmem_limit_bytes=2 << 20),
    )(other_texts)
    signs = pl.pallas_call(
        sign_kernel,
        name="signs",
        out_shape=jax.ShapeDtypeStruct((1, rows), f32),
        in_specs=[VMEM],
        out_specs=VMEM,
        compiler_params=pltpu.CompilerParams(vmem_limit_bytes=2 << 20),
    )(forget.reshape(1, rows))
    perm = pl.pallas_call(
        place_kernel,
        name="places",
        out_shape=jax.ShapeDtypeStruct((rows, 1), jnp.int32),
        in_specs=[VMEM],
        out_specs=VMEM,
        compiler_params=pltpu.CompilerParams(vmem_limit_bytes=2 << 20),
    )(pair_perm.reshape(1, rows))
    near, far = gathered_texts(texts, other_texts)
    n, m = len(near), len(far)
    near_rows, far_rows = (sum(q.shape[0] for q in group) for group in (near, far))
    embed = near[0].shape[1]

    emb_copies = pl.pallas_call(
        embed_kernel,
        name="embed",
        out_shape=jax.ShapeDtypeStruct((4, rows, feats), bf16),
        in_specs=[HBM, VMEM],
        out_specs=VMEM,
        scratch_shapes=[pltpu.VMEM((rows, width), bf16), pltpu.SemaphoreType.DMA((rows // 128,))],
        compiler_params=pltpu.CompilerParams(vmem_limit_bytes=16 << 20),
        cost_estimate=pl.CostEstimate(
            flops=2 * rows * width * feats, bytes_accessed=7 << 20, transcendentals=0
        ),
    )(in_hbm(images), weight)
    mine = exchanged(emb_copies, "zh")
    theirs = shifted(mine, "core", 1)

    def score_scratch(count, columns):
        return [
            pltpu.VMEM((columns, embed), bf16),
            pltpu.VMEM((rows, columns), f32),
            pltpu.VMEM((rows, 128), f32),
            pltpu.VMEM((rows, columns), bf16),
            pltpu.SemaphoreType.DMA((count,)),
            pltpu.SemaphoreType.DMA,
        ]

    def gradient_scratch(columns):
        return [
            pltpu.VMEM((columns, embed), bf16),
            pltpu.VMEM((2 * rows, columns), bf16),
            pltpu.SemaphoreType.DMA((embed // 512,)),
            pltpu.SemaphoreType.DMA,
        ]

    def cost(flops, columns):
        return pl.CostEstimate(
            flops=flops, bytes_accessed=4 * embed * columns, transcendentals=rows * columns
        )

    gradient_shape = (
        jax.ShapeDtypeStruct((rows, embed), f32),
        jax.ShapeDtypeStruct((rows, embed), bf16),
    )
    work = 2 * rows * embed
    near_p, near_stats, unit = pl.pallas_call(
        lambda *refs: near_score_kernel(n, group, *refs),
        name="near_scores",
        out_shape=(
            pltpu.HBM((rows, near_rows), bf16),
            jax.ShapeDtypeStruct((8, rows), f32),
            jax.ShapeDtypeStruct((rows, embed), bf16),
        ),
        in_specs=[SMEM, VMEM, VMEM, VMEM, *[HBM] * n],
        out_specs=(HBM, VMEM, VMEM),
        scratch_shapes=score_scratch(n, near_rows),
        compiler_params=pltpu.CompilerParams(vmem_limit_bytes=20 << 20),
        cost_estimate=cost(work * near_rows, near_rows),
    )(at, mine, theirs, perm, *near)
    near_p = in_hbm(near_p)
    near_soft, near_hard = pl.pallas_call(
        lambda *refs: near_gradient_kernel(n, group, *refs),
        name="near_gradient",
        out_shape=gradient_shape,
        in_specs=[SMEM, VMEM, HBM, *[HBM] * n],
        out_specs=(VMEM, VMEM),
        scratch_shapes=gradient_scratch(near_rows),
        compiler_params=pltpu.CompilerParams(vmem_limit_bytes=20 << 20),
        cost_estimate=cost(2 * work * near_rows, near_rows),
    )(at, perm, near_p, *near)
    far_p, far_stats, copies = pl.pallas_call(
        lambda *refs: far_score_kernel(m, group, *refs),
        name="far_scores",
        out_shape=(
            pltpu.HBM((rows, far_rows), bf16),
            jax.ShapeDtypeStruct((8, rows), f32),
            jax.ShapeDtypeStruct((8, 8, rows), f32),
        ),
        in_specs=[SMEM, VMEM, VMEM, VMEM, *[HBM] * m],
        out_specs=(HBM, VMEM, VMEM),
        scratch_shapes=score_scratch(m, far_rows),
        compiler_params=pltpu.CompilerParams(vmem_limit_bytes=20 << 20),
        cost_estimate=cost(work * far_rows, far_rows),
    )(at, unit, perm, near_stats, *far)
    every = exchanged(copies, ("zh", "core"))
    soft, hard = pl.pallas_call(
        lambda *refs: far_gradient_kernel(m, group, *refs),
        name="far_gradient",
        out_shape=gradient_shape,
        in_specs=[SMEM, VMEM, HBM, VMEM, VMEM, VMEM, VMEM, *[HBM] * m],
        out_specs=(VMEM, VMEM),
        scratch_shapes=gradient_scratch(far_rows),
        compiler_params=pltpu.CompilerParams(vmem_limit_bytes=20 << 20),
        cost_estimate=cost(2 * work * far_rows, far_rows),
    )(at, perm, in_hbm(far_p), near_stats, far_stats, near_soft, near_hard, *far)

    keep, give, lines = pl.pallas_call(
        combine_kernel,
        name="combine",
        out_shape=(
            jax.ShapeDtypeStruct((4, rows, feats), f32),
            jax.ShapeDtypeStruct((4, rows, feats), f32),
            jax.ShapeDtypeStruct((8, rows), f32),
        ),
        in_specs=[SMEM, VMEM, VMEM, VMEM, VMEM, VMEM, VMEM],
        out_specs=(VMEM, VMEM, VMEM),
        compiler_params=pltpu.CompilerParams(vmem_limit_bytes=20 << 20),
    )(at, near_stats, far_stats, every, signs, soft, hard)

    pair_loss = lines[0]
    chip = keep + shifted(give, "core", 1)
    parts = exchanged(chip.astype(bf16), "zh")
    share = pl.pallas_call(
        weight_kernel,
        name="weight",
        out_shape=jax.ShapeDtypeStruct((width, feats), bf16),
        in_specs=[SMEM, HBM, VMEM, VMEM, VMEM, VMEM],
        out_specs=VMEM,
        scratch_shapes=[pltpu.VMEM((rows, width), bf16), pltpu.SemaphoreType.DMA((width // 1024,))],
        compiler_params=pltpu.CompilerParams(vmem_limit_bytes=16 << 20),
    )(at, in_hbm(images), chip, parts, emb_copies, lines)
    summed = jnp.sum(exchanged(share.reshape(16, -1, feats), PLANE).astype(f32), axis=0)
    weight_grad = summed + shifted(summed, "tw", 1)
    return (pair_loss, weight_grad)


def solution(mesh):
    finer = Mesh(mesh.devices.reshape(4, 4, 4, 2, mesh.shape["tower"]), AXES)
    return jax.shard_map(
        local,
        mesh=finer,
        in_specs=(
            P(FSDP_TOWER, None),
            P(PLANE, ("zh", "core")),
            P(("y", "x", "zh", "core", "tw"), None),
            P(FSDP_TOWER),
            P(FSDP_TOWER),
        ),
        out_specs=(P(FSDP_TOWER), P(PLANE, ("zh", "core"))),
        check_vma=False,
    )
```

time: 181 us -> 185 us (1.022)
  blocking collectives: 22 us -> 71.6 us
  waiting for transfers between devices: 58.2 us -> 32.9 us
  starting transfers between devices: 57.5 us -> 37.6 us
  Pallas kernels: 27.6 us -> 33.1 us
  matrix products: 3.58 us -> 0 us
    all_to_all x1 -> x3, blocking collectives: 22 us -> 71.6 us  [exchanged(): return lax.all_to_all(x, axis, 0, 0, tiled=True)]
    all_to_all x4 -> x2, waiting for transfers between devices: 28.3 us -> 0.01 us  [exchanged(): return lax.all_to_all(x, axis, 0, 0, tiled=True)]
    all_to_all x4 -> x2, starting transfers between devices: 29.7 us -> 15.2 us  [exchanged(): return lax.all_to_all(x, axis, 0, 0, tiled=True)]
    pallas_call x3 -> x9, Pallas kernels: 26.1 us -> 31.7 us  [the longest x1 6.68 us: local(): pl.pallas_call(lambda *refs: near_score_kernel(n, group, *refs), name='ne...]
    ppermute x22, starting transfers between devices: 27.8 us -> 22.4 us  [shifted(): return lax.ppermute(x, axis, [(i, (i + step) % n) for i in range(n)])]
    dot_general x1 -> x0, matrix products: 3.58 us -> none  [local(): lax.dot_general(images, grad_emb, (((0,), (0,)), ((), ())), preferred_ele...]
    ppermute x22, waiting for transfers between devices: 29.9 us -> 32.9 us  [shifted(): return lax.ppermute(x, axis, [(i, (i + step) % n) for i in range(n)])]
    unnamed x34 -> x51, local copies, waits for them, and re-layouts: 2.71 us -> 4.88 us
  transfers between devices with their start and end apart: 26 -> 24, of which waited for: 13 -> 9; matrix products, arithmetic and copies ran while one was open for 1% -> 0% of each run, Pallas kernels for 9% -> 9%
where the time goes in v2:
time: 185 us; the launch traced here: 184 us
  blocking collectives  71.6 us (39%)
  starting transfers between devices  37.6 us (20%)
  Pallas kernels  33.1 us (18%)
  waiting for transfers between devices  32.9 us (18%)
  local copies, waits for them, and re-layouts  6.62 us (4%)
    all_to_all x3, blocking collectives, exchanged(): return lax.all_to_all(x, axis, 0, 0, tiled=True)  71.6 us
    ppermute x22, waiting for transfers between devices, shifted(): return lax.ppermute(x, axis, [(i, (i + step) % n) for i in range(n)])  32.9 us
    ppermute x22, starting transfers between devices, shifted(): return lax.ppermute(x, axis, [(i, (i + step) % n) for i in range(n)])  22.4 us
    all_to_all x2, starting transfers between devices, exchanged(): return lax.all_to_all(x, axis, 0, 0, tiled=True)  15.2 us
    pallas_call x1, Pallas kernels, local(): pl.pallas_call(lambda *refs: near_score_kernel(n, group, *refs), name='ne...  6.68 us
    pallas_call x1, Pallas kernels, local(): pl.pallas_call(lambda *refs: near_gradient_kernel(n, group, *refs), name=...  6.59 us
    pallas_call x1, Pallas kernels, local(): pl.pallas_call(weight_kernel, name='weight', out_shape=jax.ShapeDtypeStru...  5.86 us
    unnamed x51, local copies, waits for them, and re-layouts  4.88 us
  transfers between devices with their start and end apart: 24, of which 9 were waited for; matrix products, arithmetic and copies ran while one was open for 0% of the time, Pallas kernels for 9%

profile of v2, /device:TPU:2, one launch (start us, length us, event | category | flops | bytes accessed | tf_op | source)
XLA Modules:
  0.0 184.0 jit_solution(11383258146831083898)
XLA Ops:
  0.6 1.1 broadcast_in_dim.3
  1.8 25.9 %all_to_all.25 = bf16[16,320,128]{2,1,0:T(8,128)(2,1)S(1)} all-to-all(bf16[16,320,128]{2,1,0:T(8,128)(2,1)S(1)} %broadcast_in_dim.3), channel_id=1, replica_groups=mesh['y'=4,'x'=4,'zh'=4,'core'=2,'tw'=2] {'y','x'}, dimensions={0} | all-to-all | bytes 2621440 | tf_op jit(solution)/shard_map/all_to_all | solution.py:35
  27.6 4.2 %embed.1.emb_ref = bf16[4,512,128]{2,1,0:T(8,128)(2,1)} custom-call(bf16[512,5120]{1,0:T(8,128)(2,1)} %images_ref.3, bf16[5120,128]{1,0:T(8,128)(2,1)S(1)} %bitcast.10), custom_call_target="tpu_custom_call" | custom-call | flops 671088640 | bytes 7340032 | tf_op jit(solution)/shard_map/embed/pallas_call | solution.py:367
  31.8 0.0 copy-start.9
  31.8 8.5 %all-to-all-start.1 = ((bf16[4,512,128]{2,1,0:T(8,128)(2,1)}), bf16[4,512,128]{2,1,0:T(8,128)(2,1)S(1)}, u32[]{:S(2)}, u32[]{:S(2)}) async-start(bf16[4,512,128]{2,1,0:T(8,128)(2,1)} %embed.1.emb_ref), calls=%async_computation.1 | async-start | bytes 1048576 | tf_op jit(solution)/shard_map/all_to_all | solution.py:35
  40.3 1.0 collective-permute-start.8
  41.3 1.5 collective-permute-start.4
  42.8 0.3 collective-permute-start.5
  43.1 1.9 %collective-permute-start.1 = (bf16[64,1024]{1,0:T(8,128)(2,1)S(1)}, bf16[64,1024]{1,0:T(8,128)(2,1)S(1)}, u32[]{:S(2)}, u32[]{:S(2)}) collective-permute-start(bf16[64,1024]{1,0:T(8,128)(2,1)S(1)} %copy-done.16), channel_id=1, source_target_pairs={{0,16},{16,32},{32,48},{48,0},{1,17},{17,33},{33,49},{49,1},{2,18}... | collective-permute-start | bytes 393224 | tf_op jit(solution)/shard_map/ppermute | solution.py:27
  45.0 9.9 %collective-permute-done.8.in_ref = bf16[64,1024]{1,0:T(8,128)(2,1)S(1)} collective-permute-done((bf16[64,1024]{1,0:T(8,128)(2,1)S(1)}, bf16[64,1024]{1,0:T(8,128)(2,1)S(1)}, u32[]{:S(2)}, u32[]{:S(2)}) %collective-permute-start.8) | collective-permute-done | bytes 131104 | tf_op jit(solution)/shard_map/ppermute | solution.py:27
  54.9 0.9 collective-permute-start.12
  55.9 0.5 collective-permute-start.13
  56.4 0.9 collective-permute-start.9
  57.3 0.0 collective-permute-done.5
  57.3 2.5 %collective-permute-start.7 = (bf16[128,1024]{1,0:T(8,128)(2,1)S(1)}, bf16[128,1024]{1,0:T(8,128)(2,1)S(1)}, u32[]{:S(2)}, u32[]{:S(2)}) collective-permute-start(bf16[128,1024]{1,0:T(8,128)(2,1)S(1)} %constant_dynamic-update-slice_fusion.2.refs_7_.refs_6_), channel_id=1, source_target_pairs={{0,192},{64,0},{128,64},{192,128},{1,193},{65,1},{129,65},{193,129... | collective-permute-start | bytes 786440 | tf_op jit(solution)/shard_map/ppermute | solution.py:27
  59.8 0.0 collective-permute-done.1
  59.9 0.0 collective-permute-start.6
  59.9 1.5 collective-permute-done.12
  61.4 0.2 collective-permute-start.2
  61.6 2.1 %collective-permute-done.13 = bf16[64,1024]{1,0:T(8,128)(2,1)S(1)} collective-permute-done((bf16[64,1024]{1,0:T(8,128)(2,1)S(1)}, bf16[64,1024]{1,0:T(8,128)(2,1)S(1)}, u32[]{:S(2)}, u32[]{:S(2)}) %collective-permute-start.13) | collective-permute-done | bytes 131104 | tf_op jit(solution)/shard_map/ppermute | solution.py:27
  63.7 3.1 %collective-permute-start.3 = (bf16[128,1024]{1,0:T(8,128)(2,1)S(1)}, bf16[128,1024]{1,0:T(8,128)(2,1)S(1)}, u32[]{:S(2)}, u32[]{:S(2)}) collective-permute-start(bf16[128,1024]{1,0:T(8,128)(2,1)S(1)} %constant_dynamic-update-slice_fusion.refs_4_.refs_3_), channel_id=1, source_target_pairs={{0,192},{64,0},{128,64},{192,128},{1,193},{65,1},{129,65},{193,129... | collective-permute-start | bytes 786440 | tf_op jit(solution)/shard_map/ppermute | solution.py:27
  66.9 0.0 collective-permute-done.9
  66.9 0.0 all-to-all-done.1.refs_1_
  66.9 0.1 collective-permute-start
  67.1 2.0 %collective-permute-done.7.refs_9_.refs_8_ = bf16[128,1024]{1,0:T(8,128)(2,1)S(1)} collective-permute-done((bf16[128,1024]{1,0:T(8,128)(2,1)S(1)}, bf16[128,1024]{1,0:T(8,128)(2,1)S(1)}, u32[]{:S(2)}, u32[]{:S(2)}) %collective-permute-start.7) | collective-permute-done | bytes 262176 | tf_op jit(solution)/shard_map/ppermute | solution.py:27
  69.0 1.4 collective-permute-start.15
  70.5 3.8 %collective-permute-done.2.refs_5_.refs_4_ = bf16[128,1024]{1,0:T(8,128)(2,1)S(1)} collective-permute-done((bf16[128,1024]{1,0:T(8,128)(2,1)S(1)}, bf16[128,1024]{1,0:T(8,128)(2,1)S(1)}, u32[]{:S(2)}, u32[]{:S(2)}) %collective-permute-start.2) | collective-permute-done | bytes 262176 | tf_op jit(solution)/shard_map/ppermute | solution.py:27
  74.2 1.1 collective-permute-start.10
  75.4 1.3 collective-permute-start.14
  76.6 0.8 collective-permute-start.11
  77.4 0.1 places.1.refs_3_.refs_2_.refs_1_
  77.6 0.0 copy-start.7
  77.6 0.6 copy-done.7
  78.1 1.3 collective-permute-start.17
  79.4 3.8 %collective-permute-done.10.refs_11_.refs_10_ = bf16[128,1024]{1,0:T(8,128)(2,1)} collective-permute-done((bf16[128,1024]{1,0:T(8,128)(2,1)S(1)}, bf16[128,1024]{1,0:T(8,128)(2,1)}, u32[]{:S(2)}, u32[]{:S(2)}) %collective-permute-start.10) | collective-permute-done | bytes 262176 | tf_op jit(solution)/shard_map/ppermute | solution.py:27
  83.2 2.8 %collective-permute-done.14.refs_14_.refs_13_ = bf16[128,1024]{1,0:T(8,128)(2,1)} collective-permute-done((bf16[128,1024]{1,0:T(8,128)(2,1)S(1)}, bf16[128,1024]{1,0:T(8,128)(2,1)}, u32[]{:S(2)}, u32[]{:S(2)}) %collective-permute-start.14) | collective-permute-done | bytes 262176 | tf_op jit(solution)/shard_map/ppermute | solution.py:27
  86.0 2.6 %collective-permute-start.19 = (bf16[128,1024]{1,0:T(8,128)(2,1)}, bf16[128,1024]{1,0:T(8,128)(2,1)S(1)}, u32[]{:S(2)}, u32[]{:S(2)}) collective-permute-start(bf16[128,1024]{1,0:T(8,128)(2,1)} %collective-permute-done.15.refs_15_.refs_14_), channel_id=1, source_target_pairs={{0,48},{16,0},{32,16},{48,32},{1,49},{17,1},{33,17},{49,33},{2,50}... | collective-permute-start | bytes 786440 | tf_op jit(solution)/shard_map/ppermute | solution.py:27
  88.6 0.1 pad_add_fusion.refs_0_.at_ref
  88.8 6.7 %near_scores.1 = (bf16[512,1536]{1,0:T(8,128)(2,1)}, f32[8,512]{1,0:T(8,128)S(1)}, bf16[512,1024]{1,0:T(8,128)(2,1)S(1)}) custom-call(s32[4]{0:T(128)S(1)} %pad_add_fusion.refs_0_.at_ref, bf16[4,512,128]{2,1,0:T(8,128)(2,1)S(1)} %all-to-all-done.1.refs_1_, bf16[4,512,128]{2,1,0:T(8,128)(2,1)S(1)} %collective-permute-done.refs_2_, ...), custom_call_target="tpu_custom_call" | custom-call | flops 1610612736 | bytes 6291456 | tf_op jit(solution)/shard_map/near_scores/pallas_call | solution.py:410
  95.6 0.6 copy-done.11
  96.2 0.1 copy-done.12
  96.3 0.1 copy-done.13
  96.4 0.1 copy-done.14
  96.5 4.8 %far_scores.1 = (bf16[512,512]{1,0:T(8,128)(2,1)}, f32[8,512]{1,0:T(8,128)S(1)}, f32[8,8,512]{2,1,0:T(8,128)}) custom-call(s32[4]{0:T(128)S(1)} %pad_add_fusion.refs_0_.at_ref, bf16[512,1024]{1,0:T(8,128)(2,1)S(1)} %get-tuple-element.16.refs_1_, s32[512,1]{1,0:T(8,128)S(1)} %places.1.refs_3_.refs_2_.refs_1_, ...), custom_call_target="tpu_custom_call" | custom-call | flops 536870912 | bytes 2097152 | tf_op jit(solution)/shard_map/far_scores/pallas_call | solution.py:435
  101.3 0.6 copy-done
  101.9 6.7 %all-to-all-start.2 = ((f32[8,8,512]{2,1,0:T(8,128)}), f32[8,8,512]{2,1,0:T(8,128)S(1)}, u32[]{:S(2)}, u32[]{:S(2)}) async-start(f32[8,8,512]{2,1,0:T(8,128)} %get-tuple-element.18), calls=%async_computation.2 | async-start | bytes 262144 | tf_op jit(solution)/shard_map/all_to_all | solution.py:35
  108.6 6.6 %near_gradient.1 = (f32[512,1024]{1,0:T(8,128)S(1)}, bf16[512,1024]{1,0:T(8,128)(2,1)S(1)}) custom-call(s32[4]{0:T(128)S(1)} %pad_add_fusion.refs_0_.at_ref, s32[512,1]{1,0:T(8,128)S(1)} %places.1.refs_3_.refs_2_.refs_1_, bf16[512,1536]{1,0:T(8,128)(2,1)} %get-tuple-element.20.refs_2_, bf16[128,1024]{1,0:T(8,128)(2,1)} %copy-done.17, ...), custom_call_target="tpu_custom_call" | custom-call | flops 3221225472 | bytes 6291456 | tf_op jit(solution)/shard_map/near_gradient/pallas_call | solution.py:425
  115.2 0.7 copy-done.4
  115.9 3.4 %far_gradient.1 = (f32[512,1024]{1,0:T(8,128)S(1)}, bf16[512,1024]{1,0:T(8,128)(2,1)S(1)}) custom-call(s32[4]{0:T(128)S(1)} %copy-done.4, s32[512,1]{1,0:T(8,128)S(1)} %places.1.refs_3_.refs_2_.refs_1_, bf16[512,512]{1,0:T(8,128)(2,1)} %get-tuple-element.19.refs_2_, f32[8,512]{1,0:T(8,128)S(1)} %get-tuple-element.15.refs_3_.near_ref, ...), custom_call_target="tpu_custom_call" | custom-call | flops 1073741824 | bytes 2097152 | tf_op jit(solution)/shard_map/far_gradient/pallas_call | solution.py:450
  119.4 0.7 copy-done.2
  120.1 0.7 copy-done.5
  120.7 0.7 copy-done.8
  121.4 1.4 combine.1
  122.9 0.8 collective-permute-start.20
  123.7 2.3 %collective-permute-done.20 = f32[4,512,128]{2,1,0:T(8,128)S(1)} collective-permute-done((f32[4,512,128]{2,1,0:T(8,128)S(1)}, f32[4,512,128]{2,1,0:T(8,128)S(1)}, u32[]{:S(2)}, u32[]{:S(2)}) %collective-permute-start.20) | collective-permute-done | bytes 1048608 | tf_op jit(solution)/shard_map/ppermute | solution.py:27
  125.9 0.1 fusion
  126.1 23.2 %all_to_all.26.parts_ref = bf16[4,512,128]{2,1,0:T(8,128)(2,1)S(1)} all-to-all(bf16[4,512,128]{2,1,0:T(8,128)(2,1)S(1)} %get-tuple-element.28), channel_id=1, replica_groups=mesh['y'=4,'x'=4,'zh'=4,'core'=2,'tw'=2] {'zh'}, dimensions={0} | all-to-all | bytes 1048576 | tf_op jit(solution)/shard_map/all_to_all | solution.py:35
  149.3 5.9 %weight.1 = bf16[5120,128]{1,0:T(8,128)(2,1)S(1)} custom-call(s32[4]{0:T(128)S(1)} %copy-done.6, bf16[512,5120]{1,0:T(8,128)(2,1)} %images_ref.3, f32[4,512,128]{2,1,0:T(8,128)S(1)} %get-tuple-element.29.chip_ref, bf16[4,512,128]{2,1,0:T(8,128)(2,1)S(1)} %all_to_all.26.parts_ref, bf16[4,512,128]{2,1,0:T(8,128)(2,1)} %embed.1.emb_ref, ...), custom_call_target="tpu_custom_call" | custom-call | tf_op jit(solution)/shard_map/weight/pallas_call | solution.py:477
  155.1 22.6 %all_to_all.27 = bf16[16,320,128]{2,1,0:T(8,128)(2,1)S(1)} all-to-all(bf16[16,320,128]{2,1,0:T(8,128)(2,1)S(1)} %bitcast.9), channel_id=1, replica_groups=mesh['y'=4,'x'=4,'zh'=4,'core'=2,'tw'=2] {'y','x'}, dimensions={0} | all-to-all | bytes 2621440 | tf_op jit(solution)/shard_map/all_to_all | solution.py:35
  177.7 0.2 convert_reduce_fusion
  177.9 0.1 collective-permute-start.21
  178.0 0.6 slice.3
  178.6 4.7 %collective-permute-done.21 = f32[320,128]{1,0:T(8,128)S(1)} collective-permute-done((f32[320,128]{1,0:T(8,128)S(1)}, f32[320,128]{1,0:T(8,128)S(1)}, u32[]{:S(2)}, u32[]{:S(2)}) %collective-permute-start.21) | collective-permute-done | bytes 163872 | tf_op jit(solution)/shard_map/ppermute | solution.py:27
  183.3 0.7 add.11
  (58 shorter events, 0.2 us)
Async XLA Ops:
  27.6 12.7 %copy-start.16 = (bf16[64,1024]{1,0:T(8,128)(2,1)S(1)}, bf16[64,1024]{1,0:T(8,128)(2,1)}, u32[]{:S(2)}) copy-start(bf16[64,1024]{1,0:T(8,128)(2,1)} %param.7) | copy-start | bytes 393220
  31.8 45.6 %copy-start.9 = (s32[512]{0:T(512)S(1)}, s32[512]{0:T(512)}, u32[]{:S(2)}) copy-start(s32[512]{0:T(512)} %param.8) | copy-start | bytes 6148
  31.8 35.1 %all-to-all-start.1 = ((bf16[4,512,128]{2,1,0:T(8,128)(2,1)}), bf16[4,512,128]{2,1,0:T(8,128)(2,1)S(1)}, u32[]{:S(2)}, u32[]{:S(2)}) async-start(bf16[4,512,128]{2,1,0:T(8,128)(2,1)} %embed.1.emb_ref), calls=%async_computation.1 | async-start | bytes 1048576 | tf_op jit(solution)/shard_map/all_to_all | solution.py:35
  40.3 37.2 %copy-start.10 = (s32[512]{0:T(512)S(1)}, s32[512]{0:T(512)}, u32[]{:S(2)}) copy-start(s32[512]{0:T(512)} %param.9) | copy-start | bytes 6148
  40.3 14.6 %collective-permute-start.8 = (bf16[64,1024]{1,0:T(8,128)(2,1)S(1)}, bf16[64,1024]{1,0:T(8,128)(2,1)S(1)}, u32[]{:S(2)}, u32[]{:S(2)}) collective-permute-start(bf16[64,1024]{1,0:T(8,128)(2,1)S(1)} %copy-done.16), channel_id=1, source_target_pairs={{0,1},{1,0},{2,3},{3,2},{4,5},{5,4},{6,7},{7,6},{8,9},{9,8},{10,11... | collective-permute-start | bytes 393224 | tf_op jit(solution)/shard_map/ppermute | solution.py:27
  41.3 15.0 %collective-permute-start.4 = (bf16[64,1024]{1,0:T(8,128)(2,1)S(1)}, bf16[64,1024]{1,0:T(8,128)(2,1)S(1)}, u32[]{:S(2)}, u32[]{:S(2)}) collective-permute-start(bf16[64,1024]{1,0:T(8,128)(2,1)S(1)} %copy-done.16), channel_id=1, source_target_pairs={{0,48},{16,0},{32,16},{48,32},{1,49},{17,1},{33,17},{49,33},{2,50}... | collective-permute-start | bytes 393224 | tf_op jit(solution)/shard_map/ppermute | solution.py:27
  42.8 14.5 %collective-permute-start.5 = (bf16[64,1024]{1,0:T(8,128)(2,1)S(1)}, bf16[64,1024]{1,0:T(8,128)(2,1)S(1)}, u32[]{:S(2)}, u32[]{:S(2)}) collective-permute-start(bf16[64,1024]{1,0:T(8,128)(2,1)S(1)} %copy-done.16), channel_id=1, source_target_pairs={{0,32},{16,48},{32,0},{48,16},{1,33},{17,49},{33,1},{49,17},{2,34}... | collective-permute-start | bytes 393224 | tf_op jit(solution)/shard_map/ppermute | solution.py:27
  43.1 16.7 %collective-permute-start.1 = (bf16[64,1024]{1,0:T(8,128)(2,1)S(1)}, bf16[64,1024]{1,0:T(8,128)(2,1)S(1)}, u32[]{:S(2)}, u32[]{:S(2)}) collective-permute-start(bf16[64,1024]{1,0:T(8,128)(2,1)S(1)} %copy-done.16), channel_id=1, source_target_pairs={{0,16},{16,32},{32,48},{48,0},{1,17},{17,33},{33,49},{49,1},{2,18}... | collective-permute-start | bytes 393224 | tf_op jit(solution)/shard_map/ppermute | solution.py:27
  54.9 6.4 %collective-permute-start.12 = (bf16[64,1024]{1,0:T(8,128)(2,1)S(1)}, bf16[64,1024]{1,0:T(8,128)(2,1)S(1)}, u32[]{:S(2)}, u32[]{:S(2)}) collective-permute-start(bf16[64,1024]{1,0:T(8,128)(2,1)S(1)} %gate.1), channel_id=1, source_target_pairs={{0,192},{64,0},{128,64},{192,128},{1,193},{65,1},{129,65},{193,129... | collective-permute-start | bytes 393224 | tf_op jit(solution)/shard_map/ppermute | solution.py:27
  55.9 7.9 %collective-permute-start.13 = (bf16[64,1024]{1,0:T(8,128)(2,1)S(1)}, bf16[64,1024]{1,0:T(8,128)(2,1)S(1)}, u32[]{:S(2)}, u32[]{:S(2)}) collective-permute-start(bf16[64,1024]{1,0:T(8,128)(2,1)S(1)} %gate.1), channel_id=1, source_target_pairs={{0,128},{64,192},{128,0},{192,64},{1,129},{65,193},{129,1},{193,65... | collective-permute-start | bytes 393224 | tf_op jit(solution)/shard_map/ppermute | solution.py:27
  56.4 10.5 %collective-permute-start.9 = (bf16[64,1024]{1,0:T(8,128)(2,1)S(1)}, bf16[64,1024]{1,0:T(8,128)(2,1)S(1)}, u32[]{:S(2)}, u32[]{:S(2)}) collective-permute-start(bf16[64,1024]{1,0:T(8,128)(2,1)S(1)} %gate.1), channel_id=1, source_target_pairs={{0,64},{64,128},{128,192},{192,0},{1,65},{65,129},{129,193},{193,1... | collective-permute-start | bytes 393224 | tf_op jit(solution)/shard_map/ppermute | solution.py:27
  57.3 31.4 %copy-start.19 = (bf16[128,1024]{1,0:T(8,128)(2,1)}, bf16[128,1024]{1,0:T(8,128)(2,1)S(1)}, u32[]{:S(2)}) copy-start(bf16[128,1024]{1,0:T(8,128)(2,1)S(1)} %constant_dynamic-update-slice_fusion.2.refs_7_.refs_6_) | copy-start | bytes 786436
  57.3 11.7 %collective-permute-start.7 = (bf16[128,1024]{1,0:T(8,128)(2,1)S(1)}, bf16[128,1024]{1,0:T(8,128)(2,1)S(1)}, u32[]{:S(2)}, u32[]{:S(2)}) collective-permute-start(bf16[128,1024]{1,0:T(8,128)(2,1)S(1)} %constant_dynamic-update-slice_fusion.2.refs_7_.refs_6_), channel_id=1, source_target_pairs={{0,192},{64,0},{128,64},{192,128},{1,193},{65,1},{129,65},{193,129... | collective-permute-start | bytes 786440 | tf_op jit(solution)/shard_map/ppermute | solution.py:27
  59.9 15.5 %collective-permute-start.6 = (bf16[128,1024]{1,0:T(8,128)(2,1)S(1)}, bf16[128,1024]{1,0:T(8,128)(2,1)S(1)}, u32[]{:S(2)}, u32[]{:S(2)}) collective-permute-start(bf16[128,1024]{1,0:T(8,128)(2,1)S(1)} %constant_dynamic-update-slice_fusion.2.refs_7_.refs_6_), channel_id=1, source_target_pairs={{0,64},{64,128},{128,192},{192,0},{1,65},{65,129},{129,193},{193,1... | collective-permute-start | bytes 786440 | tf_op jit(solution)/shard_map/ppermute | solution.py:27
  59.9 28.9 %copy-start.17 = (bf16[128,1024]{1,0:T(8,128)(2,1)}, bf16[128,1024]{1,0:T(8,128)(2,1)S(1)}, u32[]{:S(2)}) copy-start(bf16[128,1024]{1,0:T(8,128)(2,1)S(1)} %constant_dynamic-update-slice_fusion.refs_4_.refs_3_) | copy-start | bytes 786436
  61.4 12.9 %collective-permute-start.2 = (bf16[128,1024]{1,0:T(8,128)(2,1)S(1)}, bf16[128,1024]{1,0:T(8,128)(2,1)S(1)}, u32[]{:S(2)}, u32[]{:S(2)}) collective-permute-start(bf16[128,1024]{1,0:T(8,128)(2,1)S(1)} %constant_dynamic-update-slice_fusion.refs_4_.refs_3_), channel_id=1, source_target_pairs={{0,64},{64,128},{128,192},{192,0},{1,65},{65,129},{129,193},{193,1... | collective-permute-start | bytes 786440 | tf_op jit(solution)/shard_map/ppermute | solution.py:27
  63.7 12.9 %collective-permute-start.3 = (bf16[128,1024]{1,0:T(8,128)(2,1)S(1)}, bf16[128,1024]{1,0:T(8,128)(2,1)S(1)}, u32[]{:S(2)}, u32[]{:S(2)}) collective-permute-start(bf16[128,1024]{1,0:T(8,128)(2,1)S(1)} %constant_dynamic-update-slice_fusion.refs_4_.refs_3_), channel_id=1, source_target_pairs={{0,192},{64,0},{128,64},{192,128},{1,193},{65,1},{129,65},{193,129... | collective-permute-start | bytes 786440 | tf_op jit(solution)/shard_map/ppermute | solution.py:27
  66.9 21.8 %collective-permute-start = (bf16[4,512,128]{2,1,0:T(8,128)(2,1)S(1)}, bf16[4,512,128]{2,1,0:T(8,128)(2,1)S(1)}, u32[]{:S(2)}, u32[]{:S(2)}) collective-permute-start(bf16[4,512,128]{2,1,0:T(8,128)(2,1)S(1)} %all-to-all-done.1.refs_1_), channel_id=1, source_target_pairs={{0,2},{2,0},{1,3},{3,1},{4,6},{6,4},{5,7},{7,5},{8,10},{10,8},{9,1... | collective-permute-start | bytes 1572872 | tf_op jit(solution)/shard_map/ppermute | solution.py:27
  67.0 21.7 %copy-start.18 = (bf16[128,1024]{1,0:T(8,128)(2,1)}, bf16[128,1024]{1,0:T(8,128)(2,1)S(1)}, u32[]{:S(2)}) copy-start(bf16[128,1024]{1,0:T(8,128)(2,1)S(1)} %constant_dynamic-update-slice_fusion.4.refs_13_.refs_12_) | copy-start | bytes 786436
  67.1 21.7 %copy-start.15 = (bf16[128,1024]{1,0:T(8,128)(2,1)}, bf16[128,1024]{1,0:T(8,128)(2,1)S(1)}, u32[]{:S(2)}) copy-start(bf16[128,1024]{1,0:T(8,128)(2,1)S(1)} %pad_maximum_fusion.refs_10_.refs_9_) | copy-start | bytes 786436
  69.0 19.7 %copy-start.20 = (bf16[128,1024]{1,0:T(8,128)(2,1)}, bf16[128,1024]{1,0:T(8,128)(2,1)S(1)}, u32[]{:S(2)}) copy-start(bf16[128,1024]{1,0:T(8,128)(2,1)S(1)} %collective-permute-done.7.refs_9_.refs_8_) | copy-start | bytes 786436
  69.0 9.1 %collective-permute-start.15 = (bf16[128,1024]{1,0:T(8,128)(2,1)S(1)}, bf16[128,1024]{1,0:T(8,128)(2,1)}, u32[]{:S(2)}, u32[]{:S(2)}) collective-permute-start(bf16[128,1024]{1,0:T(8,128)(2,1)S(1)} %constant_dynamic-update-slice_fusion.4.refs_13_.refs_12_), channel_id=1, source_target_pairs={{0,48},{16,0},{32,16},{48,32},{1,49},{17,1},{33,17},{49,33},{2,50}... | collective-permute-start | bytes 786440 | tf_op jit(solution)/shard_map/ppermute | solution.py:27
  74.2 14.5 %copy-start.22 = (bf16[128,1024]{1,0:T(8,128)(2,1)}, bf16[128,1024]{1,0:T(8,128)(2,1)S(1)}, u32[]{:S(2)}) copy-start(bf16[128,1024]{1,0:T(8,128)(2,1)S(1)} %collective-permute-done.2.refs_5_.refs_4_) | copy-start | bytes 786436
  74.2 8.9 %collective-permute-start.10 = (bf16[128,1024]{1,0:T(8,128)(2,1)S(1)}, bf16[128,1024]{1,0:T(8,128)(2,1)}, u32[]{:S(2)}, u32[]{:S(2)}) collective-permute-start(bf16[128,1024]{1,0:T(8,128)(2,1)S(1)} %pad_maximum_fusion.refs_10_.refs_9_), channel_id=1, source_target_pairs={{0,16},{16,32},{32,48},{48,0},{1,17},{17,33},{33,49},{49,1},{2,18}... | collective-permute-start | bytes 786440 | tf_op jit(solution)/shard_map/ppermute | solution.py:27
  75.4 13.4 %copy-start.21 = (bf16[128,1024]{1,0:T(8,128)(2,1)}, bf16[128,1024]{1,0:T(8,128)(2,1)S(1)}, u32[]{:S(2)}) copy-start(bf16[128,1024]{1,0:T(8,128)(2,1)S(1)} %collective-permute-done.6.refs_8_.refs_7_) | copy-start | bytes 786436
  75.4 10.6 %collective-permute-start.14 = (bf16[128,1024]{1,0:T(8,128)(2,1)S(1)}, bf16[128,1024]{1,0:T(8,128)(2,1)}, u32[]{:S(2)}, u32[]{:S(2)}) collective-permute-start(bf16[128,1024]{1,0:T(8,128)(2,1)S(1)} %constant_dynamic-update-slice_fusion.4.refs_13_.refs_12_), channel_id=1, source_target_pairs={{0,16},{16,32},{32,48},{48,0},{1,17},{17,33},{33,49},{49,1},{2,18}... | collective-permute-start | bytes 786440 | tf_op jit(solution)/shard_map/ppermute | solution.py:27
  76.6 12.1 %copy-start.23 = (bf16[128,1024]{1,0:T(8,128)(2,1)}, bf16[128,1024]{1,0:T(8,128)(2,1)S(1)}, u32[]{:S(2)}) copy-start(bf16[128,1024]{1,0:T(8,128)(2,1)S(1)} %collective-permute-done.3.refs_6_.refs_5_) | copy-start | bytes 786436
  76.6 12.0 %collective-permute-start.11 = (bf16[128,1024]{1,0:T(8,128)(2,1)S(1)}, bf16[128,1024]{1,0:T(8,128)(2,1)}, u32[]{:S(2)}, u32[]{:S(2)}) collective-permute-start(bf16[128,1024]{1,0:T(8,128)(2,1)S(1)} %pad_maximum_fusion.refs_10_.refs_9_), channel_id=1, source_target_pairs={{0,48},{16,0},{32,16},{48,32},{1,49},{17,1},{33,17},{49,33},{2,50}... | collective-permute-start | bytes 786440 | tf_op jit(solution)/shard_map/ppermute | solution.py:27
  77.6 0.6 copy-start.7
  78.1 17.3 %collective-permute-start.17 = (bf16[128,1024]{1,0:T(8,128)(2,1)S(1)}, bf16[128,1024]{1,0:T(8,128)(2,1)S(1)}, u32[]{:S(2)}, u32[]{:S(2)}) collective-permute-start(bf16[128,1024]{1,0:T(8,128)(2,1)S(1)} %collective-permute-done.7.refs_9_.refs_8_), channel_id=1, source_target_pairs={{0,192},{64,0},{128,64},{192,128},{1,193},{65,1},{129,65},{193,129... | collective-permute-start | bytes 786440 | tf_op jit(solution)/shard_map/ppermute | solution.py:27
  83.2 12.3 %collective-permute-start.16 = (bf16[128,1024]{1,0:T(8,128)(2,1)S(1)}, bf16[128,1024]{1,0:T(8,128)(2,1)S(1)}, u32[]{:S(2)}, u32[]{:S(2)}) collective-permute-start(bf16[128,1024]{1,0:T(8,128)(2,1)S(1)} %collective-permute-done.2.refs_5_.refs_4_), channel_id=1, source_target_pairs={{0,64},{64,128},{128,192},{192,0},{1,65},{65,129},{129,193},{193,1... | collective-permute-start | bytes 786440 | tf_op jit(solution)/shard_map/ppermute | solution.py:27
  86.0 9.5 %collective-permute-start.19 = (bf16[128,1024]{1,0:T(8,128)(2,1)}, bf16[128,1024]{1,0:T(8,128)(2,1)S(1)}, u32[]{:S(2)}, u32[]{:S(2)}) collective-permute-start(bf16[128,1024]{1,0:T(8,128)(2,1)} %collective-permute-done.15.refs_15_.refs_14_), channel_id=1, source_target_pairs={{0,48},{16,0},{32,16},{48,32},{1,49},{17,1},{33,17},{49,33},{2,50}... | collective-permute-start | bytes 786440 | tf_op jit(solution)/shard_map/ppermute | solution.py:27
  88.6 6.9 %collective-permute-start.18 = (bf16[128,1024]{1,0:T(8,128)(2,1)}, bf16[128,1024]{1,0:T(8,128)(2,1)S(1)}, u32[]{:S(2)}, u32[]{:S(2)}) collective-permute-start(bf16[128,1024]{1,0:T(8,128)(2,1)} %collective-permute-done.10.refs_11_.refs_10_), channel_id=1, source_target_pairs={{0,16},{16,32},{32,48},{48,0},{1,17},{17,33},{33,49},{49,1},{2,18}... | collective-permute-start | bytes 786440 | tf_op jit(solution)/shard_map/ppermute | solution.py:27
  88.7 19.9 %copy-start.3 = (s32[4]{0:T(128)}, s32[4]{0:T(128)S(1)}, u32[]{:S(2)}) copy-start(s32[4]{0:T(128)S(1)} %pad_add_fusion.refs_0_.at_ref) | copy-start | bytes 52
  95.5 0.7 copy-start.11
  95.5 0.8 copy-start.12
  95.5 0.8 copy-start.13
  95.6 0.9 copy-start.14
  101.3 0.6 copy-start
  101.9 17.4 %all-to-all-start.2 = ((f32[8,8,512]{2,1,0:T(8,128)}), f32[8,8,512]{2,1,0:T(8,128)S(1)}, u32[]{:S(2)}, u32[]{:S(2)}) async-start(f32[8,8,512]{2,1,0:T(8,128)} %get-tuple-element.18), calls=%async_computation.2 | async-start | bytes 262144 | tf_op jit(solution)/shard_map/all_to_all | solution.py:35
  108.6 6.6 %copy-start.1 = (f32[8,512]{1,0:T(8,128)S(1)}, f32[8,512]{1,0:T(8,128)}, u32[]{:S(2)}) copy-start(f32[8,512]{1,0:T(8,128)} %copy-done) | copy-start | bytes 49156
  115.2 0.7 copy-start.4
  119.3 0.7 copy-start.2
  120.1 0.7 copy-start.5
  120.7 0.7 copy-start.8
  122.9 3.1 %collective-permute-start.20 = (f32[4,512,128]{2,1,0:T(8,128)S(1)}, f32[4,512,128]{2,1,0:T(8,128)S(1)}, u32[]{:S(2)}, u32[]{:S(2)}) collective-permute-start(f32[4,512,128]{2,1,0:T(8,128)S(1)} %get-tuple-element.27), channel_id=1, source_target_pairs={{0,2},{2,0},{1,3},{3,1},{4,6},{6,4},{5,7},{7,5},{8,10},{10,8},{9,1... | collective-permute-start | bytes 3145736 | tf_op jit(solution)/shard_map/ppermute | solution.py:27
  125.9 23.3 %copy-start.6 = (s32[4]{0:T(128)S(1)}, s32[4]{0:T(128)}, u32[]{:S(2)}) copy-start(s32[4]{0:T(128)} %copy-done.3) | copy-start | bytes 52
  177.9 5.4 %collective-permute-start.21 = (f32[320,128]{1,0:T(8,128)S(1)}, f32[320,128]{1,0:T(8,128)S(1)}, u32[]{:S(2)}, u32[]{:S(2)}) collective-permute-start(f32[320,128]{1,0:T(8,128)S(1)} %convert_reduce_fusion), channel_id=1, source_target_pairs={{0,1},{1,0},{2,3},{3,2},{4,5},{5,4},{6,7},{7,6},{8,9},{9,8},{10,11... | collective-permute-start | bytes 491528 | tf_op jit(solution)/shard_map/ppermute | solution.py:27

commit v3 on v2

v3 whole, which is shorter than its diff:
```python
import jax
import jax.numpy as jnp
from jax import lax
from jax.experimental import pallas as pl
from jax.experimental.pallas import tpu as pltpu
from jax.sharding import Mesh
from jax.sharding import PartitionSpec as P

AXES = ("y", "x", "zh", "core", "tw")
PLANE = ("y", "x")
FSDP_TOWER = ("y", "x", "tw")
REL = (0, 3, 1, 2)
NEAR = (0, 3, 1)
AROUND = (0, 3, 1, 2)
FAR = (2,)

epsilon = 1e-06
score_scale = 100.0
f32 = jnp.float32
bf16 = jnp.bfloat16
VMEM = pl.BlockSpec(memory_space=pltpu.VMEM)
HBM = pl.BlockSpec(memory_space=pltpu.HBM)


def shifted(x, axis, step):
    n = lax.axis_size(axis)
    return lax.ppermute(x, axis, [(i, (i + step) % n) for i in range(n)])


def in_hbm(x):
    return pltpu.with_memory_space_constraint(x, pltpu.HBM)


def exchanged(x, axis):
    return lax.all_to_all(x, axis, 0, 0, tiled=True)


def from_others(x, axis):
    return [shifted(x, axis, step) for step in (1, -1, 2)]


def gathered_texts(texts, other_texts):
    near, far = [], []
    for part, inner, outer in ((texts, "x", "y"), (other_texts, "y", "x")):
        below, above, across = (shifted(part, inner, step) for step in (1, -1, 2))
        halves = [jnp.concatenate([part, below]), jnp.concatenate([above, across])]
        for half, toward in zip(halves, (1, -1)):
            first = shifted(half, outer, toward)
            second = shifted(half, outer, -toward)
            near += [half, first, second] if toward == 1 else [half, second, first]
            far.append(shifted(first, outer, toward))
    return [in_hbm(piece) for piece in near], [in_hbm(piece) for piece in far]


def fetch(pieces, whole, sem):
    at, copies = 0, []
    for k, piece in enumerate(pieces):
        n = piece.shape[0]
        copies.append(pltpu.make_async_copy(piece, whole.at[pl.ds(at, n)], sem.at[k]))
        at += n
    for copy in copies:
        copy.start()
    return copies


def tp_index():
    return lax.axis_index("zh") * 2 + lax.axis_index("core")


def column_places(group, steps):
    y, x, tp, tower = lax.axis_index("y"), lax.axis_index("x"), tp_index(), lax.axis_index("tw")
    lane = lax.broadcasted_iota(jnp.int32, (1, 128), 1)
    places = []
    for side in range(2):
        tw = tower if side == 0 else 1 - tower
        for half in range(2):
            for step in steps:
                firsts = []
                for inner in REL[2 * half : 2 * half + 2]:
                    ahead = (step, inner) if side == 0 else (inner, step)
                    plane = lax.rem(y + ahead[0], 4) * 4 + lax.rem(x + ahead[1], 4)
                    firsts.append(((plane * 8 + tp) * 2 + tw) * group)
                places.append(jnp.where(lane < group, firsts[0], firsts[1] - group) + lane)
    return places


def as_columns(lines):
    n = lines[0].shape[1]
    spare = jnp.zeros((128 - len(lines), n), f32)
    return jnp.concatenate([*lines, spare], axis=0).T


def column_copies(whole, held, sem, step):
    copies = []
    for k in range(whole.shape[1] // step):
        here = pl.ds(k * step, step)
        copies.append(pltpu.make_async_copy(whole.at[:, here], held.at[:, here], sem.at[k]))
        copies[-1].start()
    return copies


def gate_kernel(in_ref, out_ref):
    out_ref[...] = in_ref[...]


def spread_kernel(in_ref, out_ref, sem):
    copies = [pltpu.make_async_copy(in_ref, out_ref.at[k], sem.at[k]) for k in range(16)]
    for copy in copies:
        copy.start()
    for copy in copies:
        copy.wait()


def sign_kernel(forget_ref, out_ref, sign, sem):
    sign[...] = 1.0 - 2.0 * forget_ref[...].astype(f32)
    copy = pltpu.make_async_copy(sign, out_ref, sem)
    copy.start()
    copy.wait()


def place_kernel(perm_ref, out_ref):
    out_ref[...] = as_columns([perm_ref[...].astype(f32)])[:, 0:1].astype(jnp.int32)


def embed_kernel(images_ref, weight_ref, out_ref, held, rounded, sem, out_sem):
    step = 128
    for k in range(images_ref.shape[0] // step):
        here = pl.ds(k * step, step)
        pltpu.make_async_copy(images_ref.at[here], held.at[here], sem.at[k]).start()

    @pl.loop(0, images_ref.shape[0] // step)
    def _(k):
        here = pl.ds(pl.multiple_of(k * step, step), step)
        pltpu.make_async_copy(images_ref.at[here], held.at[here], sem.at[k]).wait()
        rounded[here, :] = jnp.dot(
            held[here, :], weight_ref[...], preferred_element_type=f32
        ).astype(bf16)
        pltpu.make_async_copy(rounded.at[here], out_ref.at[here], out_sem).start()

    pltpu.make_async_copy(rounded, out_ref, out_sem).wait()


def merged(one, two):
    top = jnp.maximum(one[0:1], two[0:1])
    first, second = jnp.exp(one[0:1] - top), jnp.exp(two[0:1] - top)
    total = one[1:2] * first + two[1:2] * second
    moment = one[2:3] * first + two[2:3] * second
    return jnp.concatenate([top, total, moment, one[3:4] + two[3:4], one[4:8]], axis=0)


def score_columns(unit, copies, whole, score, high, soft, perm_ref, group, steps, out_ref, out_sem, after):
    rows = unit.shape[0]
    step = 512
    per = len(copies) * step // whole.shape[0]
    for c in range(whole.shape[0] // step):
        for copy in copies[c * per : (c + 1) * per]:
            copy.wait()
        at = c * step
        chunk = score_scale * lax.dot_general(
            unit[...], whole[pl.ds(at, step)], (((1,), (1,)), ((), ())), preferred_element_type=f32
        )
        score[:, pl.ds(at, step)] = chunk
        peak = chunk[:, :128]
        for k in range(128, step, 128):
            peak = jnp.maximum(peak, chunk[:, k : k + 128])
        high[...] = peak if c == 0 else jnp.maximum(high[...], peak)

    places = column_places(group, steps)
    band = 128

    def one_band(at):
        here = pl.ds(at, band)
        perm = perm_ref[here, :]
        top = jnp.max(high[here, :], axis=1, keepdims=True)
        total = jnp.zeros((band, 128), f32)
        moment = jnp.zeros((band, 128), f32)
        found = jnp.zeros((band, 128), f32)
        for k in range(len(places)):
            cols = pl.ds(k * 128, 128)
            logit = score[here, cols]
            p = jnp.exp(logit - top)
            hit = perm == places[k]
            total += p
            moment += p * logit
            found += jnp.where(hit, logit, 0.0)
            soft[here, cols] = jnp.where(hit, 0.0, p).astype(bf16)
        if out_ref is not None:
            pltpu.make_async_copy(soft.at[here], out_ref.at[here], out_sem).start()
        sums = [jnp.sum(v, axis=1, keepdims=True) for v in (total, moment, found)]
        which = lax.broadcasted_iota(jnp.int32, (band, 128), 1)
        tile = jnp.where(which == 0, top, 0.0)
        for k, v in enumerate(sums):
            tile = jnp.where(which == k + 1, v, tile)
        high[here, :] = tile

    if after is None:
        pl.loop(0, rows // band)(lambda r: one_band(pl.multiple_of(r * band, band)))
    else:

        @pl.loop(0, rows // (2 * band))
        def _(r):
            for k in range(2):
                at = pl.multiple_of((2 * r + k) * band, band)
                one_band(at)
                after(at, band)

    return high[...]


def near_kernel(n, group, *refs):
    parts, perm_ref = refs[:8], refs[8]
    pieces = refs[9 : 9 + n]
    soft_ref, hard_ref, stats_ref, unit = refs[9 + n : 13 + n]
    whole, score, high, both, one_hot, soft, hard, sem, out_sem = refs[13 + n :]
    copies = fetch(pieces, whole, sem)
    rows, feats = parts[0].shape
    zh, core = lax.axis_index("zh"), lax.axis_index("core")
    square = jnp.zeros((rows, feats), f32)
    for ref in parts:
        part = ref[...].astype(f32)
        square += part * part
    rnorm = lax.rsqrt(jnp.sum(square, axis=1, keepdims=True) + epsilon)
    for k, ref in enumerate(parts):
        owner = lax.rem(zh + AROUND[k % 4], 4) * 2 + (core if k < 4 else 1 - core)
        to = pl.multiple_of(owner * feats, feats)
        unit[:, pl.ds(to, feats)] = (ref[...].astype(f32) * rnorm).astype(bf16)
    places = column_places(group, NEAR)

    def gradient(at, band):
        here = pl.ds(at, band)
        perm = perm_ref[here, :]
        for k in range(len(places)):
            one_hot[here, pl.ds(k * 128, 128)] = jnp.where(perm == places[k], 1.0, 0.0).astype(bf16)
        soft[here, :] = jnp.dot(both[here, :], whole[...], preferred_element_type=f32)
        hard[here, :] = jnp.dot(one_hot[here, :], whole[...], preferred_element_type=f32).astype(bf16)
        for k, (here_ref, there) in enumerate(((soft, soft_ref), (hard, hard_ref))):
            pltpu.make_async_copy(here_ref.at[here], there.at[here], out_sem.at[k]).start()

    tile = score_columns(
        unit, copies, whole, score, high, both, perm_ref, group, NEAR, None, None, gradient
    )
    which = lax.broadcasted_iota(jnp.int32, (rows, 128), 1)
    stats_ref[...] = jnp.where(which == 4, rnorm, tile).T[:8]
    pltpu.make_async_copy(soft, soft_ref, out_sem.at[0]).wait()
    pltpu.make_async_copy(hard, hard_ref, out_sem.at[1]).wait()


def far_score_kernel(n, group, *refs):
    unit, perm_ref, near_ref, sign_ref = refs[:4]
    pieces = refs[4 : 4 + n]
    out_ref, tops_ref, stats_ref = refs[4 + n : 7 + n]
    whole, score, high, soft, tops, sign, sem, out_sem, more_sem = refs[7 + n :]
    copies = fetch(pieces, whole, sem)
    flag = pltpu.make_async_copy(sign_ref, sign, more_sem)
    flag.start()
    lines = score_columns(
        unit, copies, whole, score, high, soft, perm_ref, group, FAR, out_ref, out_sem, None
    ).T[:8]
    near = near_ref[...]
    flag.wait()
    both = jnp.concatenate([merged(near, lines)[:5], sign[...], near[0:1], lines[0:1]], axis=0)
    tops[...] = both
    kept = pltpu.make_async_copy(tops, tops_ref, more_sem)
    kept.start()
    stats_ref[...] = both
    pltpu.make_async_copy(soft, out_ref, out_sem).wait()
    kept.wait()


def far_gradient_kernel(n, group, *refs):
    perm_ref, p_ref, tops_ref, near_soft_ref, near_hard_ref = refs[:5]
    pieces = refs[5 : 5 + n]
    soft_ref, hard_ref = refs[5 + n : 7 + n]
    whole, both, tops, soft, hard, sem, p_sem, more_sem, near_sem, out_sem = refs[7 + n :]
    copies = [
        pltpu.make_async_copy(p_ref, both.at[pl.ds(0, p_ref.shape[0])], p_sem),
        pltpu.make_async_copy(tops_ref, tops, more_sem),
    ]
    for copy in copies:
        copy.start()
    copies += fetch(pieces, whole, sem)
    copies += [
        pltpu.make_async_copy(near_soft_ref, soft, near_sem.at[0]),
        pltpu.make_async_copy(near_hard_ref, hard, near_sem.at[1]),
    ]
    copies[-2].start()
    copies[-1].start()
    rows = p_ref.shape[0]
    places = column_places(group, FAR)
    perm = perm_ref[...]
    for k in range(len(places)):
        both[pl.ds(rows, rows), pl.ds(k * 128, 128)] = jnp.where(
            perm == places[k], 1.0, 0.0
        ).astype(bf16)
    for copy in copies:
        copy.wait()
    top = tops[0:1]
    factors = as_columns([jnp.exp(tops[6:7] - top), jnp.exp(tops[7:8] - top)])
    first, second = factors[:, 0:1], factors[:, 1:2]
    step = 512
    for c in range(whole.shape[1] // step):
        cols = pl.ds(c * step, step)
        out = jnp.dot(both[...], whole[:, cols], preferred_element_type=f32)
        soft[:, cols] = first * soft[:, cols] + second * out[:rows]
        hard[:, cols] = hard[:, cols] + out[rows:].astype(bf16)
        for k, (here, there) in enumerate(((soft, soft_ref), (hard, hard_ref))):
            pltpu.make_async_copy(here.at[:, cols], there.at[:, cols], out_sem.at[k]).start()
    pltpu.make_async_copy(soft, soft_ref, out_sem.at[0]).wait()
    pltpu.make_async_copy(hard, hard_ref, out_sem.at[1]).wait()


def pair_kernel(mine_ref, theirs_ref, out_ref):
    even = lax.axis_index("core") == 0
    mine, theirs = mine_ref[...], theirs_ref[...]
    first, second = jnp.where(even, mine, theirs), jnp.where(even, theirs, mine)
    out_ref[...] = merged(first, second)


def combine_kernel(*refs):
    around, (tops_ref, soft_ref, hard_ref) = refs[:4], refs[4:7]
    keep_ref, give_ref, lines_ref = refs[7:10]
    every, tops, soft, hard, sem = refs[10:]
    copies = [
        pltpu.make_async_copy(tops_ref, tops, sem.at[2]),
        pltpu.make_async_copy(soft_ref, soft, sem.at[0]),
        pltpu.make_async_copy(hard_ref, hard, sem.at[1]),
    ]
    for copy in copies:
        copy.start()
    zh, core = lax.axis_index("zh"), lax.axis_index("core")
    feats = keep_ref.shape[2]
    for step, ref in zip(AROUND, around):
        every[lax.rem(zh + step, 4)] = ref[...]
    rest = [every[k] for k in range(4)]
    high = rest[0][0:1]
    for v in rest[1:]:
        high = jnp.maximum(high, v[0:1])
    mass = sum(jnp.exp(v[0:1] - high) * v[1:2] for v in rest)
    lse = high + jnp.log(mass)
    target = sum(v[3:4] for v in rest)
    mean = sum(jnp.exp(v[0:1] - lse) * v[2:3] for v in rest)
    copies[0].wait()
    sign = tops[5:6]
    lines_ref[0:1] = lse - target
    lines_ref[1:2] = sign * (mean - target)
    lines_ref[2:3] = tops[4:5]
    for_soft = score_scale * sign * jnp.exp(tops[0:1] - lse)
    weight = (sign * (jnp.exp(target - lse) - 1.0)).astype(bf16).astype(f32)
    cols = as_columns([for_soft, score_scale * weight])
    first, second = cols[:, 0:1], cols[:, 1:2]
    for copy in copies[1:]:
        copy.wait()
    for k, step in enumerate(AROUND):
        for out, which in ((keep_ref, core), (give_ref, 1 - core)):
            owner = lax.rem(zh + step, 4) * 2 + which
            at = pl.ds(pl.multiple_of(owner * feats, feats), feats)
            out[k] = first * soft[:, at] + second * hard[:, at].astype(f32)


def weight_kernel(images_ref, own_ref, one_ref, two_ref, three_ref, emb_ref, lines_ref, out_ref, held, sem):
    step = 1024
    copies = column_copies(images_ref, held, sem, step)
    grad_unit = own_ref[...]
    for ref in (one_ref, two_ref, three_ref):
        grad_unit += ref[...].astype(f32)
    cols = as_columns([lines_ref[1:2], lines_ref[2:3]])
    radial, rnorm = cols[:, 0:1], cols[:, 1:2]
    unit = emb_ref[...].astype(f32) * rnorm
    grad_emb = rnorm * (grad_unit - unit * radial)
    lines = grad_emb.T.astype(bf16)
    for k, copy in enumerate(copies):
        copy.wait()
        here = pl.ds(k * step, step)
        out_ref[here, :] = jnp.dot(lines, held[:, here], preferred_element_type=f32).T.astype(bf16)


def local(images, img_weight, texts, pair_perm, forget):
    rows, width = images.shape
    feats = img_weight.shape[1]
    group = texts.shape[0]

    copies = pl.pallas_call(
        spread_kernel,
        name="spread",
        out_shape=pltpu.HBM((16, *img_weight.shape), bf16),
        in_specs=[VMEM],
        out_specs=HBM,
        scratch_shapes=[pltpu.SemaphoreType.DMA((16,))],
        compiler_params=pltpu.CompilerParams(vmem_limit_bytes=2 << 20),
    )(img_weight)
    weight = exchanged(copies, PLANE).reshape(width, feats)
    other_texts = shifted(texts, "tw", 1)
    other_texts = pl.pallas_call(
        gate_kernel,
        name="gate",
        out_shape=jax.ShapeDtypeStruct(texts.shape, bf16),
        in_specs=[VMEM],
        out_specs=VMEM,
        compiler_params=pltpu.CompilerParams(vmem_limit_bytes=2 << 20),
    )(other_texts)
    signs = pl.pallas_call(
        sign_kernel,
        name="signs",
        out_shape=pltpu.HBM((1, rows), f32),
        in_specs=[VMEM],
        out_specs=HBM,
        scratch_shapes=[pltpu.VMEM((1, rows), f32), pltpu.SemaphoreType.DMA],
        compiler_params=pltpu.CompilerParams(vmem_limit_bytes=2 << 20),
    )(forget.reshape(1, rows))
    perm = pl.pallas_call(
        place_kernel,
        name="places",
        out_shape=jax.ShapeDtypeStruct((rows, 1), jnp.int32),
        in_specs=[VMEM],
        out_specs=VMEM,
        compiler_params=pltpu.CompilerParams(vmem_limit_bytes=2 << 20),
    )(pair_perm.reshape(1, rows))
    near, far = gathered_texts(texts, other_texts)
    n, m = len(near), len(far)
    near_rows, far_rows = (sum(q.shape[0] for q in group) for group in (near, far))
    embed = near[0].shape[1]

    emb = pl.pallas_call(
        embed_kernel,
        name="embed",
        out_shape=pltpu.HBM((rows, feats), bf16),
        in_specs=[HBM, VMEM],
        out_specs=HBM,
        scratch_shapes=[
            pltpu.VMEM((rows, width), bf16),
            pltpu.VMEM((rows, feats), bf16),
            pltpu.SemaphoreType.DMA((rows // 128,)),
            pltpu.SemaphoreType.DMA,
        ],
        compiler_params=pltpu.CompilerParams(vmem_limit_bytes=16 << 20),
        cost_estimate=pl.CostEstimate(
            flops=2 * rows * width * feats, bytes_accessed=7 << 20, transcendentals=0
        ),
    )(in_hbm(images), weight)
    mine = [emb, *from_others(emb, "zh")]
    theirs = [shifted(part, "core", 1) for part in mine]

    def cost(flops, columns):
        return pl.CostEstimate(
            flops=flops, bytes_accessed=4 * embed * columns, transcendentals=rows * columns
        )

    gradient_shape = (pltpu.HBM((rows, embed), f32), pltpu.HBM((rows, embed), bf16))
    gradient_scratch = [pltpu.VMEM((rows, embed), f32), pltpu.VMEM((rows, embed), bf16)]
    work = 2 * rows * embed
    near_soft, near_hard, near_stats, unit = pl.pallas_call(
        lambda *refs: near_kernel(n, group, *refs),
        name="near",
        out_shape=(
            *gradient_shape,
            jax.ShapeDtypeStruct((8, rows), f32),
            jax.ShapeDtypeStruct((rows, embed), bf16),
        ),
        in_specs=[*[VMEM] * 9, *[HBM] * n],
        out_specs=(HBM, HBM, VMEM, VMEM),
        scratch_shapes=[
            pltpu.VMEM((near_rows, embed), bf16),
            pltpu.VMEM((rows, near_rows), f32),
            pltpu.VMEM((rows, 128), f32),
            pltpu.VMEM((rows, near_rows), bf16),
            pltpu.VMEM((rows, near_rows), bf16),
            *gradient_scratch,
            pltpu.SemaphoreType.DMA((n,)),
            pltpu.SemaphoreType.DMA((2,)),
        ],
        compiler_params=pltpu.CompilerParams(vmem_limit_bytes=24 << 20),
        cost_estimate=cost(3 * work * near_rows, near_rows),
    )(*mine, *theirs, perm, *near)
    far_p, tops, stats = pl.pallas_call(
        lambda *refs: far_score_kernel(m, group, *refs),
        name="far_scores",
        out_shape=(
            pltpu.HBM((rows, far_rows), bf16),
            pltpu.HBM((8, rows), f32),
            jax.ShapeDtypeStruct((8, rows), f32),
        ),
        in_specs=[VMEM, VMEM, VMEM, HBM, *[HBM] * m],
        out_specs=(HBM, HBM, VMEM),
        scratch_shapes=[
            pltpu.VMEM((far_rows, embed), bf16),
            pltpu.VMEM((rows, far_rows), f32),
            pltpu.VMEM((rows, 128), f32),
            pltpu.VMEM((rows, far_rows), bf16),
            pltpu.VMEM((8, rows), f32),
            pltpu.VMEM((1, rows), f32),
            pltpu.SemaphoreType.DMA((m,)),
            pltpu.SemaphoreType.DMA,
            pltpu.SemaphoreType.DMA,
        ],
        compiler_params=pltpu.CompilerParams(vmem_limit_bytes=12 << 20),
        cost_estimate=cost(work * far_rows, far_rows),
    )(unit, perm, near_stats, in_hbm(signs), *far)
    swapped = shifted(stats, "core", 1)
    chip_stats = pl.pallas_call(
        pair_kernel,
        name="pair",
        out_shape=jax.ShapeDtypeStruct((8, rows), f32),
        in_specs=[VMEM, VMEM],
        out_specs=VMEM,
        compiler_params=pltpu.CompilerParams(vmem_limit_bytes=2 << 20),
    )(stats, swapped)
    every = [chip_stats, *from_others(chip_stats, "zh")]
    soft, hard = pl.pallas_call(
        lambda *refs: far_gradient_kernel(m, group, *refs),
        name="far_gradient",
        out_shape=gradient_shape,
        in_specs=[VMEM, HBM, HBM, HBM, HBM, *[HBM] * m],
        out_specs=(HBM, HBM),
        scratch_shapes=[
            pltpu.VMEM((far_rows, embed), bf16),
            pltpu.VMEM((2 * rows, far_rows), bf16),
            pltpu.VMEM((8, rows), f32),
            *gradient_scratch,
            pltpu.SemaphoreType.DMA((m,)),
            pltpu.SemaphoreType.DMA,
            pltpu.SemaphoreType.DMA,
            pltpu.SemaphoreType.DMA((2,)),
            pltpu.SemaphoreType.DMA((2,)),
        ],
        compiler_params=pltpu.CompilerParams(vmem_limit_bytes=16 << 20),
        cost_estimate=cost(2 * work * far_rows, far_rows),
    )(perm, in_hbm(far_p), in_hbm(tops), in_hbm(near_soft), in_hbm(near_hard), *far)

    keep, give, lines = pl.pallas_call(
        combine_kernel,
        name="combine",
        out_shape=(
            jax.ShapeDtypeStruct((4, rows, feats), f32),
            jax.ShapeDtypeStruct((4, rows, feats), f32),
            jax.ShapeDtypeStruct((8, rows), f32),
        ),
        in_specs=[VMEM, VMEM, VMEM, VMEM, HBM, HBM, HBM],
        out_specs=(VMEM, VMEM, VMEM),
        scratch_shapes=[
            pltpu.VMEM((4, 8, rows), f32),
            pltpu.VMEM((8, rows), f32),
            *gradient_scratch,
            pltpu.SemaphoreType.DMA((3,)),
        ],
        compiler_params=pltpu.CompilerParams(vmem_limit_bytes=20 << 20),
    )(*every, in_hbm(tops), in_hbm(soft), in_hbm(hard))

    pair_loss = lines[0]
    chip = keep + shifted(give, "core", 1)
    away = [chip[k].astype(bf16) for k in (2, 1, 3)]
    parts = [shifted(part, "zh", step) for part, step in zip(away, (1, -1, 2))]
    share = pl.pallas_call(
        weight_kernel,
        name="weight",
        out_shape=jax.ShapeDtypeStruct((width, feats), bf16),
        in_specs=[HBM, *[VMEM] * 6],
        out_specs=VMEM,
        scratch_shapes=[pltpu.VMEM((rows, width), bf16), pltpu.SemaphoreType.DMA((width // 1024,))],
        compiler_params=pltpu.CompilerParams(vmem_limit_bytes=16 << 20),
    )(in_hbm(images), chip[0], *parts, emb, lines)
    summed = jnp.sum(exchanged(share.reshape(16, -1, feats), PLANE).astype(f32), axis=0)
    weight_grad = summed + shifted(summed, "tw", 1)
    return (pair_loss, weight_grad)


def solution(mesh):
    finer = Mesh(mesh.devices.reshape(4, 4, 4, 2, mesh.shape["tower"]), AXES)
    return jax.shard_map(
        local,
        mesh=finer,
        in_specs=(
            P(FSDP_TOWER, None),
            P(PLANE, ("zh", "core")),
            P(("y", "x", "zh", "core", "tw"), None),
            P(FSDP_TOWER),
            P(FSDP_TOWER),
        ),
        out_specs=(P(FSDP_TOWER), P(PLANE, ("zh", "core"))),
        check_vma=False,
    )
```

time: 185 us -> 168 us (0.908)
  blocking collectives: 71.6 us -> 25 us
  starting transfers between devices: 37.6 us -> 63.3 us
  waiting for transfers between devices: 32.9 us -> 42.5 us
  local copies, waits for them, and re-layouts: 6.62 us -> 3.49 us
  Pallas kernels: 33.1 us -> 30.5 us
    all_to_all x3 -> x1, blocking collectives: 71.6 us -> 25 us  [exchanged(): return lax.all_to_all(x, axis, 0, 0, tiled=True)]
    ppermute x22 -> x35, starting transfers between devices: 22.4 us -> 55.7 us  [shifted(): return lax.ppermute(x, axis, [(i, (i + step) % n) for i in range(n)])]
    ppermute x22 -> x35, waiting for transfers between devices: 32.9 us -> 42.5 us  [shifted(): return lax.ppermute(x, axis, [(i, (i + step) % n) for i in range(n)])]
    all_to_all x2 -> x1, starting transfers between devices: 15.2 us -> 7.62 us  [exchanged(): return lax.all_to_all(x, axis, 0, 0, tiled=True)]
    pallas_call x1, Pallas kernels: 5.86 us -> 3.52 us  [local(): pl.pallas_call(weight_kernel, name='weight', out_shape=jax.ShapeDtypeStru...]
    unnamed x51 -> x37, local copies, waits for them, and re-layouts: 4.88 us -> 2.84 us
    pallas_call x4 -> x5, Pallas kernels: 17.4 us -> 15.7 us  [the longest x1 9.81 us: local(): pl.pallas_call(lambda *refs: near_kernel(n, group, *refs), name='near', o...]
  transfers between devices with their start and end apart: 24 -> 36, of which waited for: 9 -> 12; matrix products, arithmetic and copies ran while one was open for 0% -> 0% of each run, Pallas kernels for 9% -> 12%
where the time goes in v3:
time: 168 us; the launch traced here: 167 us
  starting transfers between devices  63.3 us (38%)
  waiting for transfers between devices  42.5 us (25%)
  Pallas kernels  30.5 us (18%)
  blocking collectives  25 us (15%)
  local copies, waits for them, and re-layouts  3.49 us (2%)
    ppermute x35, starting transfers between devices, shifted(): return lax.ppermute(x, axis, [(i, (i + step) % n) for i in range(n)])  55.7 us
    ppermute x35, waiting for transfers between devices, shifted(): return lax.ppermute(x, axis, [(i, (i + step) % n) for i in range(n)])  42.5 us
    all_to_all x1, blocking collectives, exchanged(): return lax.all_to_all(x, axis, 0, 0, tiled=True)  25 us
    pallas_call x1, Pallas kernels, local(): pl.pallas_call(lambda *refs: near_kernel(n, group, *refs), name='near', o...  9.81 us
    all_to_all x1, starting transfers between devices, exchanged(): return lax.all_to_all(x, axis, 0, 0, tiled=True)  7.62 us
    pallas_call x1, Pallas kernels, local(): pl.pallas_call(lambda *refs: far_gradient_kernel(m, group, *refs), name='...  4.84 us
    pallas_call x1, Pallas kernels, local(): pl.pallas_call(embed_kernel, name='embed', out_shape=pltpu.HBM((rows, fea...  3.98 us
    pallas_call x1, Pallas kernels, local(): pl.pallas_call(lambda *refs: far_score_kernel(m, group, *refs), name='far...  3.77 us
  transfers between devices with their start and end apart: 36, of which 12 were waited for; matrix products, arithmetic and copies ran while one was open for 0% of the time, Pallas kernels for 12%

profile of v3, /device:TPU:2, one launch (start us, length us, event | category | flops | bytes accessed | tf_op | source)
XLA Modules:
  0.0 166.9 jit_solution(518030148766011112)
XLA Ops:
  0.6 0.9 copy-done.1
  1.5 1.2 spread.1
  2.8 0.0 copy-start.9
  2.8 7.6 %all-to-all-start = ((bf16[16,320,128]{2,1,0:T(8,128)(2,1)}), bf16[16,320,128]{2,1,0:T(8,128)(2,1)S(1)}, u32[]{:S(2)}, u32[]{:S(2)}) async-start(bf16[16,320,128]{2,1,0:T(8,128)(2,1)} %spread.1), calls=%async_computation | async-start | bytes 2621440 | tf_op jit(solution)/shard_map/all_to_all | solution.py:35
  10.4 2.0 %collective-permute-start.14 = (bf16[64,1024]{1,0:T(8,128)(2,1)S(1)}, bf16[64,1024]{1,0:T(8,128)(2,1)S(1)}, u32[]{:S(2)}, u32[]{:S(2)}) collective-permute-start(bf16[64,1024]{1,0:T(8,128)(2,1)S(1)} %copy-done.9), channel_id=1, source_target_pairs={{0,1},{1,0},{2,3},{3,2},{4,5},{5,4},{6,7},{7,6},{8,9},{9,8},{10,11... | collective-permute-start | bytes 393224 | tf_op jit(solution)/shard_map/ppermute | solution.py:27
  12.4 0.1 collective-permute-start.10
  12.5 2.8 %collective-permute-start.11 = (bf16[64,1024]{1,0:T(8,128)(2,1)S(1)}, bf16[64,1024]{1,0:T(8,128)(2,1)S(1)}, u32[]{:S(2)}, u32[]{:S(2)}) collective-permute-start(bf16[64,1024]{1,0:T(8,128)(2,1)S(1)} %copy-done.9), channel_id=1, source_target_pairs={{0,32},{16,48},{32,0},{48,16},{1,33},{17,49},{33,1},{49,17},{2,34}... | collective-permute-start | bytes 393224 | tf_op jit(solution)/shard_map/ppermute | solution.py:27
  15.3 1.8 %collective-permute-start.7 = (bf16[64,1024]{1,0:T(8,128)(2,1)S(1)}, bf16[64,1024]{1,0:T(8,128)(2,1)S(1)}, u32[]{:S(2)}, u32[]{:S(2)}) collective-permute-start(bf16[64,1024]{1,0:T(8,128)(2,1)S(1)} %copy-done.9), channel_id=1, source_target_pairs={{0,16},{16,32},{32,48},{48,0},{1,17},{17,33},{33,49},{49,1},{2,18}... | collective-permute-start | bytes 393224 | tf_op jit(solution)/shard_map/ppermute | solution.py:27
  17.1 0.0 collective-permute-done.14.in_ref
  17.2 2.8 %collective-permute-start.18 = (bf16[64,1024]{1,0:T(8,128)(2,1)S(1)}, bf16[64,1024]{1,0:T(8,128)(2,1)S(1)}, u32[]{:S(2)}, u32[]{:S(2)}) collective-permute-start(bf16[64,1024]{1,0:T(8,128)(2,1)S(1)} %gate.1), channel_id=1, source_target_pairs={{0,192},{64,0},{128,64},{192,128},{1,193},{65,1},{129,65},{193,129... | collective-permute-start | bytes 393224 | tf_op jit(solution)/shard_map/ppermute | solution.py:27
  19.9 0.9 collective-permute-start.19
  20.8 9.9 %collective-permute-done.10 = bf16[64,1024]{1,0:T(8,128)(2,1)S(1)} collective-permute-done((bf16[64,1024]{1,0:T(8,128)(2,1)S(1)}, bf16[64,1024]{1,0:T(8,128)(2,1)S(1)}, u32[]{:S(2)}, u32[]{:S(2)}) %collective-permute-start.10) | collective-permute-done | bytes 131104 | tf_op jit(solution)/shard_map/ppermute | solution.py:27
  30.7 1.8 %collective-permute-start.15 = (bf16[64,1024]{1,0:T(8,128)(2,1)S(1)}, bf16[64,1024]{1,0:T(8,128)(2,1)S(1)}, u32[]{:S(2)}, u32[]{:S(2)}) collective-permute-start(bf16[64,1024]{1,0:T(8,128)(2,1)S(1)} %gate.1), channel_id=1, source_target_pairs={{0,64},{64,128},{128,192},{192,0},{1,65},{65,129},{129,193},{193,1... | collective-permute-start | bytes 393224 | tf_op jit(solution)/shard_map/ppermute | solution.py:27
  32.5 0.0 collective-permute-done.11
  32.5 2.7 %collective-permute-start.13 = (bf16[128,1024]{1,0:T(8,128)(2,1)S(1)}, bf16[128,1024]{1,0:T(8,128)(2,1)S(1)}, u32[]{:S(2)}, u32[]{:S(2)}) collective-permute-start(bf16[128,1024]{1,0:T(8,128)(2,1)S(1)} %constant_dynamic-update-slice_fusion.2.refs_12_), channel_id=1, source_target_pairs={{0,192},{64,0},{128,64},{192,128},{1,193},{65,1},{129,65},{193,129... | collective-permute-start | bytes 786440 | tf_op jit(solution)/shard_map/ppermute | solution.py:27
  35.3 0.0 collective-permute-done.18
  35.3 0.9 collective-permute-start.8
  36.2 2.5 %collective-permute-start.9 = (bf16[128,1024]{1,0:T(8,128)(2,1)S(1)}, bf16[128,1024]{1,0:T(8,128)(2,1)}, u32[]{:S(2)}, u32[]{:S(2)}) collective-permute-start(bf16[128,1024]{1,0:T(8,128)(2,1)S(1)} %constant_dynamic-update-slice_fusion.refs_9_), channel_id=1, source_target_pairs={{0,192},{64,0},{128,64},{192,128},{1,193},{65,1},{129,65},{193,129... | collective-permute-start | bytes 786440 | tf_op jit(solution)/shard_map/ppermute | solution.py:27
  38.8 0.5 collective-permute-start.21
  39.3 2.7 %collective-permute-done.13.refs_14_ = bf16[128,1024]{1,0:T(8,128)(2,1)S(1)} collective-permute-done((bf16[128,1024]{1,0:T(8,128)(2,1)S(1)}, bf16[128,1024]{1,0:T(8,128)(2,1)S(1)}, u32[]{:S(2)}, u32[]{:S(2)}) %collective-permute-start.13) | collective-permute-done | bytes 262176 | tf_op jit(solution)/shard_map/ppermute | solution.py:27
  42.0 6.8 %collective-permute-done.8.refs_10_ = bf16[128,1024]{1,0:T(8,128)(2,1)S(1)} collective-permute-done((bf16[128,1024]{1,0:T(8,128)(2,1)S(1)}, bf16[128,1024]{1,0:T(8,128)(2,1)S(1)}, u32[]{:S(2)}, u32[]{:S(2)}) %collective-permute-start.8) | collective-permute-done | bytes 262176 | tf_op jit(solution)/shard_map/ppermute | solution.py:27
  48.8 0.2 collective-permute-start.20
  49.0 1.8 %collective-permute-start.17 = (bf16[128,1024]{1,0:T(8,128)(2,1)S(1)}, bf16[128,1024]{1,0:T(8,128)(2,1)}, u32[]{:S(2)}, u32[]{:S(2)}) collective-permute-start(bf16[128,1024]{1,0:T(8,128)(2,1)S(1)} %pad_maximum_fusion.refs_15_), channel_id=1, source_target_pairs={{0,48},{16,0},{32,16},{48,32},{1,49},{17,1},{33,17},{49,33},{2,50}... | collective-permute-start | bytes 786440 | tf_op jit(solution)/shard_map/ppermute | solution.py:27
  50.8 4.0 %embed.1.refs_0_.emb_ref = bf16[512,128]{1,0:T(8,128)(2,1)} custom-call(bf16[512,5120]{1,0:T(8,128)(2,1)} %images_ref.3, bf16[5120,128]{1,0:T(8,128)(2,1)S(1)} %bitcast.13), custom_call_target="tpu_custom_call" | custom-call | flops 671088640 | bytes 7340032 | tf_op jit(solution)/shard_map/embed/pallas_call | solution.py:423
  54.9 3.5 %collective-permute-start = (bf16[512,128]{1,0:T(8,128)(2,1)}, bf16[512,128]{1,0:T(8,128)(2,1)S(1)}, u32[]{:S(2)}, u32[]{:S(2)}) collective-permute-start(bf16[512,128]{1,0:T(8,128)(2,1)} %embed.1.refs_0_.emb_ref), channel_id=1, source_target_pairs={{0,4},{4,8},{8,12},{12,0},{1,5},{5,9},{9,13},{13,1},{2,6},{6,10},{... | collective-permute-start | bytes 393224 | tf_op jit(solution)/shard_map/ppermute | solution.py:27
  58.4 3.1 %collective-permute-start.1 = (bf16[512,128]{1,0:T(8,128)(2,1)}, bf16[512,128]{1,0:T(8,128)(2,1)S(1)}, u32[]{:S(2)}, u32[]{:S(2)}) collective-permute-start(bf16[512,128]{1,0:T(8,128)(2,1)} %embed.1.refs_0_.emb_ref), channel_id=1, source_target_pairs={{0,12},{4,0},{8,4},{12,8},{1,13},{5,1},{9,5},{13,9},{2,14},{6,2},{... | collective-permute-start | bytes 393224 | tf_op jit(solution)/shard_map/ppermute | solution.py:27
  61.6 4.9 %collective-permute-start.2 = (bf16[512,128]{1,0:T(8,128)(2,1)}, bf16[512,128]{1,0:T(8,128)(2,1)S(1)}, u32[]{:S(2)}, u32[]{:S(2)}) collective-permute-start(bf16[512,128]{1,0:T(8,128)(2,1)} %embed.1.refs_0_.emb_ref), channel_id=1, source_target_pairs={{0,8},{4,12},{8,0},{12,4},{1,9},{5,13},{9,1},{13,5},{2,10},{6,14},... | collective-permute-start | bytes 393224 | tf_op jit(solution)/shard_map/ppermute | solution.py:27
  66.5 2.2 %collective-permute-done.refs_1_ = bf16[512,128]{1,0:T(8,128)(2,1)S(1)} collective-permute-done((bf16[512,128]{1,0:T(8,128)(2,1)}, bf16[512,128]{1,0:T(8,128)(2,1)S(1)}, u32[]{:S(2)}, u32[]{:S(2)}) %collective-permute-start) | collective-permute-done | bytes 131104 | tf_op jit(solution)/shard_map/ppermute | solution.py:27
  68.6 0.8 collective-permute-done.1.refs_2_
  69.5 1.9 %collective-permute-done.2.refs_3_ = bf16[512,128]{1,0:T(8,128)(2,1)S(1)} collective-permute-done((bf16[512,128]{1,0:T(8,128)(2,1)}, bf16[512,128]{1,0:T(8,128)(2,1)S(1)}, u32[]{:S(2)}, u32[]{:S(2)}) %collective-permute-start.2) | collective-permute-done | bytes 131104 | tf_op jit(solution)/shard_map/ppermute | solution.py:27
  71.3 0.1 places.1.refs_8_.refs_1_.refs_0_
  71.5 0.6 signs.1.refs_3_
  72.1 2.6 %collective-permute-start.23 = (bf16[128,1024]{1,0:T(8,128)(2,1)S(1)}, bf16[128,1024]{1,0:T(8,128)(2,1)S(1)}, u32[]{:S(2)}, u32[]{:S(2)}) collective-permute-start(bf16[128,1024]{1,0:T(8,128)(2,1)S(1)} %collective-permute-done.13.refs_14_), channel_id=1, source_target_pairs={{0,192},{64,0},{128,64},{192,128},{1,193},{65,1},{129,65},{193,129... | collective-permute-start | bytes 786440 | tf_op jit(solution)/shard_map/ppermute | solution.py:27
  74.7 2.2 %collective-permute-start.25 = (bf16[128,1024]{1,0:T(8,128)(2,1)S(1)}, bf16[128,1024]{1,0:T(8,128)(2,1)S(1)}, u32[]{:S(2)}, u32[]{:S(2)}) collective-permute-start(bf16[128,1024]{1,0:T(8,128)(2,1)S(1)} %collective-permute-done.21.refs_20_), channel_id=1, source_target_pairs={{0,48},{16,0},{32,16},{48,32},{1,49},{17,1},{33,17},{49,33},{2,50}... | collective-permute-start | bytes 786440 | tf_op jit(solution)/shard_map/ppermute | solution.py:27
  77.0 0.0 copy-start
  77.0 0.9 copy-done
  77.9 9.8 %near.1 = (f32[512,1024]{1,0:T(8,128)}, bf16[512,1024]{1,0:T(8,128)(2,1)}, f32[8,512]{1,0:T(8,128)S(1)}, bf16[512,1024]{1,0:T(8,128)(2,1)S(1)}) custom-call(bf16[512,128]{1,0:T(8,128)(2,1)S(1)} %copy-done, bf16[512,128]{1,0:T(8,128)(2,1)S(1)} %collective-permute-done.refs_1_, bf16[512,128]{1,0:T(8,128)(2,1)S(1)} %collective-permute-done.1.refs_2_, ...), custom_call_target="tpu_custom_call" | custom-call | flops 4831838208 | bytes 6291456 | tf_op jit(solution)/shard_map/near/pallas_call | solution.py:451
  87.8 0.6 copy-done.4
  88.4 0.1 copy-done.5
  88.5 0.1 copy-done.6
  88.7 0.1 copy-done.7
  88.8 3.8 %far_scores.1 = (bf16[512,512]{1,0:T(8,128)(2,1)}, f32[8,512]{1,0:T(8,128)}, f32[8,512]{1,0:T(8,128)S(1)}) custom-call(bf16[512,1024]{1,0:T(8,128)(2,1)S(1)} %get-tuple-element.14.refs_0_, s32[512,1]{1,0:T(8,128)S(1)} %places.1.refs_8_.refs_1_.refs_0_, f32[8,512]{1,0:T(8,128)S(1)} %get-tuple-element.15.refs_2_, f32[1,512]{1,0:T(1,128)} %signs.1.refs_3_, ...), custom_call_target="tpu_custom_call" | custom-call | flops 536870912 | bytes 2097152 | tf_op jit(solution)/shard_map/far_scores/pallas_call | solution.py:474
  92.6 0.1 collective-permute-start.26
  92.7 1.2 collective-permute-done.26.theirs_ref
  93.9 4.3 %collective-permute-start.27 = (f32[8,512]{1,0:T(8,128)S(1)}, f32[8,512]{1,0:T(8,128)S(1)}, u32[]{:S(2)}, u32[]{:S(2)}) collective-permute-start(f32[8,512]{1,0:T(8,128)S(1)} %pair.1.refs_0_), channel_id=1, source_target_pairs={{0,4},{4,8},{8,12},{12,0},{1,5},{5,9},{9,13},{13,1},{2,6},{6,10},{... | collective-permute-start | bytes 49160 | tf_op jit(solution)/shard_map/ppermute | solution.py:27
  98.2 4.4 %collective-permute-start.29 = (f32[8,512]{1,0:T(8,128)S(1)}, f32[8,512]{1,0:T(8,128)S(1)}, u32[]{:S(2)}, u32[]{:S(2)}) collective-permute-start(f32[8,512]{1,0:T(8,128)S(1)} %pair.1.refs_0_), channel_id=1, source_target_pairs={{0,8},{4,12},{8,0},{12,4},{1,9},{5,13},{9,1},{13,5},{2,10},{6,14},... | collective-permute-start | bytes 49160 | tf_op jit(solution)/shard_map/ppermute | solution.py:27
  102.6 4.8 %far_gradient.1 = (f32[512,1024]{1,0:T(8,128)}, bf16[512,1024]{1,0:T(8,128)(2,1)}) custom-call(s32[512,1]{1,0:T(8,128)S(1)} %places.1.refs_8_.refs_1_.refs_0_, bf16[512,512]{1,0:T(8,128)(2,1)} %get-tuple-element.18.refs_1_, f32[8,512]{1,0:T(8,128)} %get-tuple-element.17.refs_2_.refs_4_, f32[512,1024]{1,0:T(8,128)} %get-tuple-element.19.refs_3_, ...), custom_call_target="tpu_custom_call" | custom-call | flops 1073741824 | bytes 2097152 | tf_op jit(solution)/shard_map/far_gradient/pallas_call | solution.py:508
  107.5 2.6 %combine.1 = (f32[4,512,128]{2,1,0:T(8,128)S(1)}, f32[4,512,128]{2,1,0:T(8,128)S(1)}, f32[8,512]{1,0:T(8,128)S(1)}) custom-call(f32[8,512]{1,0:T(8,128)S(1)} %pair.1.refs_0_, f32[8,512]{1,0:T(8,128)S(1)} %collective-permute-done.27.refs_1_, f32[8,512]{1,0:T(8,128)S(1)} %collective-permute-done.28.refs_2_, f32[8,512]{1,0:T(8,128)S(1)} %collective-permute-done.29.refs_3_, ...), custom_call_target="tpu_custom_call" | custom-call | tf_op jit(solution)/shard_map/combine/pallas_call | solution.py:529
  110.1 0.1 collective-permute-start.30
  110.2 2.6 %collective-permute-done.30 = f32[4,512,128]{2,1,0:T(8,128)S(1)} collective-permute-done((f32[4,512,128]{2,1,0:T(8,128)S(1)}, f32[4,512,128]{2,1,0:T(8,128)S(1)}, u32[]{:S(2)}, u32[]{:S(2)}) %collective-permute-start.30) | collective-permute-done | bytes 1048608 | tf_op jit(solution)/shard_map/ppermute | solution.py:27
  112.9 0.1 fusion
  113.1 1.3 collective-permute-start.31
  114.4 2.9 %collective-permute-start.32 = (bf16[512,128]{1,0:T(8,128)(2,1)S(1)}, bf16[512,128]{1,0:T(8,128)(2,1)S(1)}, u32[]{:S(2)}, u32[]{:S(2)}) collective-permute-start(bf16[512,128]{1,0:T(8,128)(2,1)S(1)} %get-tuple-element.29), channel_id=1, source_target_pairs={{0,12},{4,0},{8,4},{12,8},{1,13},{5,1},{9,5},{13,9},{2,14},{6,2},{... | collective-permute-start | bytes 393224 | tf_op jit(solution)/shard_map/ppermute | solution.py:27
  117.3 2.8 %collective-permute-start.33 = (bf16[512,128]{1,0:T(8,128)(2,1)S(1)}, bf16[512,128]{1,0:T(8,128)(2,1)S(1)}, u32[]{:S(2)}, u32[]{:S(2)}) collective-permute-start(bf16[512,128]{1,0:T(8,128)(2,1)S(1)} %get-tuple-element.28), channel_id=1, source_target_pairs={{0,8},{4,12},{8,0},{12,4},{1,9},{5,13},{9,1},{13,5},{2,10},{6,14},... | collective-permute-start | bytes 393224 | tf_op jit(solution)/shard_map/ppermute | solution.py:27
  120.1 1.2 collective-permute-done.31.one_ref
  121.3 0.6 collective-permute-done.32.two_ref
  121.9 9.7 %collective-permute-done.33.three_ref = bf16[512,128]{1,0:T(8,128)(2,1)S(1)} collective-permute-done((bf16[512,128]{1,0:T(8,128)(2,1)S(1)}, bf16[512,128]{1,0:T(8,128)(2,1)S(1)}, u32[]{:S(2)}, u32[]{:S(2)}) %collective-permute-start.33) | collective-permute-done | bytes 131104 | tf_op jit(solution)/shard_map/ppermute | solution.py:27
  131.7 3.5 %weight.1 = bf16[5120,128]{1,0:T(8,128)(2,1)S(1)} custom-call(bf16[512,5120]{1,0:T(8,128)(2,1)} %images_ref.3, f32[512,128]{1,0:T(8,128)S(1)} %slice_bitcast_fusion.own_ref, bf16[512,128]{1,0:T(8,128)(2,1)S(1)} %collective-permute-done.31.one_ref, bf16[512,128]{1,0:T(8,128)(2,1)S(1)} %collective-permute-done.32.two_ref, ...), custom_call_target="tpu_custom_call" | custom-call | tf_op jit(solution)/shard_map/weight/pallas_call | solution.py:552
  135.2 25.0 %all_to_all.10 = bf16[16,320,128]{2,1,0:T(8,128)(2,1)S(1)} all-to-all(bf16[16,320,128]{2,1,0:T(8,128)(2,1)S(1)} %bitcast.14), channel_id=1, replica_groups=mesh['y'=4,'x'=4,'zh'=4,'core'=2,'tw'=2] {'y','x'}, dimensions={0} | all-to-all | bytes 2621440 | tf_op jit(solution)/shard_map/all_to_all | solution.py:35
  160.2 0.2 convert_reduce_fusion
  160.3 2.6 %collective-permute-start.34 = (f32[320,128]{1,0:T(8,128)S(1)}, f32[320,128]{1,0:T(8,128)S(1)}, u32[]{:S(2)}, u32[]{:S(2)}) collective-permute-start(f32[320,128]{1,0:T(8,128)S(1)} %convert_reduce_fusion), channel_id=1, source_target_pairs={{0,1},{1,0},{2,3},{3,2},{4,5},{5,4},{6,7},{7,6},{8,9},{9,8},{10,11... | collective-permute-start | bytes 491528 | tf_op jit(solution)/shard_map/ppermute | solution.py:27
  162.9 0.6 slice.18
  163.5 2.7 %collective-permute-done.34 = f32[320,128]{1,0:T(8,128)S(1)} collective-permute-done((f32[320,128]{1,0:T(8,128)S(1)}, f32[320,128]{1,0:T(8,128)S(1)}, u32[]{:S(2)}, u32[]{:S(2)}) %collective-permute-start.34) | collective-permute-done | bytes 163872 | tf_op jit(solution)/shard_map/ppermute | solution.py:27
  166.2 0.7 add.7
  (67 shorter events, 0.3 us)
Async XLA Ops:
  0.6 0.9 copy-start.1
  2.8 7.6 %copy-start.9 = (bf16[64,1024]{1,0:T(8,128)(2,1)S(1)}, bf16[64,1024]{1,0:T(8,128)(2,1)}, u32[]{:S(2)}) copy-start(bf16[64,1024]{1,0:T(8,128)(2,1)} %param.7) | copy-start | bytes 393220
  2.8 48.0 %all-to-all-start = ((bf16[16,320,128]{2,1,0:T(8,128)(2,1)}), bf16[16,320,128]{2,1,0:T(8,128)(2,1)S(1)}, u32[]{:S(2)}, u32[]{:S(2)}) async-start(bf16[16,320,128]{2,1,0:T(8,128)(2,1)} %spread.1), calls=%async_computation | async-start | bytes 2621440 | tf_op jit(solution)/shard_map/all_to_all | solution.py:35
  10.4 6.7 %collective-permute-start.14 = (bf16[64,1024]{1,0:T(8,128)(2,1)S(1)}, bf16[64,1024]{1,0:T(8,128)(2,1)S(1)}, u32[]{:S(2)}, u32[]{:S(2)}) collective-permute-start(bf16[64,1024]{1,0:T(8,128)(2,1)S(1)} %copy-done.9), channel_id=1, source_target_pairs={{0,1},{1,0},{2,3},{3,2},{4,5},{5,4},{6,7},{7,6},{8,9},{9,8},{10,11... | collective-permute-start | bytes 393224 | tf_op jit(solution)/shard_map/ppermute | solution.py:27
  12.4 18.3 %collective-permute-start.10 = (bf16[64,1024]{1,0:T(8,128)(2,1)S(1)}, bf16[64,1024]{1,0:T(8,128)(2,1)S(1)}, u32[]{:S(2)}, u32[]{:S(2)}) collective-permute-start(bf16[64,1024]{1,0:T(8,128)(2,1)S(1)} %copy-done.9), channel_id=1, source_target_pairs={{0,48},{16,0},{32,16},{48,32},{1,49},{17,1},{33,17},{49,33},{2,50}... | collective-permute-start | bytes 393224 | tf_op jit(solution)/shard_map/ppermute | solution.py:27
  12.5 20.0 %collective-permute-start.11 = (bf16[64,1024]{1,0:T(8,128)(2,1)S(1)}, bf16[64,1024]{1,0:T(8,128)(2,1)S(1)}, u32[]{:S(2)}, u32[]{:S(2)}) collective-permute-start(bf16[64,1024]{1,0:T(8,128)(2,1)S(1)} %copy-done.9), channel_id=1, source_target_pairs={{0,32},{16,48},{32,0},{48,16},{1,33},{17,49},{33,1},{49,17},{2,34}... | collective-permute-start | bytes 393224 | tf_op jit(solution)/shard_map/ppermute | solution.py:27
  15.3 19.9 %collective-permute-start.7 = (bf16[64,1024]{1,0:T(8,128)(2,1)S(1)}, bf16[64,1024]{1,0:T(8,128)(2,1)S(1)}, u32[]{:S(2)}, u32[]{:S(2)}) collective-permute-start(bf16[64,1024]{1,0:T(8,128)(2,1)S(1)} %copy-done.9), channel_id=1, source_target_pairs={{0,16},{16,32},{32,48},{48,0},{1,17},{17,33},{33,49},{49,1},{2,18}... | collective-permute-start | bytes 393224 | tf_op jit(solution)/shard_map/ppermute | solution.py:27
  17.2 18.2 %collective-permute-start.18 = (bf16[64,1024]{1,0:T(8,128)(2,1)S(1)}, bf16[64,1024]{1,0:T(8,128)(2,1)S(1)}, u32[]{:S(2)}, u32[]{:S(2)}) collective-permute-start(bf16[64,1024]{1,0:T(8,128)(2,1)S(1)} %gate.1), channel_id=1, source_target_pairs={{0,192},{64,0},{128,64},{192,128},{1,193},{65,1},{129,65},{193,129... | collective-permute-start | bytes 393224 | tf_op jit(solution)/shard_map/ppermute | solution.py:27
  19.9 16.3 %collective-permute-start.19 = (bf16[64,1024]{1,0:T(8,128)(2,1)S(1)}, bf16[64,1024]{1,0:T(8,128)(2,1)S(1)}, u32[]{:S(2)}, u32[]{:S(2)}) collective-permute-start(bf16[64,1024]{1,0:T(8,128)(2,1)S(1)} %gate.1), channel_id=1, source_target_pairs={{0,128},{64,192},{128,0},{192,64},{1,129},{65,193},{129,1},{193,65... | collective-permute-start | bytes 393224 | tf_op jit(solution)/shard_map/ppermute | solution.py:27
  30.7 8.1 %collective-permute-start.15 = (bf16[64,1024]{1,0:T(8,128)(2,1)S(1)}, bf16[64,1024]{1,0:T(8,128)(2,1)S(1)}, u32[]{:S(2)}, u32[]{:S(2)}) collective-permute-start(bf16[64,1024]{1,0:T(8,128)(2,1)S(1)} %gate.1), channel_id=1, source_target_pairs={{0,64},{64,128},{128,192},{192,0},{1,65},{65,129},{129,193},{193,1... | collective-permute-start | bytes 393224 | tf_op jit(solution)/shard_map/ppermute | solution.py:27
  32.5 22.3 %copy-start.12 = (bf16[128,1024]{1,0:T(8,128)(2,1)}, bf16[128,1024]{1,0:T(8,128)(2,1)S(1)}, u32[]{:S(2)}) copy-start(bf16[128,1024]{1,0:T(8,128)(2,1)S(1)} %constant_dynamic-update-slice_fusion.2.refs_12_) | copy-start | bytes 786436
  32.5 9.4 %collective-permute-start.13 = (bf16[128,1024]{1,0:T(8,128)(2,1)S(1)}, bf16[128,1024]{1,0:T(8,128)(2,1)S(1)}, u32[]{:S(2)}, u32[]{:S(2)}) collective-permute-start(bf16[128,1024]{1,0:T(8,128)(2,1)S(1)} %constant_dynamic-update-slice_fusion.2.refs_12_), channel_id=1, source_target_pairs={{0,192},{64,0},{128,64},{192,128},{1,193},{65,1},{129,65},{193,129... | collective-permute-start | bytes 786440 | tf_op jit(solution)/shard_map/ppermute | solution.py:27
  35.3 13.8 %collective-permute-start.12 = (bf16[128,1024]{1,0:T(8,128)(2,1)S(1)}, bf16[128,1024]{1,0:T(8,128)(2,1)S(1)}, u32[]{:S(2)}, u32[]{:S(2)}) collective-permute-start(bf16[128,1024]{1,0:T(8,128)(2,1)S(1)} %constant_dynamic-update-slice_fusion.2.refs_12_), channel_id=1, source_target_pairs={{0,64},{64,128},{128,192},{192,0},{1,65},{65,129},{129,193},{193,1... | collective-permute-start | bytes 786440 | tf_op jit(solution)/shard_map/ppermute | solution.py:27
  35.3 19.5 %copy-start.10 = (bf16[128,1024]{1,0:T(8,128)(2,1)}, bf16[128,1024]{1,0:T(8,128)(2,1)S(1)}, u32[]{:S(2)}) copy-start(bf16[128,1024]{1,0:T(8,128)(2,1)S(1)} %constant_dynamic-update-slice_fusion.refs_9_) | copy-start | bytes 786436
  35.3 13.5 %collective-permute-start.8 = (bf16[128,1024]{1,0:T(8,128)(2,1)S(1)}, bf16[128,1024]{1,0:T(8,128)(2,1)S(1)}, u32[]{:S(2)}, u32[]{:S(2)}) collective-permute-start(bf16[128,1024]{1,0:T(8,128)(2,1)S(1)} %constant_dynamic-update-slice_fusion.refs_9_), channel_id=1, source_target_pairs={{0,64},{64,128},{128,192},{192,0},{1,65},{65,129},{129,193},{193,1... | collective-permute-start | bytes 786440 | tf_op jit(solution)/shard_map/ppermute | solution.py:27
  36.2 18.6 %collective-permute-start.9 = (bf16[128,1024]{1,0:T(8,128)(2,1)S(1)}, bf16[128,1024]{1,0:T(8,128)(2,1)}, u32[]{:S(2)}, u32[]{:S(2)}) collective-permute-start(bf16[128,1024]{1,0:T(8,128)(2,1)S(1)} %constant_dynamic-update-slice_fusion.refs_9_), channel_id=1, source_target_pairs={{0,192},{64,0},{128,64},{192,128},{1,193},{65,1},{129,65},{193,129... | collective-permute-start | bytes 786440 | tf_op jit(solution)/shard_map/ppermute | solution.py:27
  38.8 16.1 %copy-start.11 = (bf16[128,1024]{1,0:T(8,128)(2,1)}, bf16[128,1024]{1,0:T(8,128)(2,1)S(1)}, u32[]{:S(2)}) copy-start(bf16[128,1024]{1,0:T(8,128)(2,1)S(1)} %constant_dynamic-update-slice_fusion.4.refs_18_) | copy-start | bytes 786436
  38.8 19.6 %collective-permute-start.21 = (bf16[128,1024]{1,0:T(8,128)(2,1)S(1)}, bf16[128,1024]{1,0:T(8,128)(2,1)S(1)}, u32[]{:S(2)}, u32[]{:S(2)}) collective-permute-start(bf16[128,1024]{1,0:T(8,128)(2,1)S(1)} %constant_dynamic-update-slice_fusion.4.refs_18_), channel_id=1, source_target_pairs={{0,48},{16,0},{32,16},{48,32},{1,49},{17,1},{33,17},{49,33},{2,50}... | collective-permute-start | bytes 786440 | tf_op jit(solution)/shard_map/ppermute | solution.py:27
  39.3 15.6 %copy-start.8 = (bf16[128,1024]{1,0:T(8,128)(2,1)}, bf16[128,1024]{1,0:T(8,128)(2,1)S(1)}, u32[]{:S(2)}) copy-start(bf16[128,1024]{1,0:T(8,128)(2,1)S(1)} %pad_maximum_fusion.refs_15_) | copy-start | bytes 786436
  42.0 30.1 %copy-start.13 = (bf16[128,1024]{1,0:T(8,128)(2,1)}, bf16[128,1024]{1,0:T(8,128)(2,1)S(1)}, u32[]{:S(2)}) copy-start(bf16[128,1024]{1,0:T(8,128)(2,1)S(1)} %collective-permute-done.13.refs_14_) | copy-start | bytes 786436
  42.0 19.6 %collective-permute-start.16 = (bf16[128,1024]{1,0:T(8,128)(2,1)S(1)}, bf16[128,1024]{1,0:T(8,128)(2,1)}, u32[]{:S(2)}, u32[]{:S(2)}) collective-permute-start(bf16[128,1024]{1,0:T(8,128)(2,1)S(1)} %pad_maximum_fusion.refs_15_), channel_id=1, source_target_pairs={{0,16},{16,32},{32,48},{48,0},{1,17},{17,33},{33,49},{49,1},{2,18}... | collective-permute-start | bytes 786440 | tf_op jit(solution)/shard_map/ppermute | solution.py:27
  48.8 25.9 %copy-start.14 = (bf16[128,1024]{1,0:T(8,128)(2,1)}, bf16[128,1024]{1,0:T(8,128)(2,1)S(1)}, u32[]{:S(2)}) copy-start(bf16[128,1024]{1,0:T(8,128)(2,1)S(1)} %collective-permute-done.8.refs_10_) | copy-start | bytes 786436
  48.8 17.7 %collective-permute-start.20 = (bf16[128,1024]{1,0:T(8,128)(2,1)S(1)}, bf16[128,1024]{1,0:T(8,128)(2,1)}, u32[]{:S(2)}, u32[]{:S(2)}) collective-permute-start(bf16[128,1024]{1,0:T(8,128)(2,1)S(1)} %constant_dynamic-update-slice_fusion.4.refs_18_), channel_id=1, source_target_pairs={{0,16},{16,32},{32,48},{48,0},{1,17},{17,33},{33,49},{49,1},{2,18}... | collective-permute-start | bytes 786440 | tf_op jit(solution)/shard_map/ppermute | solution.py:27
  49.0 5.8 %copy-start.15 = (bf16[128,1024]{1,0:T(8,128)(2,1)}, bf16[128,1024]{1,0:T(8,128)(2,1)S(1)}, u32[]{:S(2)}) copy-start(bf16[128,1024]{1,0:T(8,128)(2,1)S(1)} %collective-permute-done.12.refs_13_) | copy-start | bytes 786436
  49.0 23.0 %collective-permute-start.17 = (bf16[128,1024]{1,0:T(8,128)(2,1)S(1)}, bf16[128,1024]{1,0:T(8,128)(2,1)}, u32[]{:S(2)}, u32[]{:S(2)}) collective-permute-start(bf16[128,1024]{1,0:T(8,128)(2,1)S(1)} %pad_maximum_fusion.refs_15_), channel_id=1, source_target_pairs={{0,48},{16,0},{32,16},{48,32},{1,49},{17,1},{33,17},{49,33},{2,50}... | collective-permute-start | bytes 786440 | tf_op jit(solution)/shard_map/ppermute | solution.py:27
  50.8 20.5 %copy-start.2 = (s32[512]{0:T(512)S(1)}, s32[512]{0:T(512)}, u32[]{:S(2)}) copy-start(s32[512]{0:T(512)} %param.8) | copy-start | bytes 6148
  50.8 20.7 %copy-start.3 = (s32[512]{0:T(512)S(1)}, s32[512]{0:T(512)}, u32[]{:S(2)}) copy-start(s32[512]{0:T(512)} %param.9) | copy-start | bytes 6148
  54.9 13.8 %collective-permute-start = (bf16[512,128]{1,0:T(8,128)(2,1)}, bf16[512,128]{1,0:T(8,128)(2,1)S(1)}, u32[]{:S(2)}, u32[]{:S(2)}) collective-permute-start(bf16[512,128]{1,0:T(8,128)(2,1)} %embed.1.refs_0_.emb_ref), channel_id=1, source_target_pairs={{0,4},{4,8},{8,12},{12,0},{1,5},{5,9},{9,13},{13,1},{2,6},{6,10},{... | collective-permute-start | bytes 393224 | tf_op jit(solution)/shard_map/ppermute | solution.py:27
  58.4 18.6 %copy-start.16 = (bf16[128,1024]{1,0:T(8,128)(2,1)}, bf16[128,1024]{1,0:T(8,128)(2,1)S(1)}, u32[]{:S(2)}) copy-start(bf16[128,1024]{1,0:T(8,128)(2,1)S(1)} %collective-permute-done.21.refs_20_) | copy-start | bytes 786436
  58.4 11.1 %collective-permute-start.1 = (bf16[512,128]{1,0:T(8,128)(2,1)}, bf16[512,128]{1,0:T(8,128)(2,1)S(1)}, u32[]{:S(2)}, u32[]{:S(2)}) collective-permute-start(bf16[512,128]{1,0:T(8,128)(2,1)} %embed.1.refs_0_.emb_ref), channel_id=1, source_target_pairs={{0,12},{4,0},{8,4},{12,8},{1,13},{5,1},{9,5},{13,9},{2,14},{6,2},{... | collective-permute-start | bytes 393224 | tf_op jit(solution)/shard_map/ppermute | solution.py:27
  61.6 9.8 %collective-permute-start.2 = (bf16[512,128]{1,0:T(8,128)(2,1)}, bf16[512,128]{1,0:T(8,128)(2,1)S(1)}, u32[]{:S(2)}, u32[]{:S(2)}) collective-permute-start(bf16[512,128]{1,0:T(8,128)(2,1)} %embed.1.refs_0_.emb_ref), channel_id=1, source_target_pairs={{0,8},{4,12},{8,0},{12,4},{1,9},{5,13},{9,1},{13,5},{2,10},{6,14},... | collective-permute-start | bytes 393224 | tf_op jit(solution)/shard_map/ppermute | solution.py:27
  66.5 8.2 %collective-permute-start.3 = (bf16[512,128]{1,0:T(8,128)(2,1)}, bf16[512,128]{1,0:T(8,128)(2,1)S(1)}, u32[]{:S(2)}, u32[]{:S(2)}) collective-permute-start(bf16[512,128]{1,0:T(8,128)(2,1)} %embed.1.refs_0_.emb_ref), channel_id=1, source_target_pairs={{0,2},{2,0},{1,3},{3,1},{4,6},{6,4},{5,7},{7,5},{8,10},{10,8},{9,1... | collective-permute-start | bytes 393224 | tf_op jit(solution)/shard_map/ppermute | solution.py:27
  68.6 6.1 %collective-permute-start.4 = (bf16[512,128]{1,0:T(8,128)(2,1)S(1)}, bf16[512,128]{1,0:T(8,128)(2,1)S(1)}, u32[]{:S(2)}, u32[]{:S(2)}) collective-permute-start(bf16[512,128]{1,0:T(8,128)(2,1)S(1)} %collective-permute-done.refs_1_), channel_id=1, source_target_pairs={{0,2},{2,0},{1,3},{3,1},{4,6},{6,4},{5,7},{7,5},{8,10},{10,8},{9,1... | collective-permute-start | bytes 393224 | tf_op jit(solution)/shard_map/ppermute | solution.py:27
  69.5 7.5 %collective-permute-start.5 = (bf16[512,128]{1,0:T(8,128)(2,1)S(1)}, bf16[512,128]{1,0:T(8,128)(2,1)S(1)}, u32[]{:S(2)}, u32[]{:S(2)}) collective-permute-start(bf16[512,128]{1,0:T(8,128)(2,1)S(1)} %collective-permute-done.1.refs_2_), channel_id=1, source_target_pairs={{0,2},{2,0},{1,3},{3,1},{4,6},{6,4},{5,7},{7,5},{8,10},{10,8},{9,1... | collective-permute-start | bytes 393224 | tf_op jit(solution)/shard_map/ppermute | solution.py:27
  71.3 5.7 %collective-permute-start.6 = (bf16[512,128]{1,0:T(8,128)(2,1)S(1)}, bf16[512,128]{1,0:T(8,128)(2,1)S(1)}, u32[]{:S(2)}, u32[]{:S(2)}) collective-permute-start(bf16[512,128]{1,0:T(8,128)(2,1)S(1)} %collective-permute-done.2.refs_3_), channel_id=1, source_target_pairs={{0,2},{2,0},{1,3},{3,1},{4,6},{6,4},{5,7},{7,5},{8,10},{10,8},{9,1... | collective-permute-start | bytes 393224 | tf_op jit(solution)/shard_map/ppermute | solution.py:27
  72.1 15.6 %collective-permute-start.23 = (bf16[128,1024]{1,0:T(8,128)(2,1)S(1)}, bf16[128,1024]{1,0:T(8,128)(2,1)S(1)}, u32[]{:S(2)}, u32[]{:S(2)}) collective-permute-start(bf16[128,1024]{1,0:T(8,128)(2,1)S(1)} %collective-permute-done.13.refs_14_), channel_id=1, source_target_pairs={{0,192},{64,0},{128,64},{192,128},{1,193},{65,1},{129,65},{193,129... | collective-permute-start | bytes 786440 | tf_op jit(solution)/shard_map/ppermute | solution.py:27
  74.7 13.0 %collective-permute-start.22 = (bf16[128,1024]{1,0:T(8,128)(2,1)S(1)}, bf16[128,1024]{1,0:T(8,128)(2,1)S(1)}, u32[]{:S(2)}, u32[]{:S(2)}) collective-permute-start(bf16[128,1024]{1,0:T(8,128)(2,1)S(1)} %collective-permute-done.8.refs_10_), channel_id=1, source_target_pairs={{0,64},{64,128},{128,192},{192,0},{1,65},{65,129},{129,193},{193,1... | collective-permute-start | bytes 786440 | tf_op jit(solution)/shard_map/ppermute | solution.py:27
  74.7 13.0 %collective-permute-start.25 = (bf16[128,1024]{1,0:T(8,128)(2,1)S(1)}, bf16[128,1024]{1,0:T(8,128)(2,1)S(1)}, u32[]{:S(2)}, u32[]{:S(2)}) collective-permute-start(bf16[128,1024]{1,0:T(8,128)(2,1)S(1)} %collective-permute-done.21.refs_20_), channel_id=1, source_target_pairs={{0,48},{16,0},{32,16},{48,32},{1,49},{17,1},{33,17},{49,33},{2,50}... | collective-permute-start | bytes 786440 | tf_op jit(solution)/shard_map/ppermute | solution.py:27
  77.0 10.8 %collective-permute-start.24 = (bf16[128,1024]{1,0:T(8,128)(2,1)}, bf16[128,1024]{1,0:T(8,128)(2,1)S(1)}, u32[]{:S(2)}, u32[]{:S(2)}) collective-permute-start(bf16[128,1024]{1,0:T(8,128)(2,1)} %collective-permute-done.16.refs_16_), channel_id=1, source_target_pairs={{0,16},{16,32},{32,48},{48,0},{1,17},{17,33},{33,49},{49,1},{2,18}... | collective-permute-start | bytes 786440 | tf_op jit(solution)/shard_map/ppermute | solution.py:27
  77.0 0.9 copy-start
  87.7 0.7 copy-start.4
  87.8 0.8 copy-start.5
  87.8 0.9 copy-start.6
  87.8 1.0 copy-start.7
  92.6 1.3 collective-permute-start.26
  93.9 13.6 %collective-permute-start.27 = (f32[8,512]{1,0:T(8,128)S(1)}, f32[8,512]{1,0:T(8,128)S(1)}, u32[]{:S(2)}, u32[]{:S(2)}) collective-permute-start(f32[8,512]{1,0:T(8,128)S(1)} %pair.1.refs_0_), channel_id=1, source_target_pairs={{0,4},{4,8},{8,12},{12,0},{1,5},{5,9},{9,13},{13,1},{2,6},{6,10},{... | collective-permute-start | bytes 49160 | tf_op jit(solution)/shard_map/ppermute | solution.py:27
  98.2 9.3 %collective-permute-start.28 = (f32[8,512]{1,0:T(8,128)S(1)}, f32[8,512]{1,0:T(8,128)S(1)}, u32[]{:S(2)}, u32[]{:S(2)}) collective-permute-start(f32[8,512]{1,0:T(8,128)S(1)} %pair.1.refs_0_), channel_id=1, source_target_pairs={{0,12},{4,0},{8,4},{12,8},{1,13},{5,1},{9,5},{13,9},{2,14},{6,2},{... | collective-permute-start | bytes 49160 | tf_op jit(solution)/shard_map/ppermute | solution.py:27
  98.2 9.3 %collective-permute-start.29 = (f32[8,512]{1,0:T(8,128)S(1)}, f32[8,512]{1,0:T(8,128)S(1)}, u32[]{:S(2)}, u32[]{:S(2)}) collective-permute-start(f32[8,512]{1,0:T(8,128)S(1)} %pair.1.refs_0_), channel_id=1, source_target_pairs={{0,8},{4,12},{8,0},{12,4},{1,9},{5,13},{9,1},{13,5},{2,10},{6,14},... | collective-permute-start | bytes 49160 | tf_op jit(solution)/shard_map/ppermute | solution.py:27
  110.1 2.7 %collective-permute-start.30 = (f32[4,512,128]{2,1,0:T(8,128)S(1)}, f32[4,512,128]{2,1,0:T(8,128)S(1)}, u32[]{:S(2)}, u32[]{:S(2)}) collective-permute-start(f32[4,512,128]{2,1,0:T(8,128)S(1)} %get-tuple-element.25), channel_id=1, source_target_pairs={{0,2},{2,0},{1,3},{3,1},{4,6},{6,4},{5,7},{7,5},{8,10},{10,8},{9,1... | collective-permute-start | bytes 3145736 | tf_op jit(solution)/shard_map/ppermute | solution.py:27
  113.1 8.2 %collective-permute-start.31 = (bf16[512,128]{1,0:T(8,128)(2,1)S(1)}, bf16[512,128]{1,0:T(8,128)(2,1)S(1)}, u32[]{:S(2)}, u32[]{:S(2)}) collective-permute-start(bf16[512,128]{1,0:T(8,128)(2,1)S(1)} %get-tuple-element.30), channel_id=1, source_target_pairs={{0,4},{4,8},{8,12},{12,0},{1,5},{5,9},{9,13},{13,1},{2,6},{6,10},{... | collective-permute-start | bytes 393224 | tf_op jit(solution)/shard_map/ppermute | solution.py:27
  114.4 7.6 %collective-permute-start.32 = (bf16[512,128]{1,0:T(8,128)(2,1)S(1)}, bf16[512,128]{1,0:T(8,128)(2,1)S(1)}, u32[]{:S(2)}, u32[]{:S(2)}) collective-permute-start(bf16[512,128]{1,0:T(8,128)(2,1)S(1)} %get-tuple-element.29), channel_id=1, source_target_pairs={{0,12},{4,0},{8,4},{12,8},{1,13},{5,1},{9,5},{13,9},{2,14},{6,2},{... | collective-permute-start | bytes 393224 | tf_op jit(solution)/shard_map/ppermute | solution.py:27
  117.3 14.4 %collective-permute-start.33 = (bf16[512,128]{1,0:T(8,128)(2,1)S(1)}, bf16[512,128]{1,0:T(8,128)(2,1)S(1)}, u32[]{:S(2)}, u32[]{:S(2)}) collective-permute-start(bf16[512,128]{1,0:T(8,128)(2,1)S(1)} %get-tuple-element.28), channel_id=1, source_target_pairs={{0,8},{4,12},{8,0},{12,4},{1,9},{5,13},{9,1},{13,5},{2,10},{6,14},... | collective-permute-start | bytes 393224 | tf_op jit(solution)/shard_map/ppermute | solution.py:27
  160.3 5.9 %collective-permute-start.34 = (f32[320,128]{1,0:T(8,128)S(1)}, f32[320,128]{1,0:T(8,128)S(1)}, u32[]{:S(2)}, u32[]{:S(2)}) collective-permute-start(f32[320,128]{1,0:T(8,128)S(1)} %convert_reduce_fusion), channel_id=1, source_target_pairs={{0,1},{1,0},{2,3},{3,2},{4,5},{5,4},{6,7},{7,6},{8,9},{9,8},{10,11... | collective-permute-start | bytes 491528 | tf_op jit(solution)/shard_map/ppermute | solution.py:27

commit v4 on v3

--- a/solution.py
+++ b/solution.py
@@ -10,9 +10,9 @@
 PLANE = ("y", "x")
 FSDP_TOWER = ("y", "x", "tw")
 REL = (0, 3, 1, 2)
-NEAR = (0, 3, 1)
+NEAR = ((0, 3), (0, 1))
 AROUND = (0, 3, 1, 2)
-FAR = (2,)
+FAR = ((1, 2), (3, 2))
 
 epsilon = 1e-06
 score_scale = 100.0
@@ -47,8 +47,9 @@
         for half, toward in zip(halves, (1, -1)):
             first = shifted(half, outer, toward)
             second = shifted(half, outer, -toward)
-            near += [half, first, second] if toward == 1 else [half, second, first]
-            far.append(shifted(first, outer, toward))
+            across = shifted(first, outer, toward)
+            near += [half, first]
+            far += [second, across]
     return [in_hbm(piece) for piece in near], [in_hbm(piece) for piece in far]
 
 
@@ -74,7 +75,7 @@
     for side in range(2):
         tw = tower if side == 0 else 1 - tower
         for half in range(2):
-            for step in steps:
+            for step in steps[half]:
                 firsts = []
                 for inner in REL[2 * half : 2 * half + 2]:
                     ahead = (step, inner) if side == 0 else (inner, step)
@@ -103,12 +104,9 @@
     out_ref[...] = in_ref[...]
 
 
-def spread_kernel(in_ref, out_ref, sem):
-    copies = [pltpu.make_async_copy(in_ref, out_ref.at[k], sem.at[k]) for k in range(16)]
-    for copy in copies:
-        copy.start()
-    for copy in copies:
-        copy.wait()
+def spread_kernel(in_ref, out_ref):
+    for k in range(out_ref.shape[0]):
+        out_ref[k] = in_ref[...]
 
 
 def sign_kernel(forget_ref, out_ref, sign, sem):
@@ -316,45 +314,65 @@
     out_ref[...] = merged(first, second)
 
 
-def combine_kernel(*refs):
-    around, (tops_ref, soft_ref, hard_ref) = refs[:4], refs[4:7]
-    keep_ref, give_ref, lines_ref = refs[7:10]
-    every, tops, soft, hard, sem = refs[10:]
-    copies = [
-        pltpu.make_async_copy(tops_ref, tops, sem.at[2]),
-        pltpu.make_async_copy(soft_ref, soft, sem.at[0]),
-        pltpu.make_async_copy(hard_ref, hard, sem.at[1]),
-    ]
+def scaled_blocks(soft_ref, hard_ref, factors, out_ref, soft, hard, sem, which):
+    zh = lax.axis_index("zh")
+    feats = out_ref.shape[2]
+    copies = []
+    for k, step in enumerate(AROUND):
+        owner = lax.rem(zh + step, 4) * 2 + which
+        at = pl.ds(pl.multiple_of(owner * feats, feats), feats)
+        copies.append(pltpu.make_async_copy(soft_ref.at[:, at], soft.at[k], sem.at[0, k]))
+        copies.append(pltpu.make_async_copy(hard_ref.at[:, at], hard.at[k], sem.at[1, k]))
     for copy in copies:
         copy.start()
-    zh, core = lax.axis_index("zh"), lax.axis_index("core")
-    feats = keep_ref.shape[2]
-    for step, ref in zip(AROUND, around):
-        every[lax.rem(zh + step, 4)] = ref[...]
-    rest = [every[k] for k in range(4)]
-    high = rest[0][0:1]
-    for v in rest[1:]:
-        high = jnp.maximum(high, v[0:1])
-    mass = sum(jnp.exp(v[0:1] - high) * v[1:2] for v in rest)
-    lse = high + jnp.log(mass)
-    target = sum(v[3:4] for v in rest)
-    mean = sum(jnp.exp(v[0:1] - lse) * v[2:3] for v in rest)
-    copies[0].wait()
-    sign = tops[5:6]
-    lines_ref[0:1] = lse - target
-    lines_ref[1:2] = sign * (mean - target)
-    lines_ref[2:3] = tops[4:5]
-    for_soft = score_scale * sign * jnp.exp(tops[0:1] - lse)
-    weight = (sign * (jnp.exp(target - lse) - 1.0)).astype(bf16).astype(f32)
-    cols = as_columns([for_soft, score_scale * weight])
+    cols = factors()
     first, second = cols[:, 0:1], cols[:, 1:2]
-    for copy in copies[1:]:
+    for k in range(4):
+        copies[2 * k].wait()
+        copies[2 * k + 1].wait()
+        out_ref[k] = first * soft[k] + second * hard[k].astype(f32)
+
+
+def give_kernel(*refs):
+    around, (tops_ref, soft_ref, hard_ref) = refs[:4], refs[4:7]
+    give_ref, lines_ref = refs[7:9]
+    every, tops, soft, hard, sem, tops_sem = refs[9:]
+    copy = pltpu.make_async_copy(tops_ref, tops, tops_sem)
+    copy.start()
+
+    def factors():
+        zh = lax.axis_index("zh")
+        for step, ref in zip(AROUND, around):
+            every[lax.rem(zh + step, 4)] = ref[...]
+        rest = [every[k] for k in range(4)]
+        high = rest[0][0:1]
+        for v in rest[1:]:
+            high = jnp.maximum(high, v[0:1])
+        mass = sum(jnp.exp(v[0:1] - high) * v[1:2] for v in rest)
+        lse = high + jnp.log(mass)
+        target = sum(v[3:4] for v in rest)
+        mean = sum(jnp.exp(v[0:1] - lse) * v[2:3] for v in rest)
         copy.wait()
-    for k, step in enumerate(AROUND):
-        for out, which in ((keep_ref, core), (give_ref, 1 - core)):
-            owner = lax.rem(zh + step, 4) * 2 + which
-            at = pl.ds(pl.multiple_of(owner * feats, feats), feats)
-            out[k] = first * soft[:, at] + second * hard[:, at].astype(f32)
+        sign = tops[5:6]
+        for_soft = score_scale * sign * jnp.exp(tops[0:1] - lse)
+        weight = (sign * (jnp.exp(target - lse) - 1.0)).astype(bf16).astype(f32)
+        lines_ref[0:1] = lse - target
+        lines_ref[1:2] = sign * (mean - target)
+        lines_ref[2:3] = tops[4:5]
+        lines_ref[3:4] = for_soft
+        lines_ref[4:5] = score_scale * weight
+        return as_columns([for_soft, score_scale * weight])
+
+    which = 1 - lax.axis_index("core")
+    scaled_blocks(soft_ref, hard_ref, factors, give_ref, soft, hard, sem, which)
+
+
+def keep_kernel(lines_ref, soft_ref, hard_ref, keep_ref, soft, hard, sem):
+    def factors():
+        return as_columns([lines_ref[3:4], lines_ref[4:5]])
+
+    which = lax.axis_index("core")
+    scaled_blocks(soft_ref, hard_ref, factors, keep_ref, soft, hard, sem, which)
 
 
 def weight_kernel(images_ref, own_ref, one_ref, two_ref, three_ref, emb_ref, lines_ref, out_ref, held, sem):
@@ -382,11 +400,10 @@
     copies = pl.pallas_call(
         spread_kernel,
         name="spread",
-        out_shape=pltpu.HBM((16, *img_weight.shape), bf16),
+        out_shape=jax.ShapeDtypeStruct((16, *img_weight.shape), bf16),
         in_specs=[VMEM],
-        out_specs=HBM,
-        scratch_shapes=[pltpu.SemaphoreType.DMA((16,))],
-        compiler_params=pltpu.CompilerParams(vmem_limit_bytes=2 << 20),
+        out_specs=VMEM,
+        compiler_params=pltpu.CompilerParams(vmem_limit_bytes=4 << 20),
     )(img_weight)
     weight = exchanged(copies, PLANE).reshape(width, feats)
     other_texts = shifted(texts, "tw", 1)
@@ -526,27 +543,42 @@
         cost_estimate=cost(2 * work * far_rows, far_rows),
     )(perm, in_hbm(far_p), in_hbm(tops), in_hbm(near_soft), in_hbm(near_hard), *far)
 
-    keep, give, lines = pl.pallas_call(
-        combine_kernel,
-        name="combine",
+    soft, hard = in_hbm(soft), in_hbm(hard)
+    block_scratch = [
+        pltpu.VMEM((4, rows, feats), f32),
+        pltpu.VMEM((4, rows, feats), bf16),
+        pltpu.SemaphoreType.DMA((2, 4)),
+    ]
+    give, lines = pl.pallas_call(
+        give_kernel,
+        name="give",
         out_shape=(
-            jax.ShapeDtypeStruct((4, rows, feats), f32),
             jax.ShapeDtypeStruct((4, rows, feats), f32),
             jax.ShapeDtypeStruct((8, rows), f32),
         ),
         in_specs=[VMEM, VMEM, VMEM, VMEM, HBM, HBM, HBM],
-        out_specs=(VMEM, VMEM, VMEM),
+        out_specs=(VMEM, VMEM),
         scratch_shapes=[
             pltpu.VMEM((4, 8, rows), f32),
             pltpu.VMEM((8, rows), f32),
-            *gradient_scratch,
-            pltpu.SemaphoreType.DMA((3,)),
+            *block_scratch,
+            pltpu.SemaphoreType.DMA,
         ],
-        compiler_params=pltpu.CompilerParams(vmem_limit_bytes=20 << 20),
-    )(*every, in_hbm(tops), in_hbm(soft), in_hbm(hard))
+        compiler_params=pltpu.CompilerParams(vmem_limit_bytes=12 << 20),
+    )(*every, in_hbm(tops), soft, hard)
+    given = shifted(give, "core", 1)
+    keep = pl.pallas_call(
+        keep_kernel,
+        name="keep",
+        out_shape=jax.ShapeDtypeStruct((4, rows, feats), f32),
+        in_specs=[VMEM, HBM, HBM],
+        out_specs=VMEM,
+        scratch_shapes=block_scratch,
+        compiler_params=pltpu.CompilerParams(vmem_limit_bytes=12 << 20),
+    )(lines, soft, hard)
 
     pair_loss = lines[0]
-    chip = keep + shifted(give, "core", 1)
+    chip = keep + given
     away = [chip[k].astype(bf16) for k in (2, 1, 3)]
     parts = [shifted(part, "zh", step) for part, step in zip(away, (1, -1, 2))]
     share = pl.pallas_call(

time: 168 us -> 163 us (0.970)
  waiting for transfers between devices: 42.5 us -> 38.1 us
    ppermute x35, waiting for transfers between devices: 42.5 us -> 38.1 us  [shifted(): return lax.ppermute(x, axis, [(i, (i + step) % n) for i in range(n)])]
    pallas_call x1, Pallas kernels: 9.81 us -> 7.33 us  [local(): pl.pallas_call(lambda *refs: near_kernel(n, group, *refs), name='near', o...]
    pallas_call x2 -> x3, Pallas kernels: 3.86 us -> 4.57 us  [the longest x1 1.79 us: local(): pl.pallas_call(give_kernel, name='give', out_shape=(jax.ShapeDtypeStruct(...]
  transfers between devices with their start and end apart: 36 -> 36, of which waited for: 12 -> 10; matrix products, arithmetic and copies ran while one was open for 0% -> 0% of each run, Pallas kernels for 12% -> 12%
where the time goes in v4:
time: 163 us; the launch traced here: 161 us
  starting transfers between devices  62.6 us (38%)
  waiting for transfers between devices  38.1 us (23%)
  Pallas kernels  31.6 us (19%)
  blocking collectives  23.5 us (14%)
  local copies, waits for them, and re-layouts  3.5 us (2%)
    ppermute x35, starting transfers between devices, shifted(): return lax.ppermute(x, axis, [(i, (i + step) % n) for i in range(n)])  55 us
    ppermute x35, waiting for transfers between devices, shifted(): return lax.ppermute(x, axis, [(i, (i + step) % n) for i in range(n)])  38.1 us
    all_to_all x1, blocking collectives, exchanged(): return lax.all_to_all(x, axis, 0, 0, tiled=True)  23.5 us
    all_to_all x1, starting transfers between devices, exchanged(): return lax.all_to_all(x, axis, 0, 0, tiled=True)  7.61 us
    pallas_call x1, Pallas kernels, local(): pl.pallas_call(lambda *refs: near_kernel(n, group, *refs), name='near', o...  7.33 us
    pallas_call x1, Pallas kernels, local(): pl.pallas_call(lambda *refs: far_gradient_kernel(m, group, *refs), name='...  6.43 us
    pallas_call x1, Pallas kernels, local(): pl.pallas_call(lambda *refs: far_score_kernel(m, group, *refs), name='far...  4.95 us
    pallas_call x1, Pallas kernels, local(): pl.pallas_call(embed_kernel, name='embed', out_shape=pltpu.HBM((rows, fea...  3.98 us
  transfers between devices with their start and end apart: 36, of which 10 were waited for; matrix products, arithmetic and copies ran while one was open for 0% of the time, Pallas kernels for 12%

profile of v4, /device:TPU:2, one launch (start us, length us, event | category | flops | bytes accessed | tf_op | source)
XLA Modules:
  0.0 161.5 jit_solution(3751869280487509571)
XLA Ops:
  0.6 0.9 copy-done.1
  1.5 1.3 spread.1
  2.8 7.6 %all-to-all-start = ((bf16[16,320,128]{2,1,0:T(8,128)(2,1)}), bf16[16,320,128]{2,1,0:T(8,128)(2,1)S(1)}, u32[]{:S(2)}, u32[]{:S(2)}) async-start(bf16[16,320,128]{2,1,0:T(8,128)(2,1)} %spread.1), calls=%async_computation | async-start | bytes 2621440 | tf_op jit(solution)/shard_map/all_to_all | solution.py:35
  10.4 2.0 %collective-permute-start.12 = (bf16[64,1024]{1,0:T(8,128)(2,1)S(1)}, bf16[64,1024]{1,0:T(8,128)(2,1)S(1)}, u32[]{:S(2)}, u32[]{:S(2)}) collective-permute-start(bf16[64,1024]{1,0:T(8,128)(2,1)S(1)} %copy-done.5), channel_id=1, source_target_pairs={{0,1},{1,0},{2,3},{3,2},{4,5},{5,4},{6,7},{7,6},{8,9},{9,8},{10,11... | collective-permute-start | bytes 393224 | tf_op jit(solution)/shard_map/ppermute | solution.py:27
  12.4 1.5 collective-permute-start.7
  13.9 0.6 collective-permute-start.9
  14.4 2.1 %collective-permute-start.10 = (bf16[64,1024]{1,0:T(8,128)(2,1)S(1)}, bf16[64,1024]{1,0:T(8,128)(2,1)S(1)}, u32[]{:S(2)}, u32[]{:S(2)}) collective-permute-start(bf16[64,1024]{1,0:T(8,128)(2,1)S(1)} %copy-done.5), channel_id=1, source_target_pairs={{0,32},{16,48},{32,0},{48,16},{1,33},{17,49},{33,1},{49,17},{2,34}... | collective-permute-start | bytes 393224 | tf_op jit(solution)/shard_map/ppermute | solution.py:27
  16.5 3.1 %collective-permute-start.16 = (bf16[64,1024]{1,0:T(8,128)(2,1)S(1)}, bf16[64,1024]{1,0:T(8,128)(2,1)S(1)}, u32[]{:S(2)}, u32[]{:S(2)}) collective-permute-start(bf16[64,1024]{1,0:T(8,128)(2,1)S(1)} %gate.1), channel_id=1, source_target_pairs={{0,128},{64,192},{128,0},{192,64},{1,129},{65,193},{129,1},{193,65... | collective-permute-start | bytes 393224 | tf_op jit(solution)/shard_map/ppermute | solution.py:27
  19.6 1.2 collective-permute-start.15
  20.8 10.7 %collective-permute-done.7 = bf16[64,1024]{1,0:T(8,128)(2,1)S(1)} collective-permute-done((bf16[64,1024]{1,0:T(8,128)(2,1)S(1)}, bf16[64,1024]{1,0:T(8,128)(2,1)S(1)}, u32[]{:S(2)}, u32[]{:S(2)}) %collective-permute-start.7) | collective-permute-done | bytes 131104 | tf_op jit(solution)/shard_map/ppermute | solution.py:27
  31.5 1.3 collective-permute-start.13
  32.8 2.1 %collective-permute-start.18 = (bf16[128,1024]{1,0:T(8,128)(2,1)S(1)}, bf16[128,1024]{1,0:T(8,128)(2,1)S(1)}, u32[]{:S(2)}, u32[]{:S(2)}) collective-permute-start(bf16[128,1024]{1,0:T(8,128)(2,1)S(1)} %constant_dynamic-update-slice_fusion.refs_9_), channel_id=1, source_target_pairs={{0,192},{64,0},{128,64},{192,128},{1,193},{65,1},{129,65},{193,129... | collective-permute-start | bytes 786440 | tf_op jit(solution)/shard_map/ppermute | solution.py:27
  34.9 0.1 collective-permute-start.8
  35.0 3.1 %collective-permute-done.13 = bf16[64,1024]{1,0:T(8,128)(2,1)S(1)} collective-permute-done((bf16[64,1024]{1,0:T(8,128)(2,1)S(1)}, bf16[64,1024]{1,0:T(8,128)(2,1)S(1)}, u32[]{:S(2)}, u32[]{:S(2)}) %collective-permute-start.13) | collective-permute-done | bytes 131104 | tf_op jit(solution)/shard_map/ppermute | solution.py:27
  38.1 0.9 collective-permute-start.20
  39.1 2.4 %collective-permute-start.11 = (bf16[128,1024]{1,0:T(8,128)(2,1)S(1)}, bf16[128,1024]{1,0:T(8,128)(2,1)}, u32[]{:S(2)}, u32[]{:S(2)}) collective-permute-start(bf16[128,1024]{1,0:T(8,128)(2,1)S(1)} %constant_dynamic-update-slice_fusion.2.refs_11_), channel_id=1, source_target_pairs={{0,192},{64,0},{128,64},{192,128},{1,193},{65,1},{129,65},{193,129... | collective-permute-start | bytes 786440 | tf_op jit(solution)/shard_map/ppermute | solution.py:27
  41.5 0.4 collective-permute-start.22
  41.9 2.2 %collective-permute-start.14 = (bf16[128,1024]{1,0:T(8,128)(2,1)S(1)}, bf16[128,1024]{1,0:T(8,128)(2,1)}, u32[]{:S(2)}, u32[]{:S(2)}) collective-permute-start(bf16[128,1024]{1,0:T(8,128)(2,1)S(1)} %pad_maximum_fusion.refs_13_), channel_id=1, source_target_pairs={{0,16},{16,32},{32,48},{48,0},{1,17},{17,33},{33,49},{49,1},{2,18}... | collective-permute-start | bytes 786440 | tf_op jit(solution)/shard_map/ppermute | solution.py:27
  44.2 1.1 collective-permute-done.8.refs_10_
  45.3 0.8 collective-permute-start.17
  46.1 4.0 %embed.1.refs_0_.emb_ref = bf16[512,128]{1,0:T(8,128)(2,1)} custom-call(bf16[512,5120]{1,0:T(8,128)(2,1)} %images_ref.3, bf16[5120,128]{1,0:T(8,128)(2,1)S(1)} %bitcast.13), custom_call_target="tpu_custom_call" | custom-call | flops 671088640 | bytes 7340032 | tf_op jit(solution)/shard_map/embed/pallas_call | solution.py:440
  50.2 7.3 %collective-permute-start.2 = (bf16[512,128]{1,0:T(8,128)(2,1)}, bf16[512,128]{1,0:T(8,128)(2,1)S(1)}, u32[]{:S(2)}, u32[]{:S(2)}) collective-permute-start(bf16[512,128]{1,0:T(8,128)(2,1)} %embed.1.refs_0_.emb_ref), channel_id=1, source_target_pairs={{0,8},{4,12},{8,0},{12,4},{1,9},{5,13},{9,1},{13,5},{2,10},{6,14},... | collective-permute-start | bytes 393224 | tf_op jit(solution)/shard_map/ppermute | solution.py:27
  57.4 0.0 collective-permute-start.1
  57.5 2.9 %collective-permute-start = (bf16[512,128]{1,0:T(8,128)(2,1)}, bf16[512,128]{1,0:T(8,128)(2,1)S(1)}, u32[]{:S(2)}, u32[]{:S(2)}) collective-permute-start(bf16[512,128]{1,0:T(8,128)(2,1)} %embed.1.refs_0_.emb_ref), channel_id=1, source_target_pairs={{0,4},{4,8},{8,12},{12,0},{1,5},{5,9},{9,13},{13,1},{2,6},{6,10},{... | collective-permute-start | bytes 393224 | tf_op jit(solution)/shard_map/ppermute | solution.py:27
  60.4 1.9 %collective-permute-done.2.refs_3_ = bf16[512,128]{1,0:T(8,128)(2,1)S(1)} collective-permute-done((bf16[512,128]{1,0:T(8,128)(2,1)}, bf16[512,128]{1,0:T(8,128)(2,1)S(1)}, u32[]{:S(2)}, u32[]{:S(2)}) %collective-permute-start.2) | collective-permute-done | bytes 131104 | tf_op jit(solution)/shard_map/ppermute | solution.py:27
  62.3 5.8 %collective-permute-done.1.refs_2_ = bf16[512,128]{1,0:T(8,128)(2,1)S(1)} collective-permute-done((bf16[512,128]{1,0:T(8,128)(2,1)}, bf16[512,128]{1,0:T(8,128)(2,1)S(1)}, u32[]{:S(2)}, u32[]{:S(2)}) %collective-permute-start.1) | collective-permute-done | bytes 131104 | tf_op jit(solution)/shard_map/ppermute | solution.py:27
  68.1 0.5 collective-permute-start.4
  68.6 0.6 signs.1.refs_3_
  69.2 0.1 places.1.refs_8_.refs_1_.refs_0_
  69.4 2.6 %collective-permute-start.24 = (bf16[128,1024]{1,0:T(8,128)(2,1)S(1)}, bf16[128,1024]{1,0:T(8,128)(2,1)S(1)}, u32[]{:S(2)}, u32[]{:S(2)}) collective-permute-start(bf16[128,1024]{1,0:T(8,128)(2,1)S(1)} %constant_dynamic-update-slice_fusion.4.refs_15_), channel_id=1, source_target_pairs={{0,16},{16,32},{32,48},{48,0},{1,17},{17,33},{33,49},{49,1},{2,18}... | collective-permute-start | bytes 786440 | tf_op jit(solution)/shard_map/ppermute | solution.py:27
  71.9 0.7 collective-permute-start.19
  72.6 2.5 %collective-permute-start.21 = (bf16[128,1024]{1,0:T(8,128)(2,1)}, bf16[128,1024]{1,0:T(8,128)(2,1)S(1)}, u32[]{:S(2)}, u32[]{:S(2)}) collective-permute-start(bf16[128,1024]{1,0:T(8,128)(2,1)} %collective-permute-done.11.refs_12_), channel_id=1, source_target_pairs={{0,192},{64,0},{128,64},{192,128},{1,193},{65,1},{129,65},{193,129... | collective-permute-start | bytes 786440 | tf_op jit(solution)/shard_map/ppermute | solution.py:27
  75.2 0.2 collective-permute-start.23
  75.4 1.8 %collective-permute-start.25 = (bf16[128,1024]{1,0:T(8,128)(2,1)}, bf16[128,1024]{1,0:T(8,128)(2,1)S(1)}, u32[]{:S(2)}, u32[]{:S(2)}) collective-permute-start(bf16[128,1024]{1,0:T(8,128)(2,1)} %collective-permute-done.17.refs_16_), channel_id=1, source_target_pairs={{0,48},{16,0},{32,16},{48,32},{1,49},{17,1},{33,17},{49,33},{2,50}... | collective-permute-start | bytes 786440 | tf_op jit(solution)/shard_map/ppermute | solution.py:27
  77.2 0.9 copy-done
  78.1 7.3 %near.1 = (f32[512,1024]{1,0:T(8,128)}, bf16[512,1024]{1,0:T(8,128)(2,1)}, f32[8,512]{1,0:T(8,128)S(1)}, bf16[512,1024]{1,0:T(8,128)(2,1)S(1)}) custom-call(bf16[512,128]{1,0:T(8,128)(2,1)S(1)} %copy-done, bf16[512,128]{1,0:T(8,128)(2,1)S(1)} %collective-permute-done.refs_1_, bf16[512,128]{1,0:T(8,128)(2,1)S(1)} %collective-permute-done.1.refs_2_, ...), custom_call_target="tpu_custom_call" | custom-call | flops 3221225472 | bytes 4194304 | tf_op jit(solution)/shard_map/near/pallas_call | solution.py:468
  85.6 0.6 copy-done.13
  86.2 0.1 copy-done.14
  86.4 0.1 copy-done.15
  86.4 0.0 copy-done.16
  86.5 0.1 copy-done.17
  86.6 4.9 %far_scores.1 = (bf16[512,1024]{1,0:T(8,128)(2,1)}, f32[8,512]{1,0:T(8,128)}, f32[8,512]{1,0:T(8,128)S(1)}) custom-call(bf16[512,1024]{1,0:T(8,128)(2,1)S(1)} %get-tuple-element.13.refs_0_, s32[512,1]{1,0:T(8,128)S(1)} %places.1.refs_8_.refs_1_.refs_0_, f32[8,512]{1,0:T(8,128)S(1)} %get-tuple-element.14.refs_2_, f32[1,512]{1,0:T(1,128)} %signs.1.refs_3_, ...), custom_call_target="tpu_custom_call" | custom-call | flops 1073741824 | bytes 4194304 | tf_op jit(solution)/shard_map/far_scores/pallas_call | solution.py:491
  91.5 0.3 collective-permute-start.26
  91.8 1.2 collective-permute-done.26.theirs_ref
  93.0 3.8 %collective-permute-start.29 = (f32[8,512]{1,0:T(8,128)S(1)}, f32[8,512]{1,0:T(8,128)S(1)}, u32[]{:S(2)}, u32[]{:S(2)}) collective-permute-start(f32[8,512]{1,0:T(8,128)S(1)} %pair.1.refs_0_), channel_id=1, source_target_pairs={{0,8},{4,12},{8,0},{12,4},{1,9},{5,13},{9,1},{13,5},{2,10},{6,14},... | collective-permute-start | bytes 49160 | tf_op jit(solution)/shard_map/ppermute | solution.py:27
  96.9 1.1 collective-permute-start.28
  97.9 1.9 %collective-permute-start.27 = (f32[8,512]{1,0:T(8,128)S(1)}, f32[8,512]{1,0:T(8,128)S(1)}, u32[]{:S(2)}, u32[]{:S(2)}) collective-permute-start(f32[8,512]{1,0:T(8,128)S(1)} %pair.1.refs_0_), channel_id=1, source_target_pairs={{0,4},{4,8},{8,12},{12,0},{1,5},{5,9},{9,13},{13,1},{2,6},{6,10},{... | collective-permute-start | bytes 49160 | tf_op jit(solution)/shard_map/ppermute | solution.py:27
  99.8 6.4 %far_gradient.1 = (f32[512,1024]{1,0:T(8,128)}, bf16[512,1024]{1,0:T(8,128)(2,1)}) custom-call(s32[512,1]{1,0:T(8,128)S(1)} %places.1.refs_8_.refs_1_.refs_0_, bf16[512,1024]{1,0:T(8,128)(2,1)} %get-tuple-element.17.refs_1_, f32[8,512]{1,0:T(8,128)} %get-tuple-element.16.refs_2_.refs_4_, f32[512,1024]{1,0:T(8,128)} %get-tuple-element.18.refs_3_, ...), custom_call_target="tpu_custom_call" | custom-call | flops 2147483648 | bytes 4194304 | tf_op jit(solution)/shard_map/far_gradient/pallas_call | solution.py:525
  106.3 1.8 %give.1 = (f32[4,512,128]{2,1,0:T(8,128)S(1)}, f32[8,512]{1,0:T(8,128)S(1)}) custom-call(f32[8,512]{1,0:T(8,128)S(1)} %pair.1.refs_0_, f32[8,512]{1,0:T(8,128)S(1)} %collective-permute-done.27.refs_1_, f32[8,512]{1,0:T(8,128)S(1)} %collective-permute-done.28.refs_2_, f32[8,512]{1,0:T(8,128)S(1)} %collective-permute-done.29.refs_3_, ...), custom_call_target="tpu_custom_call" | custom-call | tf_op jit(solution)/shard_map/give/pallas_call | solution.py:552
  108.1 0.1 collective-permute-start.30
  108.2 1.5 keep.1
  109.7 1.1 collective-permute-done.30
  110.8 0.1 fusion
  111.0 2.5 %collective-permute-start.33 = (bf16[512,128]{1,0:T(8,128)(2,1)S(1)}, bf16[512,128]{1,0:T(8,128)(2,1)S(1)}, u32[]{:S(2)}, u32[]{:S(2)}) collective-permute-start(bf16[512,128]{1,0:T(8,128)(2,1)S(1)} %get-tuple-element.26), channel_id=1, source_target_pairs={{0,8},{4,12},{8,0},{12,4},{1,9},{5,13},{9,1},{13,5},{2,10},{6,14},... | collective-permute-start | bytes 393224 | tf_op jit(solution)/shard_map/ppermute | solution.py:27
  113.5 4.1 %collective-permute-start.32 = (bf16[512,128]{1,0:T(8,128)(2,1)S(1)}, bf16[512,128]{1,0:T(8,128)(2,1)S(1)}, u32[]{:S(2)}, u32[]{:S(2)}) collective-permute-start(bf16[512,128]{1,0:T(8,128)(2,1)S(1)} %get-tuple-element.27), channel_id=1, source_target_pairs={{0,12},{4,0},{8,4},{12,8},{1,13},{5,1},{9,5},{13,9},{2,14},{6,2},{... | collective-permute-start | bytes 393224 | tf_op jit(solution)/shard_map/ppermute | solution.py:27
  117.6 3.6 %collective-permute-done.33.three_ref = bf16[512,128]{1,0:T(8,128)(2,1)S(1)} collective-permute-done((bf16[512,128]{1,0:T(8,128)(2,1)S(1)}, bf16[512,128]{1,0:T(8,128)(2,1)S(1)}, u32[]{:S(2)}, u32[]{:S(2)}) %collective-permute-start.33) | collective-permute-done | bytes 131104 | tf_op jit(solution)/shard_map/ppermute | solution.py:27
  121.2 6.7 %collective-permute-done.32.two_ref = bf16[512,128]{1,0:T(8,128)(2,1)S(1)} collective-permute-done((bf16[512,128]{1,0:T(8,128)(2,1)S(1)}, bf16[512,128]{1,0:T(8,128)(2,1)S(1)}, u32[]{:S(2)}, u32[]{:S(2)}) %collective-permute-start.32) | collective-permute-done | bytes 131104 | tf_op jit(solution)/shard_map/ppermute | solution.py:27
  127.9 3.5 %weight.1 = bf16[5120,128]{1,0:T(8,128)(2,1)S(1)} custom-call(bf16[512,5120]{1,0:T(8,128)(2,1)} %images_ref.3, f32[512,128]{1,0:T(8,128)S(1)} %slice_bitcast_fusion.own_ref, bf16[512,128]{1,0:T(8,128)(2,1)S(1)} %collective-permute-done.31.one_ref, bf16[512,128]{1,0:T(8,128)(2,1)S(1)} %collective-permute-done.32.two_ref, ...), custom_call_target="tpu_custom_call" | custom-call | tf_op jit(solution)/shard_map/weight/pallas_call | solution.py:584
  131.5 23.5 %all_to_all.10 = bf16[16,320,128]{2,1,0:T(8,128)(2,1)S(1)} all-to-all(bf16[16,320,128]{2,1,0:T(8,128)(2,1)S(1)} %bitcast.14), channel_id=1, replica_groups=mesh['y'=4,'x'=4,'zh'=4,'core'=2,'tw'=2] {'y','x'}, dimensions={0} | all-to-all | bytes 2621440 | tf_op jit(solution)/shard_map/all_to_all | solution.py:35
  155.0 0.2 convert_reduce_fusion
  155.2 2.3 %collective-permute-start.34 = (f32[320,128]{1,0:T(8,128)S(1)}, f32[320,128]{1,0:T(8,128)S(1)}, u32[]{:S(2)}, u32[]{:S(2)}) collective-permute-start(f32[320,128]{1,0:T(8,128)S(1)} %convert_reduce_fusion), channel_id=1, source_target_pairs={{0,1},{1,0},{2,3},{3,2},{4,5},{5,4},{6,7},{7,6},{8,9},{9,8},{10,11... | collective-permute-start | bytes 491528 | tf_op jit(solution)/shard_map/ppermute | solution.py:27
  157.5 0.6 slice.18
  158.0 2.7 %collective-permute-done.34 = f32[320,128]{1,0:T(8,128)S(1)} collective-permute-done((f32[320,128]{1,0:T(8,128)S(1)}, f32[320,128]{1,0:T(8,128)S(1)}, u32[]{:S(2)}, u32[]{:S(2)}) %collective-permute-start.34) | collective-permute-done | bytes 163872 | tf_op jit(solution)/shard_map/ppermute | solution.py:27
  160.8 0.7 add.7
  (70 shorter events, 0.3 us)
Async XLA Ops:
  0.6 0.9 copy-start.1
  2.8 7.6 %copy-start.5 = (bf16[64,1024]{1,0:T(8,128)(2,1)S(1)}, bf16[64,1024]{1,0:T(8,128)(2,1)}, u32[]{:S(2)}) copy-start(bf16[64,1024]{1,0:T(8,128)(2,1)} %param.7) | copy-start | bytes 393220
  2.8 43.3 %all-to-all-start = ((bf16[16,320,128]{2,1,0:T(8,128)(2,1)}), bf16[16,320,128]{2,1,0:T(8,128)(2,1)S(1)}, u32[]{:S(2)}, u32[]{:S(2)}) async-start(bf16[16,320,128]{2,1,0:T(8,128)(2,1)} %spread.1), calls=%async_computation | async-start | bytes 2621440 | tf_op jit(solution)/shard_map/all_to_all | solution.py:35
  10.4 6.1 %collective-permute-start.12 = (bf16[64,1024]{1,0:T(8,128)(2,1)S(1)}, bf16[64,1024]{1,0:T(8,128)(2,1)S(1)}, u32[]{:S(2)}, u32[]{:S(2)}) collective-permute-start(bf16[64,1024]{1,0:T(8,128)(2,1)S(1)} %copy-done.5), channel_id=1, source_target_pairs={{0,1},{1,0},{2,3},{3,2},{4,5},{5,4},{6,7},{7,6},{8,9},{9,8},{10,11... | collective-permute-start | bytes 393224 | tf_op jit(solution)/shard_map/ppermute | solution.py:27
  12.4 19.1 %collective-permute-start.7 = (bf16[64,1024]{1,0:T(8,128)(2,1)S(1)}, bf16[64,1024]{1,0:T(8,128)(2,1)S(1)}, u32[]{:S(2)}, u32[]{:S(2)}) collective-permute-start(bf16[64,1024]{1,0:T(8,128)(2,1)S(1)} %copy-done.5), channel_id=1, source_target_pairs={{0,16},{16,32},{32,48},{48,0},{1,17},{17,33},{33,49},{49,1},{2,18}... | collective-permute-start | bytes 393224 | tf_op jit(solution)/shard_map/ppermute | solution.py:27
  13.9 18.9 %collective-permute-start.9 = (bf16[64,1024]{1,0:T(8,128)(2,1)S(1)}, bf16[64,1024]{1,0:T(8,128)(2,1)S(1)}, u32[]{:S(2)}, u32[]{:S(2)}) collective-permute-start(bf16[64,1024]{1,0:T(8,128)(2,1)S(1)} %copy-done.5), channel_id=1, source_target_pairs={{0,48},{16,0},{32,16},{48,32},{1,49},{17,1},{33,17},{49,33},{2,50}... | collective-permute-start | bytes 393224 | tf_op jit(solution)/shard_map/ppermute | solution.py:27
  14.4 20.4 %collective-permute-start.10 = (bf16[64,1024]{1,0:T(8,128)(2,1)S(1)}, bf16[64,1024]{1,0:T(8,128)(2,1)S(1)}, u32[]{:S(2)}, u32[]{:S(2)}) collective-permute-start(bf16[64,1024]{1,0:T(8,128)(2,1)S(1)} %copy-done.5), channel_id=1, source_target_pairs={{0,32},{16,48},{32,0},{48,16},{1,33},{17,49},{33,1},{49,17},{2,34}... | collective-permute-start | bytes 393224 | tf_op jit(solution)/shard_map/ppermute | solution.py:27
  16.5 22.5 %collective-permute-start.16 = (bf16[64,1024]{1,0:T(8,128)(2,1)S(1)}, bf16[64,1024]{1,0:T(8,128)(2,1)S(1)}, u32[]{:S(2)}, u32[]{:S(2)}) collective-permute-start(bf16[64,1024]{1,0:T(8,128)(2,1)S(1)} %gate.1), channel_id=1, source_target_pairs={{0,128},{64,192},{128,0},{192,64},{1,129},{65,193},{129,1},{193,65... | collective-permute-start | bytes 393224 | tf_op jit(solution)/shard_map/ppermute | solution.py:27
  19.6 21.9 %collective-permute-start.15 = (bf16[64,1024]{1,0:T(8,128)(2,1)S(1)}, bf16[64,1024]{1,0:T(8,128)(2,1)S(1)}, u32[]{:S(2)}, u32[]{:S(2)}) collective-permute-start(bf16[64,1024]{1,0:T(8,128)(2,1)S(1)} %gate.1), channel_id=1, source_target_pairs={{0,192},{64,0},{128,64},{192,128},{1,193},{65,1},{129,65},{193,129... | collective-permute-start | bytes 393224 | tf_op jit(solution)/shard_map/ppermute | solution.py:27
  31.5 6.6 %collective-permute-start.13 = (bf16[64,1024]{1,0:T(8,128)(2,1)S(1)}, bf16[64,1024]{1,0:T(8,128)(2,1)S(1)}, u32[]{:S(2)}, u32[]{:S(2)}) collective-permute-start(bf16[64,1024]{1,0:T(8,128)(2,1)S(1)} %gate.1), channel_id=1, source_target_pairs={{0,64},{64,128},{128,192},{192,0},{1,65},{65,129},{129,193},{193,1... | collective-permute-start | bytes 393224 | tf_op jit(solution)/shard_map/ppermute | solution.py:27
  32.8 17.3 %copy-start.6 = (bf16[128,1024]{1,0:T(8,128)(2,1)}, bf16[128,1024]{1,0:T(8,128)(2,1)S(1)}, u32[]{:S(2)}) copy-start(bf16[128,1024]{1,0:T(8,128)(2,1)S(1)} %constant_dynamic-update-slice_fusion.refs_9_) | copy-start | bytes 786436
  32.8 9.1 %collective-permute-start.18 = (bf16[128,1024]{1,0:T(8,128)(2,1)S(1)}, bf16[128,1024]{1,0:T(8,128)(2,1)S(1)}, u32[]{:S(2)}, u32[]{:S(2)}) collective-permute-start(bf16[128,1024]{1,0:T(8,128)(2,1)S(1)} %constant_dynamic-update-slice_fusion.refs_9_), channel_id=1, source_target_pairs={{0,192},{64,0},{128,64},{192,128},{1,193},{65,1},{129,65},{193,129... | collective-permute-start | bytes 786440 | tf_op jit(solution)/shard_map/ppermute | solution.py:27
  34.9 10.5 %collective-permute-start.8 = (bf16[128,1024]{1,0:T(8,128)(2,1)S(1)}, bf16[128,1024]{1,0:T(8,128)(2,1)S(1)}, u32[]{:S(2)}, u32[]{:S(2)}) collective-permute-start(bf16[128,1024]{1,0:T(8,128)(2,1)S(1)} %constant_dynamic-update-slice_fusion.refs_9_), channel_id=1, source_target_pairs={{0,64},{64,128},{128,192},{192,0},{1,65},{65,129},{129,193},{193,1... | collective-permute-start | bytes 786440 | tf_op jit(solution)/shard_map/ppermute | solution.py:27
  35.0 15.1 %copy-start.7 = (bf16[128,1024]{1,0:T(8,128)(2,1)}, bf16[128,1024]{1,0:T(8,128)(2,1)S(1)}, u32[]{:S(2)}) copy-start(bf16[128,1024]{1,0:T(8,128)(2,1)S(1)} %constant_dynamic-update-slice_fusion.2.refs_11_) | copy-start | bytes 786436
  38.1 12.0 %collective-permute-start.20 = (bf16[128,1024]{1,0:T(8,128)(2,1)S(1)}, bf16[128,1024]{1,0:T(8,128)(2,1)S(1)}, u32[]{:S(2)}, u32[]{:S(2)}) collective-permute-start(bf16[128,1024]{1,0:T(8,128)(2,1)S(1)} %constant_dynamic-update-slice_fusion.2.refs_11_), channel_id=1, source_target_pairs={{0,64},{64,128},{128,192},{192,0},{1,65},{65,129},{129,193},{193,1... | collective-permute-start | bytes 786440 | tf_op jit(solution)/shard_map/ppermute | solution.py:27
  39.1 11.0 %copy-start.4 = (bf16[128,1024]{1,0:T(8,128)(2,1)}, bf16[128,1024]{1,0:T(8,128)(2,1)S(1)}, u32[]{:S(2)}) copy-start(bf16[128,1024]{1,0:T(8,128)(2,1)S(1)} %pad_maximum_fusion.refs_13_) | copy-start | bytes 786436
  39.1 18.3 %collective-permute-start.11 = (bf16[128,1024]{1,0:T(8,128)(2,1)S(1)}, bf16[128,1024]{1,0:T(8,128)(2,1)}, u32[]{:S(2)}, u32[]{:S(2)}) collective-permute-start(bf16[128,1024]{1,0:T(8,128)(2,1)S(1)} %constant_dynamic-update-slice_fusion.2.refs_11_), channel_id=1, source_target_pairs={{0,192},{64,0},{128,64},{192,128},{1,193},{65,1},{129,65},{193,129... | collective-permute-start | bytes 786440 | tf_op jit(solution)/shard_map/ppermute | solution.py:27
  41.5 16.0 %collective-permute-start.22 = (bf16[128,1024]{1,0:T(8,128)(2,1)S(1)}, bf16[128,1024]{1,0:T(8,128)(2,1)S(1)}, u32[]{:S(2)}, u32[]{:S(2)}) collective-permute-start(bf16[128,1024]{1,0:T(8,128)(2,1)S(1)} %pad_maximum_fusion.refs_13_), channel_id=1, source_target_pairs={{0,48},{16,0},{32,16},{48,32},{1,49},{17,1},{33,17},{49,33},{2,50}... | collective-permute-start | bytes 786440 | tf_op jit(solution)/shard_map/ppermute | solution.py:27
  41.9 8.2 %copy-start.9 = (bf16[128,1024]{1,0:T(8,128)(2,1)}, bf16[128,1024]{1,0:T(8,128)(2,1)S(1)}, u32[]{:S(2)}) copy-start(bf16[128,1024]{1,0:T(8,128)(2,1)S(1)} %collective-permute-done.18.refs_4_.refs_5_) | copy-start | bytes 786436
  41.9 18.4 %collective-permute-start.14 = (bf16[128,1024]{1,0:T(8,128)(2,1)S(1)}, bf16[128,1024]{1,0:T(8,128)(2,1)}, u32[]{:S(2)}, u32[]{:S(2)}) collective-permute-start(bf16[128,1024]{1,0:T(8,128)(2,1)S(1)} %pad_maximum_fusion.refs_13_), channel_id=1, source_target_pairs={{0,16},{16,32},{32,48},{48,0},{1,17},{17,33},{33,49},{49,1},{2,18}... | collective-permute-start | bytes 786440 | tf_op jit(solution)/shard_map/ppermute | solution.py:27
  44.2 25.2 %copy-start.8 = (bf16[128,1024]{1,0:T(8,128)(2,1)}, bf16[128,1024]{1,0:T(8,128)(2,1)S(1)}, u32[]{:S(2)}) copy-start(bf16[128,1024]{1,0:T(8,128)(2,1)S(1)} %constant_dynamic-update-slice_fusion.4.refs_15_) | copy-start | bytes 786436
  45.3 26.6 %copy-start.12 = (bf16[128,1024]{1,0:T(8,128)(2,1)}, bf16[128,1024]{1,0:T(8,128)(2,1)S(1)}, u32[]{:S(2)}) copy-start(bf16[128,1024]{1,0:T(8,128)(2,1)S(1)} %collective-permute-done.8.refs_10_) | copy-start | bytes 786436
  45.3 24.0 %collective-permute-start.17 = (bf16[128,1024]{1,0:T(8,128)(2,1)S(1)}, bf16[128,1024]{1,0:T(8,128)(2,1)}, u32[]{:S(2)}, u32[]{:S(2)}) collective-permute-start(bf16[128,1024]{1,0:T(8,128)(2,1)S(1)} %constant_dynamic-update-slice_fusion.4.refs_15_), channel_id=1, source_target_pairs={{0,48},{16,0},{32,16},{48,32},{1,49},{17,1},{33,17},{49,33},{2,50}... | collective-permute-start | bytes 786440 | tf_op jit(solution)/shard_map/ppermute | solution.py:27
  46.1 22.5 %copy-start.3 = (s32[512]{0:T(512)S(1)}, s32[512]{0:T(512)}, u32[]{:S(2)}) copy-start(s32[512]{0:T(512)} %param.9) | copy-start | bytes 6148
  46.1 23.1 %copy-start.2 = (s32[512]{0:T(512)S(1)}, s32[512]{0:T(512)}, u32[]{:S(2)}) copy-start(s32[512]{0:T(512)} %param.8) | copy-start | bytes 6148
  50.1 35.3 %copy-start.10 = (bf16[128,1024]{1,0:T(8,128)(2,1)}, bf16[128,1024]{1,0:T(8,128)(2,1)S(1)}, u32[]{:S(2)}) copy-start(bf16[128,1024]{1,0:T(8,128)(2,1)S(1)} %collective-permute-done.20.refs_6_.refs_7_) | copy-start | bytes 786436
  50.2 12.1 %collective-permute-start.2 = (bf16[512,128]{1,0:T(8,128)(2,1)}, bf16[512,128]{1,0:T(8,128)(2,1)S(1)}, u32[]{:S(2)}, u32[]{:S(2)}) collective-permute-start(bf16[512,128]{1,0:T(8,128)(2,1)} %embed.1.refs_0_.emb_ref), channel_id=1, source_target_pairs={{0,8},{4,12},{8,0},{12,4},{1,9},{5,13},{9,1},{13,5},{2,10},{6,14},... | collective-permute-start | bytes 393224 | tf_op jit(solution)/shard_map/ppermute | solution.py:27
  57.4 10.7 %collective-permute-start.1 = (bf16[512,128]{1,0:T(8,128)(2,1)}, bf16[512,128]{1,0:T(8,128)(2,1)S(1)}, u32[]{:S(2)}, u32[]{:S(2)}) collective-permute-start(bf16[512,128]{1,0:T(8,128)(2,1)} %embed.1.refs_0_.emb_ref), channel_id=1, source_target_pairs={{0,12},{4,0},{8,4},{12,8},{1,13},{5,1},{9,5},{13,9},{2,14},{6,2},{... | collective-permute-start | bytes 393224 | tf_op jit(solution)/shard_map/ppermute | solution.py:27
  57.4 28.0 %copy-start.11 = (bf16[128,1024]{1,0:T(8,128)(2,1)}, bf16[128,1024]{1,0:T(8,128)(2,1)S(1)}, u32[]{:S(2)}) copy-start(bf16[128,1024]{1,0:T(8,128)(2,1)S(1)} %collective-permute-done.22.refs_8_.refs_9_) | copy-start | bytes 786436
  57.5 10.6 %collective-permute-start = (bf16[512,128]{1,0:T(8,128)(2,1)}, bf16[512,128]{1,0:T(8,128)(2,1)S(1)}, u32[]{:S(2)}, u32[]{:S(2)}) collective-permute-start(bf16[512,128]{1,0:T(8,128)(2,1)} %embed.1.refs_0_.emb_ref), channel_id=1, source_target_pairs={{0,4},{4,8},{8,12},{12,0},{1,5},{5,9},{9,13},{13,1},{2,6},{6,10},{... | collective-permute-start | bytes 393224 | tf_op jit(solution)/shard_map/ppermute | solution.py:27
  60.4 11.6 %collective-permute-start.3 = (bf16[512,128]{1,0:T(8,128)(2,1)}, bf16[512,128]{1,0:T(8,128)(2,1)S(1)}, u32[]{:S(2)}, u32[]{:S(2)}) collective-permute-start(bf16[512,128]{1,0:T(8,128)(2,1)} %embed.1.refs_0_.emb_ref), channel_id=1, source_target_pairs={{0,2},{2,0},{1,3},{3,1},{4,6},{6,4},{5,7},{7,5},{8,10},{10,8},{9,1... | collective-permute-start | bytes 393224 | tf_op jit(solution)/shard_map/ppermute | solution.py:27
  62.3 10.4 %collective-permute-start.6 = (bf16[512,128]{1,0:T(8,128)(2,1)S(1)}, bf16[512,128]{1,0:T(8,128)(2,1)S(1)}, u32[]{:S(2)}, u32[]{:S(2)}) collective-permute-start(bf16[512,128]{1,0:T(8,128)(2,1)S(1)} %collective-permute-done.2.refs_3_), channel_id=1, source_target_pairs={{0,2},{2,0},{1,3},{3,1},{4,6},{6,4},{5,7},{7,5},{8,10},{10,8},{9,1... | collective-permute-start | bytes 393224 | tf_op jit(solution)/shard_map/ppermute | solution.py:27
  68.1 7.1 %collective-permute-start.5 = (bf16[512,128]{1,0:T(8,128)(2,1)S(1)}, bf16[512,128]{1,0:T(8,128)(2,1)S(1)}, u32[]{:S(2)}, u32[]{:S(2)}) collective-permute-start(bf16[512,128]{1,0:T(8,128)(2,1)S(1)} %collective-permute-done.1.refs_2_), channel_id=1, source_target_pairs={{0,2},{2,0},{1,3},{3,1},{4,6},{6,4},{5,7},{7,5},{8,10},{10,8},{9,1... | collective-permute-start | bytes 393224 | tf_op jit(solution)/shard_map/ppermute | solution.py:27
  68.1 7.3 %collective-permute-start.4 = (bf16[512,128]{1,0:T(8,128)(2,1)S(1)}, bf16[512,128]{1,0:T(8,128)(2,1)S(1)}, u32[]{:S(2)}, u32[]{:S(2)}) collective-permute-start(bf16[512,128]{1,0:T(8,128)(2,1)S(1)} %collective-permute-done.refs_1_), channel_id=1, source_target_pairs={{0,2},{2,0},{1,3},{3,1},{4,6},{6,4},{5,7},{7,5},{8,10},{10,8},{9,1... | collective-permute-start | bytes 393224 | tf_op jit(solution)/shard_map/ppermute | solution.py:27
  69.4 16.1 %collective-permute-start.24 = (bf16[128,1024]{1,0:T(8,128)(2,1)S(1)}, bf16[128,1024]{1,0:T(8,128)(2,1)S(1)}, u32[]{:S(2)}, u32[]{:S(2)}) collective-permute-start(bf16[128,1024]{1,0:T(8,128)(2,1)S(1)} %constant_dynamic-update-slice_fusion.4.refs_15_), channel_id=1, source_target_pairs={{0,16},{16,32},{32,48},{48,0},{1,17},{17,33},{33,49},{49,1},{2,18}... | collective-permute-start | bytes 786440 | tf_op jit(solution)/shard_map/ppermute | solution.py:27
  71.9 13.6 %collective-permute-start.19 = (bf16[128,1024]{1,0:T(8,128)(2,1)S(1)}, bf16[128,1024]{1,0:T(8,128)(2,1)S(1)}, u32[]{:S(2)}, u32[]{:S(2)}) collective-permute-start(bf16[128,1024]{1,0:T(8,128)(2,1)S(1)} %collective-permute-done.8.refs_10_), channel_id=1, source_target_pairs={{0,64},{64,128},{128,192},{192,0},{1,65},{65,129},{129,193},{193,1... | collective-permute-start | bytes 786440 | tf_op jit(solution)/shard_map/ppermute | solution.py:27
  72.6 12.9 %collective-permute-start.21 = (bf16[128,1024]{1,0:T(8,128)(2,1)}, bf16[128,1024]{1,0:T(8,128)(2,1)S(1)}, u32[]{:S(2)}, u32[]{:S(2)}) collective-permute-start(bf16[128,1024]{1,0:T(8,128)(2,1)} %collective-permute-done.11.refs_12_), channel_id=1, source_target_pairs={{0,192},{64,0},{128,64},{192,128},{1,193},{65,1},{129,65},{193,129... | collective-permute-start | bytes 786440 | tf_op jit(solution)/shard_map/ppermute | solution.py:27
  75.2 10.4 %collective-permute-start.23 = (bf16[128,1024]{1,0:T(8,128)(2,1)}, bf16[128,1024]{1,0:T(8,128)(2,1)S(1)}, u32[]{:S(2)}, u32[]{:S(2)}) collective-permute-start(bf16[128,1024]{1,0:T(8,128)(2,1)} %collective-permute-done.14.refs_14_), channel_id=1, source_target_pairs={{0,16},{16,32},{32,48},{48,0},{1,17},{17,33},{33,49},{49,1},{2,18}... | collective-permute-start | bytes 786440 | tf_op jit(solution)/shard_map/ppermute | solution.py:27
  75.4 10.2 %collective-permute-start.25 = (bf16[128,1024]{1,0:T(8,128)(2,1)}, bf16[128,1024]{1,0:T(8,128)(2,1)S(1)}, u32[]{:S(2)}, u32[]{:S(2)}) collective-permute-start(bf16[128,1024]{1,0:T(8,128)(2,1)} %collective-permute-done.17.refs_16_), channel_id=1, source_target_pairs={{0,48},{16,0},{32,16},{48,32},{1,49},{17,1},{33,17},{49,33},{2,50}... | collective-permute-start | bytes 786440 | tf_op jit(solution)/shard_map/ppermute | solution.py:27
  77.2 0.9 copy-start
  85.5 0.7 copy-start.13
  85.5 0.8 copy-start.14
  85.5 0.9 copy-start.15
  85.6 0.9 copy-start.16
  85.6 1.0 copy-start.17
  91.5 1.5 collective-permute-start.26
  93.0 13.2 %collective-permute-start.29 = (f32[8,512]{1,0:T(8,128)S(1)}, f32[8,512]{1,0:T(8,128)S(1)}, u32[]{:S(2)}, u32[]{:S(2)}) collective-permute-start(f32[8,512]{1,0:T(8,128)S(1)} %pair.1.refs_0_), channel_id=1, source_target_pairs={{0,8},{4,12},{8,0},{12,4},{1,9},{5,13},{9,1},{13,5},{2,10},{6,14},... | collective-permute-start | bytes 49160 | tf_op jit(solution)/shard_map/ppermute | solution.py:27
  96.9 9.4 %collective-permute-start.28 = (f32[8,512]{1,0:T(8,128)S(1)}, f32[8,512]{1,0:T(8,128)S(1)}, u32[]{:S(2)}, u32[]{:S(2)}) collective-permute-start(f32[8,512]{1,0:T(8,128)S(1)} %pair.1.refs_0_), channel_id=1, source_target_pairs={{0,12},{4,0},{8,4},{12,8},{1,13},{5,1},{9,5},{13,9},{2,14},{6,2},{... | collective-permute-start | bytes 49160 | tf_op jit(solution)/shard_map/ppermute | solution.py:27
  97.9 8.3 %collective-permute-start.27 = (f32[8,512]{1,0:T(8,128)S(1)}, f32[8,512]{1,0:T(8,128)S(1)}, u32[]{:S(2)}, u32[]{:S(2)}) collective-permute-start(f32[8,512]{1,0:T(8,128)S(1)} %pair.1.refs_0_), channel_id=1, source_target_pairs={{0,4},{4,8},{8,12},{12,0},{1,5},{5,9},{9,13},{13,1},{2,6},{6,10},{... | collective-permute-start | bytes 49160 | tf_op jit(solution)/shard_map/ppermute | solution.py:27
  108.1 2.7 %collective-permute-start.30 = (f32[4,512,128]{2,1,0:T(8,128)S(1)}, f32[4,512,128]{2,1,0:T(8,128)S(1)}, u32[]{:S(2)}, u32[]{:S(2)}) collective-permute-start(f32[4,512,128]{2,1,0:T(8,128)S(1)} %get-tuple-element.23), channel_id=1, source_target_pairs={{0,2},{2,0},{1,3},{3,1},{4,6},{6,4},{5,7},{7,5},{8,10},{10,8},{9,1... | collective-permute-start | bytes 3145736 | tf_op jit(solution)/shard_map/ppermute | solution.py:27
  111.0 10.2 %collective-permute-start.33 = (bf16[512,128]{1,0:T(8,128)(2,1)S(1)}, bf16[512,128]{1,0:T(8,128)(2,1)S(1)}, u32[]{:S(2)}, u32[]{:S(2)}) collective-permute-start(bf16[512,128]{1,0:T(8,128)(2,1)S(1)} %get-tuple-element.26), channel_id=1, source_target_pairs={{0,8},{4,12},{8,0},{12,4},{1,9},{5,13},{9,1},{13,5},{2,10},{6,14},... | collective-permute-start | bytes 393224 | tf_op jit(solution)/shard_map/ppermute | solution.py:27
  113.5 14.5 %collective-permute-start.32 = (bf16[512,128]{1,0:T(8,128)(2,1)S(1)}, bf16[512,128]{1,0:T(8,128)(2,1)S(1)}, u32[]{:S(2)}, u32[]{:S(2)}) collective-permute-start(bf16[512,128]{1,0:T(8,128)(2,1)S(1)} %get-tuple-element.27), channel_id=1, source_target_pairs={{0,12},{4,0},{8,4},{12,8},{1,13},{5,1},{9,5},{13,9},{2,14},{6,2},{... | collective-permute-start | bytes 393224 | tf_op jit(solution)/shard_map/ppermute | solution.py:27
  117.6 10.3 %collective-permute-start.31 = (bf16[512,128]{1,0:T(8,128)(2,1)S(1)}, bf16[512,128]{1,0:T(8,128)(2,1)S(1)}, u32[]{:S(2)}, u32[]{:S(2)}) collective-permute-start(bf16[512,128]{1,0:T(8,128)(2,1)S(1)} %get-tuple-element.28), channel_id=1, source_target_pairs={{0,4},{4,8},{8,12},{12,0},{1,5},{5,9},{9,13},{13,1},{2,6},{6,10},{... | collective-permute-start | bytes 393224 | tf_op jit(solution)/shard_map/ppermute | solution.py:27
  155.2 5.6 %collective-permute-start.34 = (f32[320,128]{1,0:T(8,128)S(1)}, f32[320,128]{1,0:T(8,128)S(1)}, u32[]{:S(2)}, u32[]{:S(2)}) collective-permute-start(f32[320,128]{1,0:T(8,128)S(1)} %convert_reduce_fusion), channel_id=1, source_target_pairs={{0,1},{1,0},{2,3},{3,2},{4,5},{5,4},{6,7},{7,6},{8,9},{9,8},{10,11... | collective-permute-start | bytes 491528 | tf_op jit(solution)/shard_map/ppermute | solution.py:27

commit v5 on v4

--- a/solution.py
+++ b/solution.py
@@ -91,15 +91,6 @@
     return jnp.concatenate([*lines, spare], axis=0).T
 
 
-def column_copies(whole, held, sem, step):
-    copies = []
-    for k in range(whole.shape[1] // step):
-        here = pl.ds(k * step, step)
-        copies.append(pltpu.make_async_copy(whole.at[:, here], held.at[:, here], sem.at[k]))
-        copies[-1].start()
-    return copies
-
-
 def gate_kernel(in_ref, out_ref):
     out_ref[...] = in_ref[...]
 
@@ -107,6 +98,24 @@
 def spread_kernel(in_ref, out_ref):
     for k in range(out_ref.shape[0]):
         out_ref[k] = in_ref[...]
+
+
+def pull_kernel(in_ref, out_ref, sem):
+    copy = pltpu.make_async_copy(in_ref, out_ref, sem)
+    copy.start()
+    copy.wait()
+
+
+def pulled(x):
+    return pl.pallas_call(
+        pull_kernel,
+        out_shape=pltpu.VMEM(x.shape, x.dtype),
+        in_specs=[HBM],
+        out_specs=VMEM,
+        scratch_shapes=[pltpu.SemaphoreType.DMA],
+        compiler_params=pltpu.CompilerParams(vmem_limit_bytes=2 << 20),
+        cost_estimate=pl.CostEstimate(flops=0, bytes_accessed=2 * x.size * 2, transcendentals=0),
+    )(in_hbm(x))
 
 
 def sign_kernel(forget_ref, out_ref, sign, sem):
@@ -375,9 +384,8 @@
     scaled_blocks(soft_ref, hard_ref, factors, keep_ref, soft, hard, sem, which)
 
 
-def weight_kernel(images_ref, own_ref, one_ref, two_ref, three_ref, emb_ref, lines_ref, out_ref, held, sem):
+def weight_kernel(images_ref, own_ref, one_ref, two_ref, three_ref, emb_ref, lines_ref, out_ref):
     step = 1024
-    copies = column_copies(images_ref, held, sem, step)
     grad_unit = own_ref[...]
     for ref in (one_ref, two_ref, three_ref):
         grad_unit += ref[...].astype(f32)
@@ -386,10 +394,9 @@
     unit = emb_ref[...].astype(f32) * rnorm
     grad_emb = rnorm * (grad_unit - unit * radial)
     lines = grad_emb.T.astype(bf16)
-    for k, copy in enumerate(copies):
-        copy.wait()
+    for k in range(images_ref.shape[1] // step):
         here = pl.ds(k * step, step)
-        out_ref[here, :] = jnp.dot(lines, held[:, here], preferred_element_type=f32).T.astype(bf16)
+        out_ref[here, :] = jnp.dot(lines, images_ref[:, here], preferred_element_type=f32).T.astype(bf16)
 
 
 def local(images, img_weight, texts, pair_perm, forget):
@@ -585,11 +592,10 @@
         weight_kernel,
         name="weight",
         out_shape=jax.ShapeDtypeStruct((width, feats), bf16),
-        in_specs=[HBM, *[VMEM] * 6],
+        in_specs=[VMEM] * 7,
         out_specs=VMEM,
-        scratch_shapes=[pltpu.VMEM((rows, width), bf16), pltpu.SemaphoreType.DMA((width // 1024,))],
-        compiler_params=pltpu.CompilerParams(vmem_limit_bytes=16 << 20),
-    )(in_hbm(images), chip[0], *parts, emb, lines)
+        compiler_params=pltpu.CompilerParams(vmem_limit_bytes=8 << 20),
+    )(pulled(images), chip[0], *parts, emb, lines)
     summed = jnp.sum(exchanged(share.reshape(16, -1, feats), PLANE).astype(f32), axis=0)
     weight_grad = summed + shifted(summed, "tw", 1)
     return (pair_loss, weight_grad)

time: 163 us -> 162 us (level)
    pallas_call x0 -> x1, Pallas kernels: none -> 2.5 us  [pulled(): pl.pallas_call(pull_kernel, out_shape=pltpu.VMEM(x.shape, x.dtype), in_sp...]
    pallas_call x1, Pallas kernels: 3.54 us -> 1.26 us  [local(): pl.pallas_call(weight_kernel, name='weight', out_shape=jax.ShapeDtypeStru...]
  transfers between devices with their start and end apart: 36 -> 36, of which waited for: 10 -> 9; matrix products, arithmetic and copies ran while one was open for 0% -> 0% of each run, Pallas kernels for 12% -> 14%
where the time goes in v5:
time: 162 us; the launch traced here: 161 us
  starting transfers between devices  62.1 us (38%)
  waiting for transfers between devices  37.6 us (23%)
  Pallas kernels  31.8 us (20%)
  blocking collectives  23.5 us (15%)
  local copies, waits for them, and re-layouts  3.5 us (2%)
    ppermute x35, starting transfers between devices, shifted(): return lax.ppermute(x, axis, [(i, (i + step) % n) for i in range(n)])  54.6 us
    ppermute x35, waiting for transfers between devices, shifted(): return lax.ppermute(x, axis, [(i, (i + step) % n) for i in range(n)])  37.5 us
    all_to_all x1, blocking collectives, exchanged(): return lax.all_to_all(x, axis, 0, 0, tiled=True)  23.5 us
    all_to_all x1, starting transfers between devices, exchanged(): return lax.all_to_all(x, axis, 0, 0, tiled=True)  7.48 us
    pallas_call x1, Pallas kernels, local(): pl.pallas_call(lambda *refs: near_kernel(n, group, *refs), name='near', o...  7.34 us
    pallas_call x1, Pallas kernels, local(): pl.pallas_call(lambda *refs: far_gradient_kernel(m, group, *refs), name='...  6.43 us
    pallas_call x1, Pallas kernels, local(): pl.pallas_call(lambda *refs: far_score_kernel(m, group, *refs), name='far...  4.95 us
    pallas_call x1, Pallas kernels, local(): pl.pallas_call(embed_kernel, name='embed', out_shape=pltpu.HBM((rows, fea...  3.98 us
  transfers between devices with their start and end apart: 36, of which 9 were waited for; matrix products, arithmetic and copies ran while one was open for 0% of the time, Pallas kernels for 14%

profile of v5, /device:TPU:2, one launch (start us, length us, event | category | flops | bytes accessed | tf_op | source)
XLA Modules:
  0.0 160.6 jit_solution(6160261521587300933)
XLA Ops:
  0.6 0.9 copy-done.1
  1.5 1.3 spread.1
  2.8 7.5 %all-to-all-start = ((bf16[16,320,128]{2,1,0:T(8,128)(2,1)}), bf16[16,320,128]{2,1,0:T(8,128)(2,1)S(1)}, u32[]{:S(2)}, u32[]{:S(2)}) async-start(bf16[16,320,128]{2,1,0:T(8,128)(2,1)} %spread.1), calls=%async_computation | async-start | bytes 2621440 | tf_op jit(solution)/shard_map/all_to_all | solution.py:35
  10.3 2.0 %collective-permute-start.12 = (bf16[64,1024]{1,0:T(8,128)(2,1)S(1)}, bf16[64,1024]{1,0:T(8,128)(2,1)S(1)}, u32[]{:S(2)}, u32[]{:S(2)}) collective-permute-start(bf16[64,1024]{1,0:T(8,128)(2,1)S(1)} %copy-done.5), channel_id=1, source_target_pairs={{0,1},{1,0},{2,3},{3,2},{4,5},{5,4},{6,7},{7,6},{8,9},{9,8},{10,11... | collective-permute-start | bytes 393224 | tf_op jit(solution)/shard_map/ppermute | solution.py:27
  12.3 1.5 collective-permute-start.7
  13.7 0.6 collective-permute-start.9
  14.3 2.1 %collective-permute-start.10 = (bf16[64,1024]{1,0:T(8,128)(2,1)S(1)}, bf16[64,1024]{1,0:T(8,128)(2,1)S(1)}, u32[]{:S(2)}, u32[]{:S(2)}) collective-permute-start(bf16[64,1024]{1,0:T(8,128)(2,1)S(1)} %copy-done.5), channel_id=1, source_target_pairs={{0,32},{16,48},{32,0},{48,16},{1,33},{17,49},{33,1},{49,17},{2,34}... | collective-permute-start | bytes 393224 | tf_op jit(solution)/shard_map/ppermute | solution.py:27
  16.4 3.1 %collective-permute-start.16 = (bf16[64,1024]{1,0:T(8,128)(2,1)S(1)}, bf16[64,1024]{1,0:T(8,128)(2,1)S(1)}, u32[]{:S(2)}, u32[]{:S(2)}) collective-permute-start(bf16[64,1024]{1,0:T(8,128)(2,1)S(1)} %gate.1), channel_id=1, source_target_pairs={{0,128},{64,192},{128,0},{192,64},{1,129},{65,193},{129,1},{193,65... | collective-permute-start | bytes 393224 | tf_op jit(solution)/shard_map/ppermute | solution.py:27
  19.5 1.2 collective-permute-start.15
  20.6 10.7 %collective-permute-done.7 = bf16[64,1024]{1,0:T(8,128)(2,1)S(1)} collective-permute-done((bf16[64,1024]{1,0:T(8,128)(2,1)S(1)}, bf16[64,1024]{1,0:T(8,128)(2,1)S(1)}, u32[]{:S(2)}, u32[]{:S(2)}) %collective-permute-start.7) | collective-permute-done | bytes 131104 | tf_op jit(solution)/shard_map/ppermute | solution.py:27
  31.4 1.3 collective-permute-start.13
  32.7 2.1 %collective-permute-start.18 = (bf16[128,1024]{1,0:T(8,128)(2,1)S(1)}, bf16[128,1024]{1,0:T(8,128)(2,1)S(1)}, u32[]{:S(2)}, u32[]{:S(2)}) collective-permute-start(bf16[128,1024]{1,0:T(8,128)(2,1)S(1)} %constant_dynamic-update-slice_fusion.refs_9_), channel_id=1, source_target_pairs={{0,192},{64,0},{128,64},{192,128},{1,193},{65,1},{129,65},{193,129... | collective-permute-start | bytes 786440 | tf_op jit(solution)/shard_map/ppermute | solution.py:27
  34.7 0.1 collective-permute-start.8
  34.9 3.1 %collective-permute-done.13 = bf16[64,1024]{1,0:T(8,128)(2,1)S(1)} collective-permute-done((bf16[64,1024]{1,0:T(8,128)(2,1)S(1)}, bf16[64,1024]{1,0:T(8,128)(2,1)S(1)}, u32[]{:S(2)}, u32[]{:S(2)}) %collective-permute-start.13) | collective-permute-done | bytes 131104 | tf_op jit(solution)/shard_map/ppermute | solution.py:27
  38.0 0.9 collective-permute-start.20
  39.0 2.4 %collective-permute-start.11 = (bf16[128,1024]{1,0:T(8,128)(2,1)S(1)}, bf16[128,1024]{1,0:T(8,128)(2,1)}, u32[]{:S(2)}, u32[]{:S(2)}) collective-permute-start(bf16[128,1024]{1,0:T(8,128)(2,1)S(1)} %constant_dynamic-update-slice_fusion.2.refs_11_), channel_id=1, source_target_pairs={{0,192},{64,0},{128,64},{192,128},{1,193},{65,1},{129,65},{193,129... | collective-permute-start | bytes 786440 | tf_op jit(solution)/shard_map/ppermute | solution.py:27
  41.4 0.4 collective-permute-start.22
  41.8 2.2 %collective-permute-start.14 = (bf16[128,1024]{1,0:T(8,128)(2,1)S(1)}, bf16[128,1024]{1,0:T(8,128)(2,1)}, u32[]{:S(2)}, u32[]{:S(2)}) collective-permute-start(bf16[128,1024]{1,0:T(8,128)(2,1)S(1)} %pad_maximum_fusion.refs_13_), channel_id=1, source_target_pairs={{0,16},{16,32},{32,48},{48,0},{1,17},{17,33},{33,49},{49,1},{2,18}... | collective-permute-start | bytes 786440 | tf_op jit(solution)/shard_map/ppermute | solution.py:27
  44.1 1.1 collective-permute-done.8.refs_10_
  45.2 0.8 collective-permute-start.17
  46.0 4.0 %embed.1.refs_0_.emb_ref = bf16[512,128]{1,0:T(8,128)(2,1)} custom-call(bf16[512,5120]{1,0:T(8,128)(2,1)} %in_ref.3, bf16[5120,128]{1,0:T(8,128)(2,1)S(1)} %bitcast.13), custom_call_target="tpu_custom_call" | custom-call | flops 671088640 | bytes 7340032 | tf_op jit(solution)/shard_map/embed/pallas_call | solution.py:447
  50.0 7.3 %collective-permute-start.2 = (bf16[512,128]{1,0:T(8,128)(2,1)}, bf16[512,128]{1,0:T(8,128)(2,1)S(1)}, u32[]{:S(2)}, u32[]{:S(2)}) collective-permute-start(bf16[512,128]{1,0:T(8,128)(2,1)} %embed.1.refs_0_.emb_ref), channel_id=1, source_target_pairs={{0,8},{4,12},{8,0},{12,4},{1,9},{5,13},{9,1},{13,5},{2,10},{6,14},... | collective-permute-start | bytes 393224 | tf_op jit(solution)/shard_map/ppermute | solution.py:27
  57.3 0.0 collective-permute-start.1
  57.3 2.9 %collective-permute-start = (bf16[512,128]{1,0:T(8,128)(2,1)}, bf16[512,128]{1,0:T(8,128)(2,1)S(1)}, u32[]{:S(2)}, u32[]{:S(2)}) collective-permute-start(bf16[512,128]{1,0:T(8,128)(2,1)} %embed.1.refs_0_.emb_ref), channel_id=1, source_target_pairs={{0,4},{4,8},{8,12},{12,0},{1,5},{5,9},{9,13},{13,1},{2,6},{6,10},{... | collective-permute-start | bytes 393224 | tf_op jit(solution)/shard_map/ppermute | solution.py:27
  60.2 1.9 %collective-permute-done.2.refs_3_ = bf16[512,128]{1,0:T(8,128)(2,1)S(1)} collective-permute-done((bf16[512,128]{1,0:T(8,128)(2,1)}, bf16[512,128]{1,0:T(8,128)(2,1)S(1)}, u32[]{:S(2)}, u32[]{:S(2)}) %collective-permute-start.2) | collective-permute-done | bytes 131104 | tf_op jit(solution)/shard_map/ppermute | solution.py:27
  62.1 5.8 %collective-permute-done.1.refs_2_ = bf16[512,128]{1,0:T(8,128)(2,1)S(1)} collective-permute-done((bf16[512,128]{1,0:T(8,128)(2,1)}, bf16[512,128]{1,0:T(8,128)(2,1)S(1)}, u32[]{:S(2)}, u32[]{:S(2)}) %collective-permute-start.1) | collective-permute-done | bytes 131104 | tf_op jit(solution)/shard_map/ppermute | solution.py:27
  68.0 0.5 collective-permute-start.4
  68.5 0.6 signs.1.refs_3_
  69.1 0.1 places.1.refs_8_.refs_1_.refs_0_
  69.2 2.6 %collective-permute-start.24 = (bf16[128,1024]{1,0:T(8,128)(2,1)S(1)}, bf16[128,1024]{1,0:T(8,128)(2,1)S(1)}, u32[]{:S(2)}, u32[]{:S(2)}) collective-permute-start(bf16[128,1024]{1,0:T(8,128)(2,1)S(1)} %constant_dynamic-update-slice_fusion.4.refs_15_), channel_id=1, source_target_pairs={{0,16},{16,32},{32,48},{48,0},{1,17},{17,33},{33,49},{49,1},{2,18}... | collective-permute-start | bytes 786440 | tf_op jit(solution)/shard_map/ppermute | solution.py:27
  71.8 0.7 collective-permute-start.19
  72.5 2.5 %collective-permute-start.21 = (bf16[128,1024]{1,0:T(8,128)(2,1)}, bf16[128,1024]{1,0:T(8,128)(2,1)S(1)}, u32[]{:S(2)}, u32[]{:S(2)}) collective-permute-start(bf16[128,1024]{1,0:T(8,128)(2,1)} %collective-permute-done.11.refs_12_), channel_id=1, source_target_pairs={{0,192},{64,0},{128,64},{192,128},{1,193},{65,1},{129,65},{193,129... | collective-permute-start | bytes 786440 | tf_op jit(solution)/shard_map/ppermute | solution.py:27
  75.1 0.2 collective-permute-start.23
  75.2 1.9 %collective-permute-start.25 = (bf16[128,1024]{1,0:T(8,128)(2,1)}, bf16[128,1024]{1,0:T(8,128)(2,1)S(1)}, u32[]{:S(2)}, u32[]{:S(2)}) collective-permute-start(bf16[128,1024]{1,0:T(8,128)(2,1)} %collective-permute-done.17.refs_16_), channel_id=1, source_target_pairs={{0,48},{16,0},{32,16},{48,32},{1,49},{17,1},{33,17},{49,33},{2,50}... | collective-permute-start | bytes 786440 | tf_op jit(solution)/shard_map/ppermute | solution.py:27
  77.1 0.9 copy-done
  78.0 7.3 %near.1 = (f32[512,1024]{1,0:T(8,128)}, bf16[512,1024]{1,0:T(8,128)(2,1)}, f32[8,512]{1,0:T(8,128)S(1)}, bf16[512,1024]{1,0:T(8,128)(2,1)S(1)}) custom-call(bf16[512,128]{1,0:T(8,128)(2,1)S(1)} %copy-done, bf16[512,128]{1,0:T(8,128)(2,1)S(1)} %collective-permute-done.refs_1_, bf16[512,128]{1,0:T(8,128)(2,1)S(1)} %collective-permute-done.1.refs_2_, ...), custom_call_target="tpu_custom_call" | custom-call | flops 3221225472 | bytes 4194304 | tf_op jit(solution)/shard_map/near/pallas_call | solution.py:475
  85.5 0.6 copy-done.13
  86.1 0.1 copy-done.14
  86.2 0.1 copy-done.15
  86.3 0.0 copy-done.16
  86.4 0.1 copy-done.17
  86.4 4.9 %far_scores.1 = (bf16[512,1024]{1,0:T(8,128)(2,1)}, f32[8,512]{1,0:T(8,128)}, f32[8,512]{1,0:T(8,128)S(1)}) custom-call(bf16[512,1024]{1,0:T(8,128)(2,1)S(1)} %get-tuple-element.13.refs_0_, s32[512,1]{1,0:T(8,128)S(1)} %places.1.refs_8_.refs_1_.refs_0_, f32[8,512]{1,0:T(8,128)S(1)} %get-tuple-element.14.refs_2_, f32[1,512]{1,0:T(1,128)} %signs.1.refs_3_, ...), custom_call_target="tpu_custom_call" | custom-call | flops 1073741824 | bytes 4194304 | tf_op jit(solution)/shard_map/far_scores/pallas_call | solution.py:498
  91.4 0.3 collective-permute-start.26
  91.7 1.2 collective-permute-done.26.theirs_ref
  92.9 3.8 %collective-permute-start.29 = (f32[8,512]{1,0:T(8,128)S(1)}, f32[8,512]{1,0:T(8,128)S(1)}, u32[]{:S(2)}, u32[]{:S(2)}) collective-permute-start(f32[8,512]{1,0:T(8,128)S(1)} %pair.1.refs_0_), channel_id=1, source_target_pairs={{0,8},{4,12},{8,0},{12,4},{1,9},{5,13},{9,1},{13,5},{2,10},{6,14},... | collective-permute-start | bytes 49160 | tf_op jit(solution)/shard_map/ppermute | solution.py:27
  96.7 1.1 collective-permute-start.28
  97.8 1.8 %collective-permute-start.27 = (f32[8,512]{1,0:T(8,128)S(1)}, f32[8,512]{1,0:T(8,128)S(1)}, u32[]{:S(2)}, u32[]{:S(2)}) collective-permute-start(f32[8,512]{1,0:T(8,128)S(1)} %pair.1.refs_0_), channel_id=1, source_target_pairs={{0,4},{4,8},{8,12},{12,0},{1,5},{5,9},{9,13},{13,1},{2,6},{6,10},{... | collective-permute-start | bytes 49160 | tf_op jit(solution)/shard_map/ppermute | solution.py:27
  99.6 6.4 %far_gradient.1 = (f32[512,1024]{1,0:T(8,128)}, bf16[512,1024]{1,0:T(8,128)(2,1)}) custom-call(s32[512,1]{1,0:T(8,128)S(1)} %places.1.refs_8_.refs_1_.refs_0_, bf16[512,1024]{1,0:T(8,128)(2,1)} %get-tuple-element.17.refs_1_, f32[8,512]{1,0:T(8,128)} %get-tuple-element.16.refs_2_.refs_4_, f32[512,1024]{1,0:T(8,128)} %get-tuple-element.18.refs_3_, ...), custom_call_target="tpu_custom_call" | custom-call | flops 2147483648 | bytes 4194304 | tf_op jit(solution)/shard_map/far_gradient/pallas_call | solution.py:532
  106.1 1.8 %give.1 = (f32[4,512,128]{2,1,0:T(8,128)S(1)}, f32[8,512]{1,0:T(8,128)S(1)}) custom-call(f32[8,512]{1,0:T(8,128)S(1)} %pair.1.refs_0_, f32[8,512]{1,0:T(8,128)S(1)} %collective-permute-done.27.refs_1_, f32[8,512]{1,0:T(8,128)S(1)} %collective-permute-done.28.refs_2_, f32[8,512]{1,0:T(8,128)S(1)} %collective-permute-done.29.refs_3_, ...), custom_call_target="tpu_custom_call" | custom-call | tf_op jit(solution)/shard_map/give/pallas_call | solution.py:559
  107.9 0.1 collective-permute-start.30
  108.0 2.5 %shard_map.68.images_ref = bf16[512,5120]{1,0:T(8,128)(2,1)S(1)} custom-call(bf16[512,5120]{1,0:T(8,128)(2,1)} %in_ref.3), custom_call_target="tpu_custom_call" | custom-call | bytes 10485760 | tf_op jit(solution)/shard_map/pallas_call | solution.py:110
  110.5 1.5 keep.1
  112.1 0.1 fusion
  112.2 2.5 %collective-permute-start.33 = (bf16[512,128]{1,0:T(8,128)(2,1)S(1)}, bf16[512,128]{1,0:T(8,128)(2,1)S(1)}, u32[]{:S(2)}, u32[]{:S(2)}) collective-permute-start(bf16[512,128]{1,0:T(8,128)(2,1)S(1)} %get-tuple-element.26), channel_id=1, source_target_pairs={{0,8},{4,12},{8,0},{12,4},{1,9},{5,13},{9,1},{13,5},{2,10},{6,14},... | collective-permute-start | bytes 393224 | tf_op jit(solution)/shard_map/ppermute | solution.py:27
  114.7 4.1 %collective-permute-start.32 = (bf16[512,128]{1,0:T(8,128)(2,1)S(1)}, bf16[512,128]{1,0:T(8,128)(2,1)S(1)}, u32[]{:S(2)}, u32[]{:S(2)}) collective-permute-start(bf16[512,128]{1,0:T(8,128)(2,1)S(1)} %get-tuple-element.27), channel_id=1, source_target_pairs={{0,12},{4,0},{8,4},{12,8},{1,13},{5,1},{9,5},{13,9},{2,14},{6,2},{... | collective-permute-start | bytes 393224 | tf_op jit(solution)/shard_map/ppermute | solution.py:27
  118.9 3.9 %collective-permute-done.33.three_ref = bf16[512,128]{1,0:T(8,128)(2,1)S(1)} collective-permute-done((bf16[512,128]{1,0:T(8,128)(2,1)S(1)}, bf16[512,128]{1,0:T(8,128)(2,1)S(1)}, u32[]{:S(2)}, u32[]{:S(2)}) %collective-permute-start.33) | collective-permute-done | bytes 131104 | tf_op jit(solution)/shard_map/ppermute | solution.py:27
  122.8 6.8 %collective-permute-done.32.two_ref = bf16[512,128]{1,0:T(8,128)(2,1)S(1)} collective-permute-done((bf16[512,128]{1,0:T(8,128)(2,1)S(1)}, bf16[512,128]{1,0:T(8,128)(2,1)S(1)}, u32[]{:S(2)}, u32[]{:S(2)}) %collective-permute-start.32) | collective-permute-done | bytes 131104 | tf_op jit(solution)/shard_map/ppermute | solution.py:27
  129.6 1.3 weight.1
  130.8 23.5 %all_to_all.10 = bf16[16,320,128]{2,1,0:T(8,128)(2,1)S(1)} all-to-all(bf16[16,320,128]{2,1,0:T(8,128)(2,1)S(1)} %bitcast.14), channel_id=1, replica_groups=mesh['y'=4,'x'=4,'zh'=4,'core'=2,'tw'=2] {'y','x'}, dimensions={0} | all-to-all | bytes 2621440 | tf_op jit(solution)/shard_map/all_to_all | solution.py:35
  154.3 0.2 convert_reduce_fusion
  154.5 1.9 %collective-permute-start.34 = (f32[320,128]{1,0:T(8,128)S(1)}, f32[320,128]{1,0:T(8,128)S(1)}, u32[]{:S(2)}, u32[]{:S(2)}) collective-permute-start(f32[320,128]{1,0:T(8,128)S(1)} %convert_reduce_fusion), channel_id=1, source_target_pairs={{0,1},{1,0},{2,3},{3,2},{4,5},{5,4},{6,7},{7,6},{8,9},{9,8},{10,11... | collective-permute-start | bytes 491528 | tf_op jit(solution)/shard_map/ppermute | solution.py:27
  156.4 0.6 slice.18
  156.9 3.0 %collective-permute-done.34 = f32[320,128]{1,0:T(8,128)S(1)} collective-permute-done((f32[320,128]{1,0:T(8,128)S(1)}, f32[320,128]{1,0:T(8,128)S(1)}, u32[]{:S(2)}, u32[]{:S(2)}) %collective-permute-start.34) | collective-permute-done | bytes 163872 | tf_op jit(solution)/shard_map/ppermute | solution.py:27
  159.9 0.7 add.7
  (71 shorter events, 0.3 us)
Async XLA Ops:
  0.6 0.9 copy-start.1
  1.5 8.8 %copy-start.5 = (bf16[64,1024]{1,0:T(8,128)(2,1)S(1)}, bf16[64,1024]{1,0:T(8,128)(2,1)}, u32[]{:S(2)}) copy-start(bf16[64,1024]{1,0:T(8,128)(2,1)} %param.7) | copy-start | bytes 393220
  2.8 43.2 %all-to-all-start = ((bf16[16,320,128]{2,1,0:T(8,128)(2,1)}), bf16[16,320,128]{2,1,0:T(8,128)(2,1)S(1)}, u32[]{:S(2)}, u32[]{:S(2)}) async-start(bf16[16,320,128]{2,1,0:T(8,128)(2,1)} %spread.1), calls=%async_computation | async-start | bytes 2621440 | tf_op jit(solution)/shard_map/all_to_all | solution.py:35
  10.3 6.1 %collective-permute-start.12 = (bf16[64,1024]{1,0:T(8,128)(2,1)S(1)}, bf16[64,1024]{1,0:T(8,128)(2,1)S(1)}, u32[]{:S(2)}, u32[]{:S(2)}) collective-permute-start(bf16[64,1024]{1,0:T(8,128)(2,1)S(1)} %copy-done.5), channel_id=1, source_target_pairs={{0,1},{1,0},{2,3},{3,2},{4,5},{5,4},{6,7},{7,6},{8,9},{9,8},{10,11... | collective-permute-start | bytes 393224 | tf_op jit(solution)/shard_map/ppermute | solution.py:27
  12.3 19.1 %collective-permute-start.7 = (bf16[64,1024]{1,0:T(8,128)(2,1)S(1)}, bf16[64,1024]{1,0:T(8,128)(2,1)S(1)}, u32[]{:S(2)}, u32[]{:S(2)}) collective-permute-start(bf16[64,1024]{1,0:T(8,128)(2,1)S(1)} %copy-done.5), channel_id=1, source_target_pairs={{0,16},{16,32},{32,48},{48,0},{1,17},{17,33},{33,49},{49,1},{2,18}... | collective-permute-start | bytes 393224 | tf_op jit(solution)/shard_map/ppermute | solution.py:27
  13.7 18.9 %collective-permute-start.9 = (bf16[64,1024]{1,0:T(8,128)(2,1)S(1)}, bf16[64,1024]{1,0:T(8,128)(2,1)S(1)}, u32[]{:S(2)}, u32[]{:S(2)}) collective-permute-start(bf16[64,1024]{1,0:T(8,128)(2,1)S(1)} %copy-done.5), channel_id=1, source_target_pairs={{0,48},{16,0},{32,16},{48,32},{1,49},{17,1},{33,17},{49,33},{2,50}... | collective-permute-start | bytes 393224 | tf_op jit(solution)/shard_map/ppermute | solution.py:27
  14.3 20.4 %collective-permute-start.10 = (bf16[64,1024]{1,0:T(8,128)(2,1)S(1)}, bf16[64,1024]{1,0:T(8,128)(2,1)S(1)}, u32[]{:S(2)}, u32[]{:S(2)}) collective-permute-start(bf16[64,1024]{1,0:T(8,128)(2,1)S(1)} %copy-done.5), channel_id=1, source_target_pairs={{0,32},{16,48},{32,0},{48,16},{1,33},{17,49},{33,1},{49,17},{2,34}... | collective-permute-start | bytes 393224 | tf_op jit(solution)/shard_map/ppermute | solution.py:27
  16.4 22.5 %collective-permute-start.16 = (bf16[64,1024]{1,0:T(8,128)(2,1)S(1)}, bf16[64,1024]{1,0:T(8,128)(2,1)S(1)}, u32[]{:S(2)}, u32[]{:S(2)}) collective-permute-start(bf16[64,1024]{1,0:T(8,128)(2,1)S(1)} %gate.1), channel_id=1, source_target_pairs={{0,128},{64,192},{128,0},{192,64},{1,129},{65,193},{129,1},{193,65... | collective-permute-start | bytes 393224 | tf_op jit(solution)/shard_map/ppermute | solution.py:27
  19.5 21.9 %collective-permute-start.15 = (bf16[64,1024]{1,0:T(8,128)(2,1)S(1)}, bf16[64,1024]{1,0:T(8,128)(2,1)S(1)}, u32[]{:S(2)}, u32[]{:S(2)}) collective-permute-start(bf16[64,1024]{1,0:T(8,128)(2,1)S(1)} %gate.1), channel_id=1, source_target_pairs={{0,192},{64,0},{128,64},{192,128},{1,193},{65,1},{129,65},{193,129... | collective-permute-start | bytes 393224 | tf_op jit(solution)/shard_map/ppermute | solution.py:27
  31.4 6.6 %collective-permute-start.13 = (bf16[64,1024]{1,0:T(8,128)(2,1)S(1)}, bf16[64,1024]{1,0:T(8,128)(2,1)S(1)}, u32[]{:S(2)}, u32[]{:S(2)}) collective-permute-start(bf16[64,1024]{1,0:T(8,128)(2,1)S(1)} %gate.1), channel_id=1, source_target_pairs={{0,64},{64,128},{128,192},{192,0},{1,65},{65,129},{129,193},{193,1... | collective-permute-start | bytes 393224 | tf_op jit(solution)/shard_map/ppermute | solution.py:27
  32.6 17.3 %copy-start.6 = (bf16[128,1024]{1,0:T(8,128)(2,1)}, bf16[128,1024]{1,0:T(8,128)(2,1)S(1)}, u32[]{:S(2)}) copy-start(bf16[128,1024]{1,0:T(8,128)(2,1)S(1)} %constant_dynamic-update-slice_fusion.refs_9_) | copy-start | bytes 786436
  32.7 9.1 %collective-permute-start.18 = (bf16[128,1024]{1,0:T(8,128)(2,1)S(1)}, bf16[128,1024]{1,0:T(8,128)(2,1)S(1)}, u32[]{:S(2)}, u32[]{:S(2)}) collective-permute-start(bf16[128,1024]{1,0:T(8,128)(2,1)S(1)} %constant_dynamic-update-slice_fusion.refs_9_), channel_id=1, source_target_pairs={{0,192},{64,0},{128,64},{192,128},{1,193},{65,1},{129,65},{193,129... | collective-permute-start | bytes 786440 | tf_op jit(solution)/shard_map/ppermute | solution.py:27
  34.7 10.5 %collective-permute-start.8 = (bf16[128,1024]{1,0:T(8,128)(2,1)S(1)}, bf16[128,1024]{1,0:T(8,128)(2,1)S(1)}, u32[]{:S(2)}, u32[]{:S(2)}) collective-permute-start(bf16[128,1024]{1,0:T(8,128)(2,1)S(1)} %constant_dynamic-update-slice_fusion.refs_9_), channel_id=1, source_target_pairs={{0,64},{64,128},{128,192},{192,0},{1,65},{65,129},{129,193},{193,1... | collective-permute-start | bytes 786440 | tf_op jit(solution)/shard_map/ppermute | solution.py:27
  34.9 15.1 %copy-start.7 = (bf16[128,1024]{1,0:T(8,128)(2,1)}, bf16[128,1024]{1,0:T(8,128)(2,1)S(1)}, u32[]{:S(2)}) copy-start(bf16[128,1024]{1,0:T(8,128)(2,1)S(1)} %constant_dynamic-update-slice_fusion.2.refs_11_) | copy-start | bytes 786436
  38.0 12.0 %collective-permute-start.20 = (bf16[128,1024]{1,0:T(8,128)(2,1)S(1)}, bf16[128,1024]{1,0:T(8,128)(2,1)S(1)}, u32[]{:S(2)}, u32[]{:S(2)}) collective-permute-start(bf16[128,1024]{1,0:T(8,128)(2,1)S(1)} %constant_dynamic-update-slice_fusion.2.refs_11_), channel_id=1, source_target_pairs={{0,64},{64,128},{128,192},{192,0},{1,65},{65,129},{129,193},{193,1... | collective-permute-start | bytes 786440 | tf_op jit(solution)/shard_map/ppermute | solution.py:27
  38.9 11.0 %copy-start.4 = (bf16[128,1024]{1,0:T(8,128)(2,1)}, bf16[128,1024]{1,0:T(8,128)(2,1)S(1)}, u32[]{:S(2)}) copy-start(bf16[128,1024]{1,0:T(8,128)(2,1)S(1)} %pad_maximum_fusion.refs_13_) | copy-start | bytes 786436
  39.0 18.3 %collective-permute-start.11 = (bf16[128,1024]{1,0:T(8,128)(2,1)S(1)}, bf16[128,1024]{1,0:T(8,128)(2,1)}, u32[]{:S(2)}, u32[]{:S(2)}) collective-permute-start(bf16[128,1024]{1,0:T(8,128)(2,1)S(1)} %constant_dynamic-update-slice_fusion.2.refs_11_), channel_id=1, source_target_pairs={{0,192},{64,0},{128,64},{192,128},{1,193},{65,1},{129,65},{193,129... | collective-permute-start | bytes 786440 | tf_op jit(solution)/shard_map/ppermute | solution.py:27
  41.4 15.9 %collective-permute-start.22 = (bf16[128,1024]{1,0:T(8,128)(2,1)S(1)}, bf16[128,1024]{1,0:T(8,128)(2,1)S(1)}, u32[]{:S(2)}, u32[]{:S(2)}) collective-permute-start(bf16[128,1024]{1,0:T(8,128)(2,1)S(1)} %pad_maximum_fusion.refs_13_), channel_id=1, source_target_pairs={{0,48},{16,0},{32,16},{48,32},{1,49},{17,1},{33,17},{49,33},{2,50}... | collective-permute-start | bytes 786440 | tf_op jit(solution)/shard_map/ppermute | solution.py:27
  41.8 8.2 %copy-start.9 = (bf16[128,1024]{1,0:T(8,128)(2,1)}, bf16[128,1024]{1,0:T(8,128)(2,1)S(1)}, u32[]{:S(2)}) copy-start(bf16[128,1024]{1,0:T(8,128)(2,1)S(1)} %collective-permute-done.18.refs_4_.refs_5_) | copy-start | bytes 786436
  41.8 18.4 %collective-permute-start.14 = (bf16[128,1024]{1,0:T(8,128)(2,1)S(1)}, bf16[128,1024]{1,0:T(8,128)(2,1)}, u32[]{:S(2)}, u32[]{:S(2)}) collective-permute-start(bf16[128,1024]{1,0:T(8,128)(2,1)S(1)} %pad_maximum_fusion.refs_13_), channel_id=1, source_target_pairs={{0,16},{16,32},{32,48},{48,0},{1,17},{17,33},{33,49},{49,1},{2,18}... | collective-permute-start | bytes 786440 | tf_op jit(solution)/shard_map/ppermute | solution.py:27
  44.1 25.2 %copy-start.8 = (bf16[128,1024]{1,0:T(8,128)(2,1)}, bf16[128,1024]{1,0:T(8,128)(2,1)S(1)}, u32[]{:S(2)}) copy-start(bf16[128,1024]{1,0:T(8,128)(2,1)S(1)} %constant_dynamic-update-slice_fusion.4.refs_15_) | copy-start | bytes 786436
  45.2 26.6 %copy-start.12 = (bf16[128,1024]{1,0:T(8,128)(2,1)}, bf16[128,1024]{1,0:T(8,128)(2,1)S(1)}, u32[]{:S(2)}) copy-start(bf16[128,1024]{1,0:T(8,128)(2,1)S(1)} %collective-permute-done.8.refs_10_) | copy-start | bytes 786436
  45.2 24.0 %collective-permute-start.17 = (bf16[128,1024]{1,0:T(8,128)(2,1)S(1)}, bf16[128,1024]{1,0:T(8,128)(2,1)}, u32[]{:S(2)}, u32[]{:S(2)}) collective-permute-start(bf16[128,1024]{1,0:T(8,128)(2,1)S(1)} %constant_dynamic-update-slice_fusion.4.refs_15_), channel_id=1, source_target_pairs={{0,48},{16,0},{32,16},{48,32},{1,49},{17,1},{33,17},{49,33},{2,50}... | collective-permute-start | bytes 786440 | tf_op jit(solution)/shard_map/ppermute | solution.py:27
  46.0 22.5 %copy-start.3 = (s32[512]{0:T(512)S(1)}, s32[512]{0:T(512)}, u32[]{:S(2)}) copy-start(s32[512]{0:T(512)} %param.9) | copy-start | bytes 6148
  46.0 23.1 %copy-start.2 = (s32[512]{0:T(512)S(1)}, s32[512]{0:T(512)}, u32[]{:S(2)}) copy-start(s32[512]{0:T(512)} %param.8) | copy-start | bytes 6148
  50.0 35.3 %copy-start.10 = (bf16[128,1024]{1,0:T(8,128)(2,1)}, bf16[128,1024]{1,0:T(8,128)(2,1)S(1)}, u32[]{:S(2)}) copy-start(bf16[128,1024]{1,0:T(8,128)(2,1)S(1)} %collective-permute-done.20.refs_6_.refs_7_) | copy-start | bytes 786436
  50.0 12.1 %collective-permute-start.2 = (bf16[512,128]{1,0:T(8,128)(2,1)}, bf16[512,128]{1,0:T(8,128)(2,1)S(1)}, u32[]{:S(2)}, u32[]{:S(2)}) collective-permute-start(bf16[512,128]{1,0:T(8,128)(2,1)} %embed.1.refs_0_.emb_ref), channel_id=1, source_target_pairs={{0,8},{4,12},{8,0},{12,4},{1,9},{5,13},{9,1},{13,5},{2,10},{6,14},... | collective-permute-start | bytes 393224 | tf_op jit(solution)/shard_map/ppermute | solution.py:27
  57.3 10.7 %collective-permute-start.1 = (bf16[512,128]{1,0:T(8,128)(2,1)}, bf16[512,128]{1,0:T(8,128)(2,1)S(1)}, u32[]{:S(2)}, u32[]{:S(2)}) collective-permute-start(bf16[512,128]{1,0:T(8,128)(2,1)} %embed.1.refs_0_.emb_ref), channel_id=1, source_target_pairs={{0,12},{4,0},{8,4},{12,8},{1,13},{5,1},{9,5},{13,9},{2,14},{6,2},{... | collective-permute-start | bytes 393224 | tf_op jit(solution)/shard_map/ppermute | solution.py:27
  57.3 28.0 %copy-start.11 = (bf16[128,1024]{1,0:T(8,128)(2,1)}, bf16[128,1024]{1,0:T(8,128)(2,1)S(1)}, u32[]{:S(2)}) copy-start(bf16[128,1024]{1,0:T(8,128)(2,1)S(1)} %collective-permute-done.22.refs_8_.refs_9_) | copy-start | bytes 786436
  57.3 10.6 %collective-permute-start = (bf16[512,128]{1,0:T(8,128)(2,1)}, bf16[512,128]{1,0:T(8,128)(2,1)S(1)}, u32[]{:S(2)}, u32[]{:S(2)}) collective-permute-start(bf16[512,128]{1,0:T(8,128)(2,1)} %embed.1.refs_0_.emb_ref), channel_id=1, source_target_pairs={{0,4},{4,8},{8,12},{12,0},{1,5},{5,9},{9,13},{13,1},{2,6},{6,10},{... | collective-permute-start | bytes 393224 | tf_op jit(solution)/shard_map/ppermute | solution.py:27
  60.2 11.6 %collective-permute-start.3 = (bf16[512,128]{1,0:T(8,128)(2,1)}, bf16[512,128]{1,0:T(8,128)(2,1)S(1)}, u32[]{:S(2)}, u32[]{:S(2)}) collective-permute-start(bf16[512,128]{1,0:T(8,128)(2,1)} %embed.1.refs_0_.emb_ref), channel_id=1, source_target_pairs={{0,2},{2,0},{1,3},{3,1},{4,6},{6,4},{5,7},{7,5},{8,10},{10,8},{9,1... | collective-permute-start | bytes 393224 | tf_op jit(solution)/shard_map/ppermute | solution.py:27
  62.1 10.4 %collective-permute-start.6 = (bf16[512,128]{1,0:T(8,128)(2,1)S(1)}, bf16[512,128]{1,0:T(8,128)(2,1)S(1)}, u32[]{:S(2)}, u32[]{:S(2)}) collective-permute-start(bf16[512,128]{1,0:T(8,128)(2,1)S(1)} %collective-permute-done.2.refs_3_), channel_id=1, source_target_pairs={{0,2},{2,0},{1,3},{3,1},{4,6},{6,4},{5,7},{7,5},{8,10},{10,8},{9,1... | collective-permute-start | bytes 393224 | tf_op jit(solution)/shard_map/ppermute | solution.py:27
  68.0 7.1 %collective-permute-start.5 = (bf16[512,128]{1,0:T(8,128)(2,1)S(1)}, bf16[512,128]{1,0:T(8,128)(2,1)S(1)}, u32[]{:S(2)}, u32[]{:S(2)}) collective-permute-start(bf16[512,128]{1,0:T(8,128)(2,1)S(1)} %collective-permute-done.1.refs_2_), channel_id=1, source_target_pairs={{0,2},{2,0},{1,3},{3,1},{4,6},{6,4},{5,7},{7,5},{8,10},{10,8},{9,1... | collective-permute-start | bytes 393224 | tf_op jit(solution)/shard_map/ppermute | solution.py:27
  68.0 7.3 %collective-permute-start.4 = (bf16[512,128]{1,0:T(8,128)(2,1)S(1)}, bf16[512,128]{1,0:T(8,128)(2,1)S(1)}, u32[]{:S(2)}, u32[]{:S(2)}) collective-permute-start(bf16[512,128]{1,0:T(8,128)(2,1)S(1)} %collective-permute-done.refs_1_), channel_id=1, source_target_pairs={{0,2},{2,0},{1,3},{3,1},{4,6},{6,4},{5,7},{7,5},{8,10},{10,8},{9,1... | collective-permute-start | bytes 393224 | tf_op jit(solution)/shard_map/ppermute | solution.py:27
  69.2 16.1 %collective-permute-start.24 = (bf16[128,1024]{1,0:T(8,128)(2,1)S(1)}, bf16[128,1024]{1,0:T(8,128)(2,1)S(1)}, u32[]{:S(2)}, u32[]{:S(2)}) collective-permute-start(bf16[128,1024]{1,0:T(8,128)(2,1)S(1)} %constant_dynamic-update-slice_fusion.4.refs_15_), channel_id=1, source_target_pairs={{0,16},{16,32},{32,48},{48,0},{1,17},{17,33},{33,49},{49,1},{2,18}... | collective-permute-start | bytes 786440 | tf_op jit(solution)/shard_map/ppermute | solution.py:27
  71.8 13.6 %collective-permute-start.19 = (bf16[128,1024]{1,0:T(8,128)(2,1)S(1)}, bf16[128,1024]{1,0:T(8,128)(2,1)S(1)}, u32[]{:S(2)}, u32[]{:S(2)}) collective-permute-start(bf16[128,1024]{1,0:T(8,128)(2,1)S(1)} %collective-permute-done.8.refs_10_), channel_id=1, source_target_pairs={{0,64},{64,128},{128,192},{192,0},{1,65},{65,129},{129,193},{193,1... | collective-permute-start | bytes 786440 | tf_op jit(solution)/shard_map/ppermute | solution.py:27
  72.5 12.9 %collective-permute-start.21 = (bf16[128,1024]{1,0:T(8,128)(2,1)}, bf16[128,1024]{1,0:T(8,128)(2,1)S(1)}, u32[]{:S(2)}, u32[]{:S(2)}) collective-permute-start(bf16[128,1024]{1,0:T(8,128)(2,1)} %collective-permute-done.11.refs_12_), channel_id=1, source_target_pairs={{0,192},{64,0},{128,64},{192,128},{1,193},{65,1},{129,65},{193,129... | collective-permute-start | bytes 786440 | tf_op jit(solution)/shard_map/ppermute | solution.py:27
  75.1 10.4 %collective-permute-start.23 = (bf16[128,1024]{1,0:T(8,128)(2,1)}, bf16[128,1024]{1,0:T(8,128)(2,1)S(1)}, u32[]{:S(2)}, u32[]{:S(2)}) collective-permute-start(bf16[128,1024]{1,0:T(8,128)(2,1)} %collective-permute-done.14.refs_14_), channel_id=1, source_target_pairs={{0,16},{16,32},{32,48},{48,0},{1,17},{17,33},{33,49},{49,1},{2,18}... | collective-permute-start | bytes 786440 | tf_op jit(solution)/shard_map/ppermute | solution.py:27
  75.2 10.2 %collective-permute-start.25 = (bf16[128,1024]{1,0:T(8,128)(2,1)}, bf16[128,1024]{1,0:T(8,128)(2,1)S(1)}, u32[]{:S(2)}, u32[]{:S(2)}) collective-permute-start(bf16[128,1024]{1,0:T(8,128)(2,1)} %collective-permute-done.17.refs_16_), channel_id=1, source_target_pairs={{0,48},{16,0},{32,16},{48,32},{1,49},{17,1},{33,17},{49,33},{2,50}... | collective-permute-start | bytes 786440 | tf_op jit(solution)/shard_map/ppermute | solution.py:27
  77.1 0.9 copy-start
  85.4 0.7 copy-start.13
  85.4 0.8 copy-start.14
  85.4 0.9 copy-start.15
  85.4 0.9 copy-start.16
  85.5 1.0 copy-start.17
  91.4 1.5 collective-permute-start.26
  92.9 13.2 %collective-permute-start.29 = (f32[8,512]{1,0:T(8,128)S(1)}, f32[8,512]{1,0:T(8,128)S(1)}, u32[]{:S(2)}, u32[]{:S(2)}) collective-permute-start(f32[8,512]{1,0:T(8,128)S(1)} %pair.1.refs_0_), channel_id=1, source_target_pairs={{0,8},{4,12},{8,0},{12,4},{1,9},{5,13},{9,1},{13,5},{2,10},{6,14},... | collective-permute-start | bytes 49160 | tf_op jit(solution)/shard_map/ppermute | solution.py:27
  96.7 9.4 %collective-permute-start.28 = (f32[8,512]{1,0:T(8,128)S(1)}, f32[8,512]{1,0:T(8,128)S(1)}, u32[]{:S(2)}, u32[]{:S(2)}) collective-permute-start(f32[8,512]{1,0:T(8,128)S(1)} %pair.1.refs_0_), channel_id=1, source_target_pairs={{0,12},{4,0},{8,4},{12,8},{1,13},{5,1},{9,5},{13,9},{2,14},{6,2},{... | collective-permute-start | bytes 49160 | tf_op jit(solution)/shard_map/ppermute | solution.py:27
  97.8 8.3 %collective-permute-start.27 = (f32[8,512]{1,0:T(8,128)S(1)}, f32[8,512]{1,0:T(8,128)S(1)}, u32[]{:S(2)}, u32[]{:S(2)}) collective-permute-start(f32[8,512]{1,0:T(8,128)S(1)} %pair.1.refs_0_), channel_id=1, source_target_pairs={{0,4},{4,8},{8,12},{12,0},{1,5},{5,9},{9,13},{13,1},{2,6},{6,10},{... | collective-permute-start | bytes 49160 | tf_op jit(solution)/shard_map/ppermute | solution.py:27
  107.9 4.1 %collective-permute-start.30 = (f32[4,512,128]{2,1,0:T(8,128)S(1)}, f32[4,512,128]{2,1,0:T(8,128)S(1)}, u32[]{:S(2)}, u32[]{:S(2)}) collective-permute-start(f32[4,512,128]{2,1,0:T(8,128)S(1)} %get-tuple-element.23), channel_id=1, source_target_pairs={{0,2},{2,0},{1,3},{3,1},{4,6},{6,4},{5,7},{7,5},{8,10},{10,8},{9,1... | collective-permute-start | bytes 3145736 | tf_op jit(solution)/shard_map/ppermute | solution.py:27
  112.2 10.5 %collective-permute-start.33 = (bf16[512,128]{1,0:T(8,128)(2,1)S(1)}, bf16[512,128]{1,0:T(8,128)(2,1)S(1)}, u32[]{:S(2)}, u32[]{:S(2)}) collective-permute-start(bf16[512,128]{1,0:T(8,128)(2,1)S(1)} %get-tuple-element.26), channel_id=1, source_target_pairs={{0,8},{4,12},{8,0},{12,4},{1,9},{5,13},{9,1},{13,5},{2,10},{6,14},... | collective-permute-start | bytes 393224 | tf_op jit(solution)/shard_map/ppermute | solution.py:27
  114.7 14.8 %collective-permute-start.32 = (bf16[512,128]{1,0:T(8,128)(2,1)S(1)}, bf16[512,128]{1,0:T(8,128)(2,1)S(1)}, u32[]{:S(2)}, u32[]{:S(2)}) collective-permute-start(bf16[512,128]{1,0:T(8,128)(2,1)S(1)} %get-tuple-element.27), channel_id=1, source_target_pairs={{0,12},{4,0},{8,4},{12,8},{1,13},{5,1},{9,5},{13,9},{2,14},{6,2},{... | collective-permute-start | bytes 393224 | tf_op jit(solution)/shard_map/ppermute | solution.py:27
  118.9 10.7 %collective-permute-start.31 = (bf16[512,128]{1,0:T(8,128)(2,1)S(1)}, bf16[512,128]{1,0:T(8,128)(2,1)S(1)}, u32[]{:S(2)}, u32[]{:S(2)}) collective-permute-start(bf16[512,128]{1,0:T(8,128)(2,1)S(1)} %get-tuple-element.28), channel_id=1, source_target_pairs={{0,4},{4,8},{8,12},{12,0},{1,5},{5,9},{9,13},{13,1},{2,6},{6,10},{... | collective-permute-start | bytes 393224 | tf_op jit(solution)/shard_map/ppermute | solution.py:27
  154.5 5.4 %collective-permute-start.34 = (f32[320,128]{1,0:T(8,128)S(1)}, f32[320,128]{1,0:T(8,128)S(1)}, u32[]{:S(2)}, u32[]{:S(2)}) collective-permute-start(f32[320,128]{1,0:T(8,128)S(1)} %convert_reduce_fusion), channel_id=1, source_target_pairs={{0,1},{1,0},{2,3},{3,2},{4,5},{5,4},{6,7},{7,6},{8,9},{9,8},{10,11... | collective-permute-start | bytes 491528 | tf_op jit(solution)/shard_map/ppermute | solution.py:27

commit v6 on v5

--- a/solution.py
+++ b/solution.py
@@ -95,9 +95,12 @@
     out_ref[...] = in_ref[...]
 
 
-def spread_kernel(in_ref, out_ref):
+def spread_kernel(in_ref, out_ref, held, sem):
+    copy = pltpu.make_async_copy(in_ref, held, sem)
+    copy.start()
+    copy.wait()
     for k in range(out_ref.shape[0]):
-        out_ref[k] = in_ref[...]
+        out_ref[k] = held[...]
 
 
 def pull_kernel(in_ref, out_ref, sem):
@@ -408,10 +411,14 @@
         spread_kernel,
         name="spread",
         out_shape=jax.ShapeDtypeStruct((16, *img_weight.shape), bf16),
-        in_specs=[VMEM],
+        in_specs=[HBM],
         out_specs=VMEM,
+        scratch_shapes=[
+            pltpu.VMEM(img_weight.shape, bf16),
+            pltpu.SemaphoreType.DMA,
+        ],
         compiler_params=pltpu.CompilerParams(vmem_limit_bytes=4 << 20),
-    )(img_weight)
+    )(in_hbm(img_weight))
     weight = exchanged(copies, PLANE).reshape(width, feats)
     other_texts = shifted(texts, "tw", 1)
     other_texts = pl.pallas_call(

time: 162 us -> 162 us (level)
  no operation moved by 1% of the time
where the time goes in v6:
time: 162 us; the launch traced here: 161 us
  starting transfers between devices  62.6 us (39%)
  waiting for transfers between devices  37.3 us (23%)
  Pallas kernels  32.7 us (20%)
  blocking collectives  23.5 us (15%)
  local copies, waits for them, and re-layouts  2.61 us (2%)
    ppermute x35, starting transfers between devices, shifted(): return lax.ppermute(x, axis, [(i, (i + step) % n) for i in range(n)])  55.2 us
    ppermute x35, waiting for transfers between devices, shifted(): return lax.ppermute(x, axis, [(i, (i + step) % n) for i in range(n)])  37.3 us
    all_to_all x1, blocking collectives, exchanged(): return lax.all_to_all(x, axis, 0, 0, tiled=True)  23.5 us
    all_to_all x1, starting transfers between devices, exchanged(): return lax.all_to_all(x, axis, 0, 0, tiled=True)  7.49 us
    pallas_call x1, Pallas kernels, local(): pl.pallas_call(lambda *refs: near_kernel(n, group, *refs), name='near', o...  7.32 us
    pallas_call x1, Pallas kernels, local(): pl.pallas_call(lambda *refs: far_gradient_kernel(m, group, *refs), name='...  6.46 us
    pallas_call x1, Pallas kernels, local(): pl.pallas_call(lambda *refs: far_score_kernel(m, group, *refs), name='far...  4.95 us
    pallas_call x1, Pallas kernels, local(): pl.pallas_call(embed_kernel, name='embed', out_shape=pltpu.HBM((rows, fea...  3.98 us
  transfers between devices with their start and end apart: 36, of which 9 were waited for; matrix products, arithmetic and copies ran while one was open for 0% of the time, Pallas kernels for 14%

profile of v6, /device:TPU:2, one launch (start us, length us, event | category | flops | bytes accessed | tf_op | source)
XLA Modules:
  0.0 161.0 jit_solution(8175246121666415972)
XLA Ops:
  0.6 2.2 %spread.1 = bf16[16,320,128]{2,1,0:T(8,128)(2,1)} custom-call(bf16[320,128]{1,0:T(8,128)(2,1)} %in_ref.2), custom_call_target="tpu_custom_call" | custom-call | tf_op jit(solution)/shard_map/spread/pallas_call | solution.py:410
  2.8 7.5 %all-to-all-start = ((bf16[16,320,128]{2,1,0:T(8,128)(2,1)}), bf16[16,320,128]{2,1,0:T(8,128)(2,1)S(1)}, u32[]{:S(2)}, u32[]{:S(2)}) async-start(bf16[16,320,128]{2,1,0:T(8,128)(2,1)} %spread.1), calls=%async_computation | async-start | bytes 2621440 | tf_op jit(solution)/shard_map/all_to_all | solution.py:35
  10.3 2.0 %collective-permute-start.12 = (bf16[64,1024]{1,0:T(8,128)(2,1)S(1)}, bf16[64,1024]{1,0:T(8,128)(2,1)S(1)}, u32[]{:S(2)}, u32[]{:S(2)}) collective-permute-start(bf16[64,1024]{1,0:T(8,128)(2,1)S(1)} %copy-done.4), channel_id=1, source_target_pairs={{0,1},{1,0},{2,3},{3,2},{4,5},{5,4},{6,7},{7,6},{8,9},{9,8},{10,11... | collective-permute-start | bytes 393224 | tf_op jit(solution)/shard_map/ppermute | solution.py:27
  12.3 1.5 collective-permute-start.7
  13.8 0.6 collective-permute-start.9
  14.4 2.1 %collective-permute-start.10 = (bf16[64,1024]{1,0:T(8,128)(2,1)S(1)}, bf16[64,1024]{1,0:T(8,128)(2,1)S(1)}, u32[]{:S(2)}, u32[]{:S(2)}) collective-permute-start(bf16[64,1024]{1,0:T(8,128)(2,1)S(1)} %copy-done.4), channel_id=1, source_target_pairs={{0,32},{16,48},{32,0},{48,16},{1,33},{17,49},{33,1},{49,17},{2,34}... | collective-permute-start | bytes 393224 | tf_op jit(solution)/shard_map/ppermute | solution.py:27
  16.5 3.1 %collective-permute-start.16 = (bf16[64,1024]{1,0:T(8,128)(2,1)S(1)}, bf16[64,1024]{1,0:T(8,128)(2,1)S(1)}, u32[]{:S(2)}, u32[]{:S(2)}) collective-permute-start(bf16[64,1024]{1,0:T(8,128)(2,1)S(1)} %gate.1), channel_id=1, source_target_pairs={{0,128},{64,192},{128,0},{192,64},{1,129},{65,193},{129,1},{193,65... | collective-permute-start | bytes 393224 | tf_op jit(solution)/shard_map/ppermute | solution.py:27
  19.5 1.2 collective-permute-start.15
  20.7 10.7 %collective-permute-done.7 = bf16[64,1024]{1,0:T(8,128)(2,1)S(1)} collective-permute-done((bf16[64,1024]{1,0:T(8,128)(2,1)S(1)}, bf16[64,1024]{1,0:T(8,128)(2,1)S(1)}, u32[]{:S(2)}, u32[]{:S(2)}) %collective-permute-start.7) | collective-permute-done | bytes 131104 | tf_op jit(solution)/shard_map/ppermute | solution.py:27
  31.4 1.3 collective-permute-start.13
  32.7 2.1 %collective-permute-start.18 = (bf16[128,1024]{1,0:T(8,128)(2,1)S(1)}, bf16[128,1024]{1,0:T(8,128)(2,1)S(1)}, u32[]{:S(2)}, u32[]{:S(2)}) collective-permute-start(bf16[128,1024]{1,0:T(8,128)(2,1)S(1)} %constant_dynamic-update-slice_fusion.refs_9_), channel_id=1, source_target_pairs={{0,192},{64,0},{128,64},{192,128},{1,193},{65,1},{129,65},{193,129... | collective-permute-start | bytes 786440 | tf_op jit(solution)/shard_map/ppermute | solution.py:27
  34.8 0.0 collective-permute-done.10
  34.8 0.1 collective-permute-start.8
  35.0 3.1 %collective-permute-done.13 = bf16[64,1024]{1,0:T(8,128)(2,1)S(1)} collective-permute-done((bf16[64,1024]{1,0:T(8,128)(2,1)S(1)}, bf16[64,1024]{1,0:T(8,128)(2,1)S(1)}, u32[]{:S(2)}, u32[]{:S(2)}) %collective-permute-start.13) | collective-permute-done | bytes 131104 | tf_op jit(solution)/shard_map/ppermute | solution.py:27
  38.1 0.9 collective-permute-start.20
  39.0 2.4 %collective-permute-start.11 = (bf16[128,1024]{1,0:T(8,128)(2,1)S(1)}, bf16[128,1024]{1,0:T(8,128)(2,1)}, u32[]{:S(2)}, u32[]{:S(2)}) collective-permute-start(bf16[128,1024]{1,0:T(8,128)(2,1)S(1)} %constant_dynamic-update-slice_fusion.2.refs_11_), channel_id=1, source_target_pairs={{0,192},{64,0},{128,64},{192,128},{1,193},{65,1},{129,65},{193,129... | collective-permute-start | bytes 786440 | tf_op jit(solution)/shard_map/ppermute | solution.py:27
  41.4 0.4 collective-permute-start.22
  41.9 2.2 %collective-permute-start.14 = (bf16[128,1024]{1,0:T(8,128)(2,1)S(1)}, bf16[128,1024]{1,0:T(8,128)(2,1)}, u32[]{:S(2)}, u32[]{:S(2)}) collective-permute-start(bf16[128,1024]{1,0:T(8,128)(2,1)S(1)} %pad_maximum_fusion.refs_13_), channel_id=1, source_target_pairs={{0,16},{16,32},{32,48},{48,0},{1,17},{17,33},{33,49},{49,1},{2,18}... | collective-permute-start | bytes 786440 | tf_op jit(solution)/shard_map/ppermute | solution.py:27
  44.1 1.1 collective-permute-done.8.refs_10_
  45.3 0.8 collective-permute-start.17
  46.0 4.0 %embed.1.refs_0_.emb_ref = bf16[512,128]{1,0:T(8,128)(2,1)} custom-call(bf16[512,5120]{1,0:T(8,128)(2,1)} %in_ref.3, bf16[5120,128]{1,0:T(8,128)(2,1)S(1)} %bitcast.13), custom_call_target="tpu_custom_call" | custom-call | flops 671088640 | bytes 7340032 | tf_op jit(solution)/shard_map/embed/pallas_call | solution.py:454
  50.1 7.3 %collective-permute-start.2 = (bf16[512,128]{1,0:T(8,128)(2,1)}, bf16[512,128]{1,0:T(8,128)(2,1)S(1)}, u32[]{:S(2)}, u32[]{:S(2)}) collective-permute-start(bf16[512,128]{1,0:T(8,128)(2,1)} %embed.1.refs_0_.emb_ref), channel_id=1, source_target_pairs={{0,8},{4,12},{8,0},{12,4},{1,9},{5,13},{9,1},{13,5},{2,10},{6,14},... | collective-permute-start | bytes 393224 | tf_op jit(solution)/shard_map/ppermute | solution.py:27
  57.4 0.0 collective-permute-start.1
  57.4 2.9 %collective-permute-start = (bf16[512,128]{1,0:T(8,128)(2,1)}, bf16[512,128]{1,0:T(8,128)(2,1)S(1)}, u32[]{:S(2)}, u32[]{:S(2)}) collective-permute-start(bf16[512,128]{1,0:T(8,128)(2,1)} %embed.1.refs_0_.emb_ref), channel_id=1, source_target_pairs={{0,4},{4,8},{8,12},{12,0},{1,5},{5,9},{9,13},{13,1},{2,6},{6,10},{... | collective-permute-start | bytes 393224 | tf_op jit(solution)/shard_map/ppermute | solution.py:27
  60.3 1.9 %collective-permute-done.2.refs_3_ = bf16[512,128]{1,0:T(8,128)(2,1)S(1)} collective-permute-done((bf16[512,128]{1,0:T(8,128)(2,1)}, bf16[512,128]{1,0:T(8,128)(2,1)S(1)}, u32[]{:S(2)}, u32[]{:S(2)}) %collective-permute-start.2) | collective-permute-done | bytes 131104 | tf_op jit(solution)/shard_map/ppermute | solution.py:27
  62.2 5.8 %collective-permute-done.1.refs_2_ = bf16[512,128]{1,0:T(8,128)(2,1)S(1)} collective-permute-done((bf16[512,128]{1,0:T(8,128)(2,1)}, bf16[512,128]{1,0:T(8,128)(2,1)S(1)}, u32[]{:S(2)}, u32[]{:S(2)}) %collective-permute-start.1) | collective-permute-done | bytes 131104 | tf_op jit(solution)/shard_map/ppermute | solution.py:27
  68.0 0.5 collective-permute-start.4
  68.5 0.6 signs.1.refs_3_
  69.2 0.1 places.1.refs_8_.refs_1_.refs_0_
  69.3 2.6 %collective-permute-start.24 = (bf16[128,1024]{1,0:T(8,128)(2,1)S(1)}, bf16[128,1024]{1,0:T(8,128)(2,1)S(1)}, u32[]{:S(2)}, u32[]{:S(2)}) collective-permute-start(bf16[128,1024]{1,0:T(8,128)(2,1)S(1)} %constant_dynamic-update-slice_fusion.4.refs_15_), channel_id=1, source_target_pairs={{0,16},{16,32},{32,48},{48,0},{1,17},{17,33},{33,49},{49,1},{2,18}... | collective-permute-start | bytes 786440 | tf_op jit(solution)/shard_map/ppermute | solution.py:27
  71.9 0.7 collective-permute-start.19
  72.6 2.5 %collective-permute-start.21 = (bf16[128,1024]{1,0:T(8,128)(2,1)}, bf16[128,1024]{1,0:T(8,128)(2,1)S(1)}, u32[]{:S(2)}, u32[]{:S(2)}) collective-permute-start(bf16[128,1024]{1,0:T(8,128)(2,1)} %collective-permute-done.11.refs_12_), channel_id=1, source_target_pairs={{0,192},{64,0},{128,64},{192,128},{1,193},{65,1},{129,65},{193,129... | collective-permute-start | bytes 786440 | tf_op jit(solution)/shard_map/ppermute | solution.py:27
  75.1 0.2 collective-permute-start.23
  75.3 1.8 %collective-permute-start.25 = (bf16[128,1024]{1,0:T(8,128)(2,1)}, bf16[128,1024]{1,0:T(8,128)(2,1)S(1)}, u32[]{:S(2)}, u32[]{:S(2)}) collective-permute-start(bf16[128,1024]{1,0:T(8,128)(2,1)} %collective-permute-done.17.refs_16_), channel_id=1, source_target_pairs={{0,48},{16,0},{32,16},{48,32},{1,49},{17,1},{33,17},{49,33},{2,50}... | collective-permute-start | bytes 786440 | tf_op jit(solution)/shard_map/ppermute | solution.py:27
  77.2 0.9 copy-done
  78.1 7.3 %near.1 = (f32[512,1024]{1,0:T(8,128)}, bf16[512,1024]{1,0:T(8,128)(2,1)}, f32[8,512]{1,0:T(8,128)S(1)}, bf16[512,1024]{1,0:T(8,128)(2,1)S(1)}) custom-call(bf16[512,128]{1,0:T(8,128)(2,1)S(1)} %copy-done, bf16[512,128]{1,0:T(8,128)(2,1)S(1)} %collective-permute-done.refs_1_, bf16[512,128]{1,0:T(8,128)(2,1)S(1)} %collective-permute-done.1.refs_2_, ...), custom_call_target="tpu_custom_call" | custom-call | flops 3221225472 | bytes 4194304 | tf_op jit(solution)/shard_map/near/pallas_call | solution.py:482
  85.5 0.6 copy-done.12
  86.1 0.1 copy-done.13
  86.3 0.1 copy-done.14
  86.4 0.0 copy-done.15
  86.4 0.1 copy-done.16
  86.5 5.0 %far_scores.1 = (bf16[512,1024]{1,0:T(8,128)(2,1)}, f32[8,512]{1,0:T(8,128)}, f32[8,512]{1,0:T(8,128)S(1)}) custom-call(bf16[512,1024]{1,0:T(8,128)(2,1)S(1)} %get-tuple-element.13.refs_0_, s32[512,1]{1,0:T(8,128)S(1)} %places.1.refs_8_.refs_1_.refs_0_, f32[8,512]{1,0:T(8,128)S(1)} %get-tuple-element.14.refs_2_, f32[1,512]{1,0:T(1,128)} %signs.1.refs_3_, ...), custom_call_target="tpu_custom_call" | custom-call | flops 1073741824 | bytes 4194304 | tf_op jit(solution)/shard_map/far_scores/pallas_call | solution.py:505
  91.4 0.3 collective-permute-start.26
  91.8 1.2 collective-permute-done.26.theirs_ref
  93.0 3.8 %collective-permute-start.29 = (f32[8,512]{1,0:T(8,128)S(1)}, f32[8,512]{1,0:T(8,128)S(1)}, u32[]{:S(2)}, u32[]{:S(2)}) collective-permute-start(f32[8,512]{1,0:T(8,128)S(1)} %pair.1.refs_0_), channel_id=1, source_target_pairs={{0,8},{4,12},{8,0},{12,4},{1,9},{5,13},{9,1},{13,5},{2,10},{6,14},... | collective-permute-start | bytes 49160 | tf_op jit(solution)/shard_map/ppermute | solution.py:27
  96.8 1.1 collective-permute-start.28
  97.9 1.9 %collective-permute-start.27 = (f32[8,512]{1,0:T(8,128)S(1)}, f32[8,512]{1,0:T(8,128)S(1)}, u32[]{:S(2)}, u32[]{:S(2)}) collective-permute-start(f32[8,512]{1,0:T(8,128)S(1)} %pair.1.refs_0_), channel_id=1, source_target_pairs={{0,4},{4,8},{8,12},{12,0},{1,5},{5,9},{9,13},{13,1},{2,6},{6,10},{... | collective-permute-start | bytes 49160 | tf_op jit(solution)/shard_map/ppermute | solution.py:27
  99.7 6.5 %far_gradient.1 = (f32[512,1024]{1,0:T(8,128)}, bf16[512,1024]{1,0:T(8,128)(2,1)}) custom-call(s32[512,1]{1,0:T(8,128)S(1)} %places.1.refs_8_.refs_1_.refs_0_, bf16[512,1024]{1,0:T(8,128)(2,1)} %get-tuple-element.17.refs_1_, f32[8,512]{1,0:T(8,128)} %get-tuple-element.16.refs_2_.refs_4_, f32[512,1024]{1,0:T(8,128)} %get-tuple-element.18.refs_3_, ...), custom_call_target="tpu_custom_call" | custom-call | flops 2147483648 | bytes 4194304 | tf_op jit(solution)/shard_map/far_gradient/pallas_call | solution.py:539
  106.2 1.8 %give.1 = (f32[4,512,128]{2,1,0:T(8,128)S(1)}, f32[8,512]{1,0:T(8,128)S(1)}) custom-call(f32[8,512]{1,0:T(8,128)S(1)} %pair.1.refs_0_, f32[8,512]{1,0:T(8,128)S(1)} %collective-permute-done.27.refs_1_, f32[8,512]{1,0:T(8,128)S(1)} %collective-permute-done.28.refs_2_, f32[8,512]{1,0:T(8,128)S(1)} %collective-permute-done.29.refs_3_, ...), custom_call_target="tpu_custom_call" | custom-call | tf_op jit(solution)/shard_map/give/pallas_call | solution.py:566
  108.0 0.1 collective-permute-start.30
  108.1 2.5 %shard_map.68.images_ref = bf16[512,5120]{1,0:T(8,128)(2,1)S(1)} custom-call(bf16[512,5120]{1,0:T(8,128)(2,1)} %in_ref.3), custom_call_target="tpu_custom_call" | custom-call | bytes 10485760 | tf_op jit(solution)/shard_map/pallas_call | solution.py:113
  110.6 1.5 keep.1
  112.1 0.1 fusion
  112.3 2.5 %collective-permute-start.33 = (bf16[512,128]{1,0:T(8,128)(2,1)S(1)}, bf16[512,128]{1,0:T(8,128)(2,1)S(1)}, u32[]{:S(2)}, u32[]{:S(2)}) collective-permute-start(bf16[512,128]{1,0:T(8,128)(2,1)S(1)} %get-tuple-element.26), channel_id=1, source_target_pairs={{0,8},{4,12},{8,0},{12,4},{1,9},{5,13},{9,1},{13,5},{2,10},{6,14},... | collective-permute-start | bytes 393224 | tf_op jit(solution)/shard_map/ppermute | solution.py:27
  114.8 4.1 %collective-permute-start.32 = (bf16[512,128]{1,0:T(8,128)(2,1)S(1)}, bf16[512,128]{1,0:T(8,128)(2,1)S(1)}, u32[]{:S(2)}, u32[]{:S(2)}) collective-permute-start(bf16[512,128]{1,0:T(8,128)(2,1)S(1)} %get-tuple-element.27), channel_id=1, source_target_pairs={{0,12},{4,0},{8,4},{12,8},{1,13},{5,1},{9,5},{13,9},{2,14},{6,2},{... | collective-permute-start | bytes 393224 | tf_op jit(solution)/shard_map/ppermute | solution.py:27
  119.0 3.9 %collective-permute-done.33.three_ref = bf16[512,128]{1,0:T(8,128)(2,1)S(1)} collective-permute-done((bf16[512,128]{1,0:T(8,128)(2,1)S(1)}, bf16[512,128]{1,0:T(8,128)(2,1)S(1)}, u32[]{:S(2)}, u32[]{:S(2)}) %collective-permute-start.33) | collective-permute-done | bytes 131104 | tf_op jit(solution)/shard_map/ppermute | solution.py:27
  122.9 6.8 %collective-permute-done.32.two_ref = bf16[512,128]{1,0:T(8,128)(2,1)S(1)} collective-permute-done((bf16[512,128]{1,0:T(8,128)(2,1)S(1)}, bf16[512,128]{1,0:T(8,128)(2,1)S(1)}, u32[]{:S(2)}, u32[]{:S(2)}) %collective-permute-start.32) | collective-permute-done | bytes 131104 | tf_op jit(solution)/shard_map/ppermute | solution.py:27
  129.6 1.3 weight.1
  130.9 23.5 %all_to_all.10 = bf16[16,320,128]{2,1,0:T(8,128)(2,1)S(1)} all-to-all(bf16[16,320,128]{2,1,0:T(8,128)(2,1)S(1)} %bitcast.14), channel_id=1, replica_groups=mesh['y'=4,'x'=4,'zh'=4,'core'=2,'tw'=2] {'y','x'}, dimensions={0} | all-to-all | bytes 2621440 | tf_op jit(solution)/shard_map/all_to_all | solution.py:35
  154.4 0.2 convert_reduce_fusion
  154.6 2.4 %collective-permute-start.34 = (f32[320,128]{1,0:T(8,128)S(1)}, f32[320,128]{1,0:T(8,128)S(1)}, u32[]{:S(2)}, u32[]{:S(2)}) collective-permute-start(f32[320,128]{1,0:T(8,128)S(1)} %convert_reduce_fusion), channel_id=1, source_target_pairs={{0,1},{1,0},{2,3},{3,2},{4,5},{5,4},{6,7},{7,6},{8,9},{9,8},{10,11... | collective-permute-start | bytes 491528 | tf_op jit(solution)/shard_map/ppermute | solution.py:27
  157.0 0.6 slice.18
  157.5 2.7 %collective-permute-done.34 = f32[320,128]{1,0:T(8,128)S(1)} collective-permute-done((f32[320,128]{1,0:T(8,128)S(1)}, f32[320,128]{1,0:T(8,128)S(1)}, u32[]{:S(2)}, u32[]{:S(2)}) %collective-permute-start.34) | collective-permute-done | bytes 163872 | tf_op jit(solution)/shard_map/ppermute | solution.py:27
  160.3 0.7 add.7
  (69 shorter events, 0.3 us)
Async XLA Ops:
  0.6 9.7 %copy-start.4 = (bf16[64,1024]{1,0:T(8,128)(2,1)S(1)}, bf16[64,1024]{1,0:T(8,128)(2,1)}, u32[]{:S(2)}) copy-start(bf16[64,1024]{1,0:T(8,128)(2,1)} %param.7) | copy-start | bytes 393220
  2.8 43.2 %all-to-all-start = ((bf16[16,320,128]{2,1,0:T(8,128)(2,1)}), bf16[16,320,128]{2,1,0:T(8,128)(2,1)S(1)}, u32[]{:S(2)}, u32[]{:S(2)}) async-start(bf16[16,320,128]{2,1,0:T(8,128)(2,1)} %spread.1), calls=%async_computation | async-start | bytes 2621440 | tf_op jit(solution)/shard_map/all_to_all | solution.py:35
  10.3 6.1 %collective-permute-start.12 = (bf16[64,1024]{1,0:T(8,128)(2,1)S(1)}, bf16[64,1024]{1,0:T(8,128)(2,1)S(1)}, u32[]{:S(2)}, u32[]{:S(2)}) collective-permute-start(bf16[64,1024]{1,0:T(8,128)(2,1)S(1)} %copy-done.4), channel_id=1, source_target_pairs={{0,1},{1,0},{2,3},{3,2},{4,5},{5,4},{6,7},{7,6},{8,9},{9,8},{10,11... | collective-permute-start | bytes 393224 | tf_op jit(solution)/shard_map/ppermute | solution.py:27
  12.3 19.1 %collective-permute-start.7 = (bf16[64,1024]{1,0:T(8,128)(2,1)S(1)}, bf16[64,1024]{1,0:T(8,128)(2,1)S(1)}, u32[]{:S(2)}, u32[]{:S(2)}) collective-permute-start(bf16[64,1024]{1,0:T(8,128)(2,1)S(1)} %copy-done.4), channel_id=1, source_target_pairs={{0,16},{16,32},{32,48},{48,0},{1,17},{17,33},{33,49},{49,1},{2,18}... | collective-permute-start | bytes 393224 | tf_op jit(solution)/shard_map/ppermute | solution.py:27
  13.8 18.9 %collective-permute-start.9 = (bf16[64,1024]{1,0:T(8,128)(2,1)S(1)}, bf16[64,1024]{1,0:T(8,128)(2,1)S(1)}, u32[]{:S(2)}, u32[]{:S(2)}) collective-permute-start(bf16[64,1024]{1,0:T(8,128)(2,1)S(1)} %copy-done.4), channel_id=1, source_target_pairs={{0,48},{16,0},{32,16},{48,32},{1,49},{17,1},{33,17},{49,33},{2,50}... | collective-permute-start | bytes 393224 | tf_op jit(solution)/shard_map/ppermute | solution.py:27
  14.4 20.4 %collective-permute-start.10 = (bf16[64,1024]{1,0:T(8,128)(2,1)S(1)}, bf16[64,1024]{1,0:T(8,128)(2,1)S(1)}, u32[]{:S(2)}, u32[]{:S(2)}) collective-permute-start(bf16[64,1024]{1,0:T(8,128)(2,1)S(1)} %copy-done.4), channel_id=1, source_target_pairs={{0,32},{16,48},{32,0},{48,16},{1,33},{17,49},{33,1},{49,17},{2,34}... | collective-permute-start | bytes 393224 | tf_op jit(solution)/shard_map/ppermute | solution.py:27
  16.5 22.5 %collective-permute-start.16 = (bf16[64,1024]{1,0:T(8,128)(2,1)S(1)}, bf16[64,1024]{1,0:T(8,128)(2,1)S(1)}, u32[]{:S(2)}, u32[]{:S(2)}) collective-permute-start(bf16[64,1024]{1,0:T(8,128)(2,1)S(1)} %gate.1), channel_id=1, source_target_pairs={{0,128},{64,192},{128,0},{192,64},{1,129},{65,193},{129,1},{193,65... | collective-permute-start | bytes 393224 | tf_op jit(solution)/shard_map/ppermute | solution.py:27
  19.5 21.9 %collective-permute-start.15 = (bf16[64,1024]{1,0:T(8,128)(2,1)S(1)}, bf16[64,1024]{1,0:T(8,128)(2,1)S(1)}, u32[]{:S(2)}, u32[]{:S(2)}) collective-permute-start(bf16[64,1024]{1,0:T(8,128)(2,1)S(1)} %gate.1), channel_id=1, source_target_pairs={{0,192},{64,0},{128,64},{192,128},{1,193},{65,1},{129,65},{193,129... | collective-permute-start | bytes 393224 | tf_op jit(solution)/shard_map/ppermute | solution.py:27
  31.4 6.6 %collective-permute-start.13 = (bf16[64,1024]{1,0:T(8,128)(2,1)S(1)}, bf16[64,1024]{1,0:T(8,128)(2,1)S(1)}, u32[]{:S(2)}, u32[]{:S(2)}) collective-permute-start(bf16[64,1024]{1,0:T(8,128)(2,1)S(1)} %gate.1), channel_id=1, source_target_pairs={{0,64},{64,128},{128,192},{192,0},{1,65},{65,129},{129,193},{193,1... | collective-permute-start | bytes 393224 | tf_op jit(solution)/shard_map/ppermute | solution.py:27
  32.7 17.3 %copy-start.5 = (bf16[128,1024]{1,0:T(8,128)(2,1)}, bf16[128,1024]{1,0:T(8,128)(2,1)S(1)}, u32[]{:S(2)}) copy-start(bf16[128,1024]{1,0:T(8,128)(2,1)S(1)} %constant_dynamic-update-slice_fusion.refs_9_) | copy-start | bytes 786436
  32.7 9.1 %collective-permute-start.18 = (bf16[128,1024]{1,0:T(8,128)(2,1)S(1)}, bf16[128,1024]{1,0:T(8,128)(2,1)S(1)}, u32[]{:S(2)}, u32[]{:S(2)}) collective-permute-start(bf16[128,1024]{1,0:T(8,128)(2,1)S(1)} %constant_dynamic-update-slice_fusion.refs_9_), channel_id=1, source_target_pairs={{0,192},{64,0},{128,64},{192,128},{1,193},{65,1},{129,65},{193,129... | collective-permute-start | bytes 786440 | tf_op jit(solution)/shard_map/ppermute | solution.py:27
  34.8 10.5 %collective-permute-start.8 = (bf16[128,1024]{1,0:T(8,128)(2,1)S(1)}, bf16[128,1024]{1,0:T(8,128)(2,1)S(1)}, u32[]{:S(2)}, u32[]{:S(2)}) collective-permute-start(bf16[128,1024]{1,0:T(8,128)(2,1)S(1)} %constant_dynamic-update-slice_fusion.refs_9_), channel_id=1, source_target_pairs={{0,64},{64,128},{128,192},{192,0},{1,65},{65,129},{129,193},{193,1... | collective-permute-start | bytes 786440 | tf_op jit(solution)/shard_map/ppermute | solution.py:27
  34.9 15.1 %copy-start.6 = (bf16[128,1024]{1,0:T(8,128)(2,1)}, bf16[128,1024]{1,0:T(8,128)(2,1)S(1)}, u32[]{:S(2)}) copy-start(bf16[128,1024]{1,0:T(8,128)(2,1)S(1)} %constant_dynamic-update-slice_fusion.2.refs_11_) | copy-start | bytes 786436
  38.1 12.0 %collective-permute-start.20 = (bf16[128,1024]{1,0:T(8,128)(2,1)S(1)}, bf16[128,1024]{1,0:T(8,128)(2,1)S(1)}, u32[]{:S(2)}, u32[]{:S(2)}) collective-permute-start(bf16[128,1024]{1,0:T(8,128)(2,1)S(1)} %constant_dynamic-update-slice_fusion.2.refs_11_), channel_id=1, source_target_pairs={{0,64},{64,128},{128,192},{192,0},{1,65},{65,129},{129,193},{193,1... | collective-permute-start | bytes 786440 | tf_op jit(solution)/shard_map/ppermute | solution.py:27
  39.0 11.0 %copy-start.3 = (bf16[128,1024]{1,0:T(8,128)(2,1)}, bf16[128,1024]{1,0:T(8,128)(2,1)S(1)}, u32[]{:S(2)}) copy-start(bf16[128,1024]{1,0:T(8,128)(2,1)S(1)} %pad_maximum_fusion.refs_13_) | copy-start | bytes 786436
  39.0 18.3 %collective-permute-start.11 = (bf16[128,1024]{1,0:T(8,128)(2,1)S(1)}, bf16[128,1024]{1,0:T(8,128)(2,1)}, u32[]{:S(2)}, u32[]{:S(2)}) collective-permute-start(bf16[128,1024]{1,0:T(8,128)(2,1)S(1)} %constant_dynamic-update-slice_fusion.2.refs_11_), channel_id=1, source_target_pairs={{0,192},{64,0},{128,64},{192,128},{1,193},{65,1},{129,65},{193,129... | collective-permute-start | bytes 786440 | tf_op jit(solution)/shard_map/ppermute | solution.py:27
  41.4 16.0 %collective-permute-start.22 = (bf16[128,1024]{1,0:T(8,128)(2,1)S(1)}, bf16[128,1024]{1,0:T(8,128)(2,1)S(1)}, u32[]{:S(2)}, u32[]{:S(2)}) collective-permute-start(bf16[128,1024]{1,0:T(8,128)(2,1)S(1)} %pad_maximum_fusion.refs_13_), channel_id=1, source_target_pairs={{0,48},{16,0},{32,16},{48,32},{1,49},{17,1},{33,17},{49,33},{2,50}... | collective-permute-start | bytes 786440 | tf_op jit(solution)/shard_map/ppermute | solution.py:27
  41.9 8.2 %copy-start.8 = (bf16[128,1024]{1,0:T(8,128)(2,1)}, bf16[128,1024]{1,0:T(8,128)(2,1)S(1)}, u32[]{:S(2)}) copy-start(bf16[128,1024]{1,0:T(8,128)(2,1)S(1)} %collective-permute-done.18.refs_4_.refs_5_) | copy-start | bytes 786436
  41.9 18.4 %collective-permute-start.14 = (bf16[128,1024]{1,0:T(8,128)(2,1)S(1)}, bf16[128,1024]{1,0:T(8,128)(2,1)}, u32[]{:S(2)}, u32[]{:S(2)}) collective-permute-start(bf16[128,1024]{1,0:T(8,128)(2,1)S(1)} %pad_maximum_fusion.refs_13_), channel_id=1, source_target_pairs={{0,16},{16,32},{32,48},{48,0},{1,17},{17,33},{33,49},{49,1},{2,18}... | collective-permute-start | bytes 786440 | tf_op jit(solution)/shard_map/ppermute | solution.py:27
  44.1 25.2 %copy-start.7 = (bf16[128,1024]{1,0:T(8,128)(2,1)}, bf16[128,1024]{1,0:T(8,128)(2,1)S(1)}, u32[]{:S(2)}) copy-start(bf16[128,1024]{1,0:T(8,128)(2,1)S(1)} %constant_dynamic-update-slice_fusion.4.refs_15_) | copy-start | bytes 786436
  45.3 26.6 %copy-start.11 = (bf16[128,1024]{1,0:T(8,128)(2,1)}, bf16[128,1024]{1,0:T(8,128)(2,1)S(1)}, u32[]{:S(2)}) copy-start(bf16[128,1024]{1,0:T(8,128)(2,1)S(1)} %collective-permute-done.8.refs_10_) | copy-start | bytes 786436
  45.3 24.0 %collective-permute-start.17 = (bf16[128,1024]{1,0:T(8,128)(2,1)S(1)}, bf16[128,1024]{1,0:T(8,128)(2,1)}, u32[]{:S(2)}, u32[]{:S(2)}) collective-permute-start(bf16[128,1024]{1,0:T(8,128)(2,1)S(1)} %constant_dynamic-update-slice_fusion.4.refs_15_), channel_id=1, source_target_pairs={{0,48},{16,0},{32,16},{48,32},{1,49},{17,1},{33,17},{49,33},{2,50}... | collective-permute-start | bytes 786440 | tf_op jit(solution)/shard_map/ppermute | solution.py:27
  46.0 22.5 %copy-start.2 = (s32[512]{0:T(512)S(1)}, s32[512]{0:T(512)}, u32[]{:S(2)}) copy-start(s32[512]{0:T(512)} %param.9) | copy-start | bytes 6148
  46.0 23.1 %copy-start.1 = (s32[512]{0:T(512)S(1)}, s32[512]{0:T(512)}, u32[]{:S(2)}) copy-start(s32[512]{0:T(512)} %param.8) | copy-start | bytes 6148
  50.1 35.3 %copy-start.9 = (bf16[128,1024]{1,0:T(8,128)(2,1)}, bf16[128,1024]{1,0:T(8,128)(2,1)S(1)}, u32[]{:S(2)}) copy-start(bf16[128,1024]{1,0:T(8,128)(2,1)S(1)} %collective-permute-done.20.refs_6_.refs_7_) | copy-start | bytes 786436
  50.1 12.1 %collective-permute-start.2 = (bf16[512,128]{1,0:T(8,128)(2,1)}, bf16[512,128]{1,0:T(8,128)(2,1)S(1)}, u32[]{:S(2)}, u32[]{:S(2)}) collective-permute-start(bf16[512,128]{1,0:T(8,128)(2,1)} %embed.1.refs_0_.emb_ref), channel_id=1, source_target_pairs={{0,8},{4,12},{8,0},{12,4},{1,9},{5,13},{9,1},{13,5},{2,10},{6,14},... | collective-permute-start | bytes 393224 | tf_op jit(solution)/shard_map/ppermute | solution.py:27
  57.4 10.7 %collective-permute-start.1 = (bf16[512,128]{1,0:T(8,128)(2,1)}, bf16[512,128]{1,0:T(8,128)(2,1)S(1)}, u32[]{:S(2)}, u32[]{:S(2)}) collective-permute-start(bf16[512,128]{1,0:T(8,128)(2,1)} %embed.1.refs_0_.emb_ref), channel_id=1, source_target_pairs={{0,12},{4,0},{8,4},{12,8},{1,13},{5,1},{9,5},{13,9},{2,14},{6,2},{... | collective-permute-start | bytes 393224 | tf_op jit(solution)/shard_map/ppermute | solution.py:27
  57.4 28.0 %copy-start.10 = (bf16[128,1024]{1,0:T(8,128)(2,1)}, bf16[128,1024]{1,0:T(8,128)(2,1)S(1)}, u32[]{:S(2)}) copy-start(bf16[128,1024]{1,0:T(8,128)(2,1)S(1)} %collective-permute-done.22.refs_8_.refs_9_) | copy-start | bytes 786436
  57.4 10.6 %collective-permute-start = (bf16[512,128]{1,0:T(8,128)(2,1)}, bf16[512,128]{1,0:T(8,128)(2,1)S(1)}, u32[]{:S(2)}, u32[]{:S(2)}) collective-permute-start(bf16[512,128]{1,0:T(8,128)(2,1)} %embed.1.refs_0_.emb_ref), channel_id=1, source_target_pairs={{0,4},{4,8},{8,12},{12,0},{1,5},{5,9},{9,13},{13,1},{2,6},{6,10},{... | collective-permute-start | bytes 393224 | tf_op jit(solution)/shard_map/ppermute | solution.py:27
  60.3 11.6 %collective-permute-start.3 = (bf16[512,128]{1,0:T(8,128)(2,1)}, bf16[512,128]{1,0:T(8,128)(2,1)S(1)}, u32[]{:S(2)}, u32[]{:S(2)}) collective-permute-start(bf16[512,128]{1,0:T(8,128)(2,1)} %embed.1.refs_0_.emb_ref), channel_id=1, source_target_pairs={{0,2},{2,0},{1,3},{3,1},{4,6},{6,4},{5,7},{7,5},{8,10},{10,8},{9,1... | collective-permute-start | bytes 393224 | tf_op jit(solution)/shard_map/ppermute | solution.py:27
  62.2 10.4 %collective-permute-start.6 = (bf16[512,128]{1,0:T(8,128)(2,1)S(1)}, bf16[512,128]{1,0:T(8,128)(2,1)S(1)}, u32[]{:S(2)}, u32[]{:S(2)}) collective-permute-start(bf16[512,128]{1,0:T(8,128)(2,1)S(1)} %collective-permute-done.2.refs_3_), channel_id=1, source_target_pairs={{0,2},{2,0},{1,3},{3,1},{4,6},{6,4},{5,7},{7,5},{8,10},{10,8},{9,1... | collective-permute-start | bytes 393224 | tf_op jit(solution)/shard_map/ppermute | solution.py:27
  68.0 7.1 %collective-permute-start.5 = (bf16[512,128]{1,0:T(8,128)(2,1)S(1)}, bf16[512,128]{1,0:T(8,128)(2,1)S(1)}, u32[]{:S(2)}, u32[]{:S(2)}) collective-permute-start(bf16[512,128]{1,0:T(8,128)(2,1)S(1)} %collective-permute-done.1.refs_2_), channel_id=1, source_target_pairs={{0,2},{2,0},{1,3},{3,1},{4,6},{6,4},{5,7},{7,5},{8,10},{10,8},{9,1... | collective-permute-start | bytes 393224 | tf_op jit(solution)/shard_map/ppermute | solution.py:27
  68.0 7.3 %collective-permute-start.4 = (bf16[512,128]{1,0:T(8,128)(2,1)S(1)}, bf16[512,128]{1,0:T(8,128)(2,1)S(1)}, u32[]{:S(2)}, u32[]{:S(2)}) collective-permute-start(bf16[512,128]{1,0:T(8,128)(2,1)S(1)} %collective-permute-done.refs_1_), channel_id=1, source_target_pairs={{0,2},{2,0},{1,3},{3,1},{4,6},{6,4},{5,7},{7,5},{8,10},{10,8},{9,1... | collective-permute-start | bytes 393224 | tf_op jit(solution)/shard_map/ppermute | solution.py:27
  69.3 16.1 %collective-permute-start.24 = (bf16[128,1024]{1,0:T(8,128)(2,1)S(1)}, bf16[128,1024]{1,0:T(8,128)(2,1)S(1)}, u32[]{:S(2)}, u32[]{:S(2)}) collective-permute-start(bf16[128,1024]{1,0:T(8,128)(2,1)S(1)} %constant_dynamic-update-slice_fusion.4.refs_15_), channel_id=1, source_target_pairs={{0,16},{16,32},{32,48},{48,0},{1,17},{17,33},{33,49},{49,1},{2,18}... | collective-permute-start | bytes 786440 | tf_op jit(solution)/shard_map/ppermute | solution.py:27
  71.9 13.6 %collective-permute-start.19 = (bf16[128,1024]{1,0:T(8,128)(2,1)S(1)}, bf16[128,1024]{1,0:T(8,128)(2,1)S(1)}, u32[]{:S(2)}, u32[]{:S(2)}) collective-permute-start(bf16[128,1024]{1,0:T(8,128)(2,1)S(1)} %collective-permute-done.8.refs_10_), channel_id=1, source_target_pairs={{0,64},{64,128},{128,192},{192,0},{1,65},{65,129},{129,193},{193,1... | collective-permute-start | bytes 786440 | tf_op jit(solution)/shard_map/ppermute | solution.py:27
  72.6 12.9 %collective-permute-start.21 = (bf16[128,1024]{1,0:T(8,128)(2,1)}, bf16[128,1024]{1,0:T(8,128)(2,1)S(1)}, u32[]{:S(2)}, u32[]{:S(2)}) collective-permute-start(bf16[128,1024]{1,0:T(8,128)(2,1)} %collective-permute-done.11.refs_12_), channel_id=1, source_target_pairs={{0,192},{64,0},{128,64},{192,128},{1,193},{65,1},{129,65},{193,129... | collective-permute-start | bytes 786440 | tf_op jit(solution)/shard_map/ppermute | solution.py:27
  75.1 10.3 %collective-permute-start.23 = (bf16[128,1024]{1,0:T(8,128)(2,1)}, bf16[128,1024]{1,0:T(8,128)(2,1)S(1)}, u32[]{:S(2)}, u32[]{:S(2)}) collective-permute-start(bf16[128,1024]{1,0:T(8,128)(2,1)} %collective-permute-done.14.refs_14_), channel_id=1, source_target_pairs={{0,16},{16,32},{32,48},{48,0},{1,17},{17,33},{33,49},{49,1},{2,18}... | collective-permute-start | bytes 786440 | tf_op jit(solution)/shard_map/ppermute | solution.py:27
  75.3 10.2 %collective-permute-start.25 = (bf16[128,1024]{1,0:T(8,128)(2,1)}, bf16[128,1024]{1,0:T(8,128)(2,1)S(1)}, u32[]{:S(2)}, u32[]{:S(2)}) collective-permute-start(bf16[128,1024]{1,0:T(8,128)(2,1)} %collective-permute-done.17.refs_16_), channel_id=1, source_target_pairs={{0,48},{16,0},{32,16},{48,32},{1,49},{17,1},{33,17},{49,33},{2,50}... | collective-permute-start | bytes 786440 | tf_op jit(solution)/shard_map/ppermute | solution.py:27
  77.2 0.9 copy-start
  85.4 0.7 copy-start.12
  85.4 0.8 copy-start.13
  85.5 0.9 copy-start.14
  85.5 0.9 copy-start.15
  85.5 1.0 copy-start.16
  91.4 1.5 collective-permute-start.26
  93.0 13.2 %collective-permute-start.29 = (f32[8,512]{1,0:T(8,128)S(1)}, f32[8,512]{1,0:T(8,128)S(1)}, u32[]{:S(2)}, u32[]{:S(2)}) collective-permute-start(f32[8,512]{1,0:T(8,128)S(1)} %pair.1.refs_0_), channel_id=1, source_target_pairs={{0,8},{4,12},{8,0},{12,4},{1,9},{5,13},{9,1},{13,5},{2,10},{6,14},... | collective-permute-start | bytes 49160 | tf_op jit(solution)/shard_map/ppermute | solution.py:27
  96.8 9.4 %collective-permute-start.28 = (f32[8,512]{1,0:T(8,128)S(1)}, f32[8,512]{1,0:T(8,128)S(1)}, u32[]{:S(2)}, u32[]{:S(2)}) collective-permute-start(f32[8,512]{1,0:T(8,128)S(1)} %pair.1.refs_0_), channel_id=1, source_target_pairs={{0,12},{4,0},{8,4},{12,8},{1,13},{5,1},{9,5},{13,9},{2,14},{6,2},{... | collective-permute-start | bytes 49160 | tf_op jit(solution)/shard_map/ppermute | solution.py:27
  97.9 8.3 %collective-permute-start.27 = (f32[8,512]{1,0:T(8,128)S(1)}, f32[8,512]{1,0:T(8,128)S(1)}, u32[]{:S(2)}, u32[]{:S(2)}) collective-permute-start(f32[8,512]{1,0:T(8,128)S(1)} %pair.1.refs_0_), channel_id=1, source_target_pairs={{0,4},{4,8},{8,12},{12,0},{1,5},{5,9},{9,13},{13,1},{2,6},{6,10},{... | collective-permute-start | bytes 49160 | tf_op jit(solution)/shard_map/ppermute | solution.py:27
  108.0 4.1 %collective-permute-start.30 = (f32[4,512,128]{2,1,0:T(8,128)S(1)}, f32[4,512,128]{2,1,0:T(8,128)S(1)}, u32[]{:S(2)}, u32[]{:S(2)}) collective-permute-start(f32[4,512,128]{2,1,0:T(8,128)S(1)} %get-tuple-element.23), channel_id=1, source_target_pairs={{0,2},{2,0},{1,3},{3,1},{4,6},{6,4},{5,7},{7,5},{8,10},{10,8},{9,1... | collective-permute-start | bytes 3145736 | tf_op jit(solution)/shard_map/ppermute | solution.py:27
  112.3 10.6 %collective-permute-start.33 = (bf16[512,128]{1,0:T(8,128)(2,1)S(1)}, bf16[512,128]{1,0:T(8,128)(2,1)S(1)}, u32[]{:S(2)}, u32[]{:S(2)}) collective-permute-start(bf16[512,128]{1,0:T(8,128)(2,1)S(1)} %get-tuple-element.26), channel_id=1, source_target_pairs={{0,8},{4,12},{8,0},{12,4},{1,9},{5,13},{9,1},{13,5},{2,10},{6,14},... | collective-permute-start | bytes 393224 | tf_op jit(solution)/shard_map/ppermute | solution.py:27
  114.8 14.8 %collective-permute-start.32 = (bf16[512,128]{1,0:T(8,128)(2,1)S(1)}, bf16[512,128]{1,0:T(8,128)(2,1)S(1)}, u32[]{:S(2)}, u32[]{:S(2)}) collective-permute-start(bf16[512,128]{1,0:T(8,128)(2,1)S(1)} %get-tuple-element.27), channel_id=1, source_target_pairs={{0,12},{4,0},{8,4},{12,8},{1,13},{5,1},{9,5},{13,9},{2,14},{6,2},{... | collective-permute-start | bytes 393224 | tf_op jit(solution)/shard_map/ppermute | solution.py:27
  118.9 10.7 %collective-permute-start.31 = (bf16[512,128]{1,0:T(8,128)(2,1)S(1)}, bf16[512,128]{1,0:T(8,128)(2,1)S(1)}, u32[]{:S(2)}, u32[]{:S(2)}) collective-permute-start(bf16[512,128]{1,0:T(8,128)(2,1)S(1)} %get-tuple-element.28), channel_id=1, source_target_pairs={{0,4},{4,8},{8,12},{12,0},{1,5},{5,9},{9,13},{13,1},{2,6},{6,10},{... | collective-permute-start | bytes 393224 | tf_op jit(solution)/shard_map/ppermute | solution.py:27
  154.6 5.7 %collective-permute-start.34 = (f32[320,128]{1,0:T(8,128)S(1)}, f32[320,128]{1,0:T(8,128)S(1)}, u32[]{:S(2)}, u32[]{:S(2)}) collective-permute-start(f32[320,128]{1,0:T(8,128)S(1)} %convert_reduce_fusion), channel_id=1, source_target_pairs={{0,1},{1,0},{2,3},{3,2},{4,5},{5,4},{6,7},{7,6},{8,9},{9,8},{10,11... | collective-permute-start | bytes 491528 | tf_op jit(solution)/shard_map/ppermute | solution.py:27
